TPU v7x, 32 devices: a whole 2x2x4 slice. The times are simulated.
32 devices in a mesh: groups: 2 (over x), ctx: 16 (over z, y, core).
Axes of the slice: x: 2, y: 2, z: 4, core: 2. Of those that a mesh axis runs over, the one named last changes fastest.
Arguments:
- queries: bfloat16 [6144, 4096], P(('groups', 'ctx')), parts along dimension 0, may hold values from -2.390625 to 2.390625
- keys: bfloat16 [6144, 4096], P(('groups', 'ctx')), parts along dimension 0, may hold values from -2.390625 to 2.390625
- values: bfloat16 [6144, 4096], P(('groups', 'ctx')), parts along dimension 0, may hold values from -6 to 6
- carried_state: float32 [64, 128, 128], P('groups', 'ctx'), parts along dimension 0, may hold values from -6 to 6
- gain: float32 [4096], replicated, may hold values from 0.5 to 1.5
- out_grad: bfloat16 [6144, 4096], P(('groups', 'ctx')), parts along dimension 0, may hold values from -3 to 3
Outputs:
- attended: bfloat16 [6144, 4096], P(('groups', 'ctx')), parts along dimension 0
- q_grad: bfloat16 [6144, 4096], P(('groups', 'ctx')), parts along dimension 0
- k_grad: bfloat16 [6144, 4096], P(('groups', 'ctx')), parts along dimension 0
- v_grad: bfloat16 [6144, 4096], P(('groups', 'ctx')), parts along dimension 0
- state_grad: float32 [64, 128, 128], P('groups', 'ctx'), parts along dimension 0
There are 2 independent parts, one for each index of `groups`. A program takes and returns all parts, laid end to end along the dimension named above; an argument that names none is the same for every part. Nothing has to cross between parts.
All inputs are finite; a program needn't handle non-finite values.
Results may differ from a plain program's by a relative error of at most 0.0075.
Values may be sent and summed in bfloat16 or wider, within the bound.
No kernel may reach another device: no remote copies, remote signals or barrier semaphores. Data moves between devices by JAX's collectives and lax.ppermute only.
A program may use at most 128 MiB of HBM per device.

v0:
```python
import jax
import jax.numpy as jnp
from jax import lax
from jax.sharding import PartitionSpec as P


def causal_mask(count):
    row_ids = lax.broadcasted_iota(jnp.int32, (count, count), 0)
    col_ids = lax.broadcasted_iota(jnp.int32, (count, count), 1)
    return (col_ids <= row_ids)[None]


def earlier_rows(blocks):
    earlier = jnp.cumsum(blocks, axis=0) - blocks
    return lax.all_to_all(earlier, "ctx", split_axis=0, concat_axis=2, tiled=True)


def later_and_total(blocks):
    inclusive = jnp.cumsum(blocks, axis=0)
    total = inclusive[-1:]
    later = (total - inclusive).astype(jnp.bfloat16)
    return (lax.all_to_all(later, "ctx", split_axis=0, concat_axis=2, tiled=True), total)


def on_device(queries, keys, values, carried_state, gain, out_grad):
    tokens = queries.shape[0]
    heads = carried_state.shape[0]
    head_dim = carried_state.shape[2]
    query_heads = queries.reshape(tokens, heads, head_dim)
    key_heads = keys.reshape(tokens, heads, head_dim)
    value_heads = values.reshape(tokens, heads, head_dim)
    whole_carried = lax.all_gather(
        carried_state.astype(jnp.bfloat16), "ctx", axis=1, tiled=True
    ).astype(carried_state.dtype)
    local_state = jnp.einsum(
        "thd,the->hde", key_heads, value_heads, preferred_element_type=jnp.float32
    )
    earlier_sum = earlier_rows(
        lax.all_to_all(local_state[None], "ctx", split_axis=2, concat_axis=0, tiled=True)
    )[0]
    prior_bf = (whole_carried + earlier_sum).astype(jnp.bfloat16)
    causal = causal_mask(tokens)
    scores = jnp.einsum("thd,shd->hts", query_heads, key_heads, preferred_element_type=jnp.float32)
    scores_bf = jnp.where(causal, scores, 0.0).astype(jnp.bfloat16)
    mixed = jnp.einsum("hts,she->the", scores_bf, value_heads, preferred_element_type=jnp.float32)
    mixed = mixed + jnp.einsum(
        "thd,hde->the", query_heads, prior_bf, preferred_element_type=jnp.float32
    )
    inv_rms = lax.rsqrt(jnp.mean(mixed * mixed, axis=2, keepdims=True) + 1e-06)
    gain_heads = gain.reshape(1, heads, head_dim)
    attended = (gain_heads * mixed * inv_rms).astype(jnp.bfloat16)
    scaled = gain_heads * out_grad.reshape(tokens, heads, head_dim).astype(jnp.float32)
    grad_mixed = (
        inv_rms * scaled
        - mixed * (inv_rms * inv_rms * inv_rms) * jnp.mean(scaled * mixed, axis=2, keepdims=True)
    ).astype(jnp.bfloat16)
    local_grad = jnp.einsum(
        "thd,the->hde", query_heads, grad_mixed, preferred_element_type=jnp.float32
    )
    later_all, total_rows = later_and_total(
        lax.all_to_all(local_grad[None], "ctx", split_axis=2, concat_axis=0, tiled=True)
    )
    later_bf = later_all[0]
    state_grad = total_rows[0]
    grad_scores = jnp.einsum(
        "the,she->hts", grad_mixed, value_heads, preferred_element_type=jnp.float32
    )
    grad_scores = jnp.where(causal, grad_scores, 0.0).astype(jnp.bfloat16)
    q_grad = jnp.einsum("hts,shd->thd", grad_scores, key_heads, preferred_element_type=jnp.float32)
    q_grad = q_grad + jnp.einsum(
        "the,hde->thd", grad_mixed, prior_bf, preferred_element_type=jnp.float32
    )
    k_grad = jnp.einsum(
        "hts,thd->shd", grad_scores, query_heads, preferred_element_type=jnp.float32
    )
    k_grad = k_grad + jnp.einsum(
        "she,hde->shd", value_heads, later_bf, preferred_element_type=jnp.float32
    )
    v_grad = jnp.einsum("hts,the->she", scores_bf, grad_mixed, preferred_element_type=jnp.float32)
    v_grad = v_grad + jnp.einsum(
        "shd,hde->she", key_heads, later_bf, preferred_element_type=jnp.float32
    )
    width = heads * head_dim
    return (
        attended.reshape(tokens, width),
        q_grad.astype(jnp.bfloat16).reshape(tokens, width),
        k_grad.astype(jnp.bfloat16).reshape(tokens, width),
        v_grad.astype(jnp.bfloat16).reshape(tokens, width),
        state_grad,
    )


def solution(mesh):
    placed = (
        P(("groups", "ctx"), None),
        P(("groups", "ctx"), None),
        P(("groups", "ctx"), None),
        P("groups", "ctx", None),
        P(),
        P(("groups", "ctx"), None),
    )
    return jax.shard_map(
        on_device,
        mesh=mesh,
        in_specs=placed,
        out_specs=(
            P(("groups", "ctx"), None),
            P(("groups", "ctx"), None),
            P(("groups", "ctx"), None),
            P(("groups", "ctx"), None),
            P("groups", "ctx", None),
        ),
        check_vma=False,
    )
```

profile of v0, /device:TPU:9, one launch (start us, length us, event | category | flops | bytes accessed | tf_op | source)
XLA Modules:
  0.0 247.9 jit_solution(12481713315073803085)
XLA Ops:
  7.2 0.0 copy-start
  7.2 2.8 %convolution_bitcast_fusion.1 = f32[1,32,128,128]{3,2,1,0:T(8,128)S(1)} fusion(bf16[192,4096]{1,0:T(8,128)(2,1)} %param.8, bf16[192,4096]{1,0:T(8,128)(2,1)} %param.7), kind=kOutput, calls=%fused_computation.24 | convolution fusion | flops 201326592 | bytes 5242880 | tf_op jit(solution)/shard_map/thd,the->hde/dot_general | solution.py:35
  10.0 1.2 copy.82
  11.2 54.2 %all_to_all.66 = f32[1,32,128,128]{3,1,0,2:T(8,128)S(1)} all-to-all(f32[1,32,128,128]{3,1,0,2:T(8,128)S(1)} %copy.82), channel_id=1, replica_groups=mesh['groups'=2,'ctx'=16] {'ctx'}, dimensions={2} | all-to-all | bytes 4194304 | tf_op jit(solution)/shard_map/all_to_all | solution.py:39
  65.4 2.6 %bitcast_subtract_fusion = f32[16,32,8,128]{3,2,1,0:T(8,128)} fusion(f32[1,32,16,8,128]{4,1,3,2,0:T(8,128)S(1)} %bitcast.188), kind=kOutput, calls=%fused_computation.14 | output fusion | flops 8388608 | bytes 4194304 | tf_op jit(solution)/shard_map/jit(cumsum)/reduce_window_sum | solution.py:14
  68.0 0.0 copy-start.13
  68.0 0.0 copy-start.1
  68.0 4.6 %all-to-all-start.1 = ((f32[16,32,8,128]{3,2,1,0:T(8,128)}), f32[16,32,8,128]{3,2,1,0:T(8,128)}, u32[]{:S(2)}, u32[]{:S(2)}) async-start(f32[16,32,8,128]{3,2,1,0:T(8,128)} %bitcast_subtract_fusion), calls=%async_computation.1 | async-start | bytes 4194304 | tf_op jit(solution)/shard_map/all_to_all | solution.py:15
  72.6 0.0 all-gather.2.cloned.1.call-start
  72.6 0.0 copy-done.13
  72.6 0.6 convert_element_type.43
  73.3 0.0 all-gather.2.cloned.1.call-update
  73.3 0.0 copy-done
  73.3 0.0 copy-done.1
  73.4 0.0 copy-start.4
  73.4 1.0 select_convert_fusion.1
  74.4 0.0 copy-start.7
  74.4 1.6 copy-done.7
  76.0 0.0 copy-done.4
  76.0 0.0 copy-start.9
  76.0 0.0 copy-start.14
  76.0 2.7 %fusion.12 = f32[32,192,128]{2,1,0:T(8,128)} fusion(bf16[32,192,192]{2,1,0:T(8,128)(2,1)S(1)} %select_convert_fusion.1, bf16[192,4096]{1,0:T(8,128)(2,1)S(1)} %copy-done.4), kind=kOutput, calls=%fused_computation.33 | convolution fusion | flops 301989888 | bytes 7077888 | tf_op jit(solution)/shard_map/hts,she->the/dot_general | solution.py:45
  78.7 51.9 %all-gather.2.cloned.1.call-done = bf16[32,128,128]{2,1,0:T(8,128)(2,1)} async-done(((bf16[32,8,128]{2,1,0:T(8,128)(2,1)}), bf16[32,128,128]{2,1,0:T(8,128)(2,1)}) %all-gather.2.cloned.1.call-update) | async-done | bytes 1048592 | tf_op jit(solution)/shard_map/all_gather | solution.py:32
  130.5 0.0 all-to-all-done.1
  130.5 0.0 copy-done.9
  130.5 0.0 copy-done.14
  130.6 0.0 copy-start.10
  130.6 5.5 %multiply_reduce_fusion = (f32[192,32]{0,1:T(8,128)S(1)}, f32[192,32]{0,1:T(8,128)S(1)}, f32[192,32,128]{2,0,1:T(8,128)S(1)}) fusion(f32[32,128]{1,0:T(8,128)S(1)} %bitcast.193, bf16[32,128,128]{2,1,0:T(8,128)(2,1)} %all-gather.2.cloned.1.call-done, f32[32,192,128]{2,1,0:T(8,128)} %fusion.12, bf16[192,4096]{1,0:T(8,128)(2,1)S(1)} %copy-done.9, ...), kind=kOutput, calls=%fused_computation.11 | convolution fusion | flops 208392192 | bytes 12648448 | tf_op jit(solution)/shard_map/thd,hde->the/dot_general | solution.py:46
  136.1 0.0 copy-done.10
  136.1 4.6 %subtract_convert_fusion = (bf16[192,32,128]{2,0,1:T(8,128)(2,1)S(1)}, bf16[32,24,8,128]{3,2,1,0:T(8,128)(2,1)}) fusion(f32[192,32,128]{2,0,1:T(8,128)S(1)} %get-tuple-element.11, f32[192,32]{0,1:T(8,128)S(1)} %get-tuple-element.12, f32[192,32]{0,1:T(8,128)S(1)} %get-tuple-element.9, f32[192,32]{0,1:T(8,128)S(1)} %get-tuple-element.10, ...), kind=kLoop, calls=%fused_computation.10 | loop fusion | flops 7864320 | bytes 7954432 | tf_op jit(solution)/shard_map/convert_element_type | solution.py:56
  140.7 2.1 convolution_bitcast_fusion
  142.9 3.1 %copy.95 = f32[1,32,128,128]{3,1,0,2:T(8,128)} copy(f32[1,32,128,128]{2,3,1,0:T(8,128)} %convolution_bitcast_fusion) | data formatting | bytes 4194304 | tf_op jit(solution)/shard_map/broadcast_in_dim | solution.py:61
  146.0 5.2 %all-to-all-start.2 = ((f32[1,32,128,128]{3,1,0,2:T(8,128)}), f32[1,32,128,128]{3,1,0,2:T(8,128)}, u32[]{:S(2)}, u32[]{:S(2)}) async-start(f32[1,32,128,128]{3,1,0,2:T(8,128)} %copy.95), calls=%async_computation.2 | async-start | bytes 4194304 | tf_op jit(solution)/shard_map/all_to_all | solution.py:61
  151.2 3.0 %copy.201 = bf16[32,24,8,128]{3,2,0,1:T(8,128)(2,1)} copy(bf16[32,24,8,128]{3,2,1,0:T(8,128)(2,1)} %get-tuple-element.8) | data formatting | bytes 3145728 | tf_op jit(solution)/shard_map/reshape | solution.py:85
  154.2 43.2 %all-to-all-done.2 = f32[1,32,128,128]{3,1,0,2:T(8,128)} async-done(((f32[1,32,128,128]{3,1,0,2:T(8,128)}), f32[1,32,128,128]{3,1,0,2:T(8,128)}, u32[]{:S(2)}, u32[]{:S(2)}) %all-to-all-start.2) | async-done | bytes 2097184 | tf_op jit(solution)/shard_map/all_to_all | solution.py:61
  197.4 2.9 %fusion.4 = f32[16,32,8,128]{3,2,1,0:T(8,128)S(1)} fusion(f32[16,32,8,128]{3,1,2,0:T(8,128)} %bitcast.18), kind=kOutput, calls=%fused_computation.17 | output fusion | flops 7864320 | bytes 4194304 | tf_op jit(solution)/shard_map/jit(cumsum)/reduce_window_sum | solution.py:19
  200.3 0.0 copy-start.12
  200.4 1.2 subtract_convert_fusion.1
  201.6 0.0 copy-done.12
  201.6 6.3 %all-to-all-start.3 = ((bf16[16,32,8,128]{3,2,1,0:T(8,128)(2,1)}), bf16[16,32,8,128]{3,2,1,0:T(8,128)(2,1)}, u32[]{:S(2)}, u32[]{:S(2)}) async-start(bf16[16,32,8,128]{3,2,1,0:T(8,128)(2,1)} %subtract_convert_fusion.1), calls=%async_computation.3 | async-start | bytes 2097152 | tf_op jit(solution)/shard_map/all_to_all | solution.py:22
  207.9 0.0 copy-start.2
  207.9 2.5 %select_convert_fusion = bf16[32,192,192]{2,1,0:T(8,128)(2,1)S(1)} fusion(pred[192,192]{1,0:T(8,128)(4,1)S(1)} %iota_compare_fusion, bf16[192,32,128]{2,0,1:T(8,128)(2,1)S(1)} %get-tuple-element.7, bf16[192,4096]{1,0:T(8,128)(2,1)} %param.8), kind=kOutput, calls=%fused_computation | convolution fusion | flops 304349184 | bytes 5541888 | tf_op jit(solution)/shard_map/the,she->hts/dot_general | solution.py:65
  210.4 0.0 copy-done.2
  210.4 0.0 copy-start.11
  210.4 1.0 fusion.15
  211.4 0.2 copy-done.11
  211.7 2.4 fusion.27
  214.1 0.0 copy-start.8
  214.1 1.6 copy.200
  215.6 0.9 copy-done.8
  216.5 3.0 %fusion.49 = f32[32,128,192]{1,2,0:T(8,128)} fusion(bf16[192,32,128]{2,0,1:T(8,128)(2,1)S(1)} %get-tuple-element.7, bf16[32,192,192]{2,1,0:T(8,128)(2,1)S(1)} %copy-done.8), kind=kOutput, calls=%fused_computation.69 | convolution fusion | flops 301989888 | bytes 7077888 | tf_op jit(solution)/shard_map/hts,the->she/dot_general | solution.py:79
  219.5 0.0 copy-start.3
  219.5 3.0 %fusion.20 = f32[32,192,128]{2,1,0:T(8,128)} fusion(bf16[32,192,192]{2,1,0:T(8,128)(2,1)S(1)} %select_convert_fusion, bf16[192,4096]{1,0:T(8,128)(2,1)S(1)} %copy-done), kind=kOutput, calls=%fused_computation.41 | convolution fusion | flops 301989888 | bytes 7077888 | tf_op jit(solution)/shard_map/hts,thd->shd/dot_general | solution.py:73
  222.5 10.4 %all-to-all-done.3 = bf16[16,32,8,128]{3,2,1,0:T(8,128)(2,1)} async-done(((bf16[16,32,8,128]{3,2,1,0:T(8,128)(2,1)}), bf16[16,32,8,128]{3,2,1,0:T(8,128)(2,1)}, u32[]{:S(2)}, u32[]{:S(2)}) %all-to-all-start.3) | async-done | bytes 1048608 | tf_op jit(solution)/shard_map/all_to_all | solution.py:22
  232.9 0.0 copy-done.3
  232.9 0.0 copy-start.6
  232.9 3.0 %fusion.24 = bf16[32,24,8,128]{3,2,1,0:T(8,128)(2,1)S(1)} fusion(f32[32,128,192]{1,2,0:T(8,128)} %fusion.49, bf16[192,4096]{1,0:T(8,128)(2,1)S(1)} %copy-done.3, bf16[16,32,8,128]{3,2,1,0:T(8,128)(2,1)} %all-to-all-done.3), kind=kOutput, calls=%fused_computation.45 | convolution fusion | flops 202899456 | bytes 7340032 | tf_op jit(solution)/shard_map/shd,hde->she/dot_general | solution.py:80
  235.9 0.0 copy-start.5
  235.9 1.6 copy.198
  237.5 0.0 copy-done.6
  237.5 0.0 copy-done.5
  237.5 2.0 fusion.28
  239.5 1.6 copy.199
  (3 shorter events, 0.0 us)
Async XLA Ops:
  7.2 66.2 %copy-start = (bf16[192,4096]{1,0:T(8,128)(2,1)S(1)}, bf16[192,4096]{1,0:T(8,128)(2,1)}, u32[]{:S(2)}) copy-start(bf16[192,4096]{1,0:T(8,128)(2,1)} %param.6) | copy-start | bytes 4718596
  68.0 4.7 %copy-start.13 = (f32[32,8,128]{2,1,0:T(8,128)S(1)}, f32[32,8,128]{2,1,0:T(8,128)}, u32[]{:S(2)}) copy-start(f32[32,8,128]{2,1,0:T(8,128)} %param.9) | copy-start | bytes 393220
  68.0 5.4 %copy-start.1 = (bf16[192,4096]{1,0:T(8,128)(2,1)S(1)}, bf16[192,4096]{1,0:T(8,128)(2,1)}, u32[]{:S(2)}) copy-start(bf16[192,4096]{1,0:T(8,128)(2,1)} %param.7) | copy-start | bytes 4718596
  68.0 62.6 %all-to-all-start.1 = ((f32[16,32,8,128]{3,2,1,0:T(8,128)}), f32[16,32,8,128]{3,2,1,0:T(8,128)}, u32[]{:S(2)}, u32[]{:S(2)}) async-start(f32[16,32,8,128]{3,2,1,0:T(8,128)} %bitcast_subtract_fusion), calls=%async_computation.1 | async-start | bytes 4194304 | tf_op jit(solution)/shard_map/all_to_all | solution.py:15
  72.6 58.0 %all-gather.2.cloned.1.call-start = ((), (), s32[]{:S(2)}) async-start(), calls=%async_computation.4 | async-start | bytes 1114112 | tf_op jit(solution)/shard_map/all_gather | solution.py:32
  73.4 2.7 %copy-start.4 = (bf16[192,4096]{1,0:T(8,128)(2,1)S(1)}, bf16[192,4096]{1,0:T(8,128)(2,1)}, u32[]{:S(2)}) copy-start(bf16[192,4096]{1,0:T(8,128)(2,1)} %param.8) | copy-start | bytes 4718596
  74.4 1.6 copy-start.7
  76.0 54.5 %copy-start.9 = (bf16[192,4096]{1,0:T(8,128)(2,1)S(1)}, bf16[192,4096]{1,0:T(8,128)(2,1)}, u32[]{:S(2)}) copy-start(bf16[192,4096]{1,0:T(8,128)(2,1)} %param.11) | copy-start | bytes 4718596
  76.0 54.5 %copy-start.14 = (f32[4096]{0:T(1024)S(1)}, f32[4096]{0:T(1024)}, u32[]{:S(2)}) copy-start(f32[4096]{0:T(1024)} %param.10) | copy-start | bytes 49156
  130.6 5.5 %copy-start.10 = (bf16[192,4096]{1,0:T(8,128)(2,1)S(1)}, bf16[192,4096]{1,0:T(8,128)(2,1)}, u32[]{:S(2)}) copy-start(bf16[192,4096]{1,0:T(8,128)(2,1)} %param.11) | copy-start | bytes 4718596
  146.0 51.4 %all-to-all-start.2 = ((f32[1,32,128,128]{3,1,0,2:T(8,128)}), f32[1,32,128,128]{3,1,0,2:T(8,128)}, u32[]{:S(2)}, u32[]{:S(2)}) async-start(f32[1,32,128,128]{3,1,0,2:T(8,128)} %copy.95), calls=%async_computation.2 | async-start | bytes 4194304 | tf_op jit(solution)/shard_map/all_to_all | solution.py:61
  200.3 1.3 copy-start.12
  201.6 31.3 %all-to-all-start.3 = ((bf16[16,32,8,128]{3,2,1,0:T(8,128)(2,1)}), bf16[16,32,8,128]{3,2,1,0:T(8,128)(2,1)}, u32[]{:S(2)}, u32[]{:S(2)}) async-start(bf16[16,32,8,128]{3,2,1,0:T(8,128)(2,1)} %subtract_convert_fusion.1), calls=%async_computation.3 | async-start | bytes 2097152 | tf_op jit(solution)/shard_map/all_to_all | solution.py:22
  207.9 2.5 %copy-start.2 = (bf16[192,4096]{1,0:T(8,128)(2,1)S(1)}, bf16[192,4096]{1,0:T(8,128)(2,1)}, u32[]{:S(2)}) copy-start(bf16[192,4096]{1,0:T(8,128)(2,1)} %param.7) | copy-start | bytes 4718596
  210.4 1.2 copy-start.11
  214.1 2.5 copy-start.8
  219.5 13.4 %copy-start.3 = (bf16[192,4096]{1,0:T(8,128)(2,1)S(1)}, bf16[192,4096]{1,0:T(8,128)(2,1)}, u32[]{:S(2)}) copy-start(bf16[192,4096]{1,0:T(8,128)(2,1)} %param.7) | copy-start | bytes 4718596
  232.9 4.5 %copy-start.6 = (f32[32,192,128]{2,1,0:T(8,128)S(1)}, f32[32,192,128]{2,1,0:T(8,128)}, u32[]{:S(2)}) copy-start(f32[32,192,128]{2,1,0:T(8,128)} %fusion.20) | copy-start | bytes 9437188
  235.9 1.6 copy-start.5
Sparse Core Ops, SparseCore 0:
  76.1 54.3 all-gather.1
where the time goes:
time: 248 us
  waiting for transfers between devices  106 us (43%)
  blocking collectives  54.2 us (22%)
  matrix products  30.9 us (12%)
  starting transfers between devices  16.2 us (7%)
  local copies, waits for them, and re-layouts  14.8 us (6%)
  between operations  14.2 us (6%)
  other arithmetic  12.1 us (5%)
    all_to_all x1, blocking collectives, on_device(): lax.all_to_all(local_state[None], 'ctx', split_axis=2, concat_axis=0, til...  54.2 us
    all_gather x1, waiting for transfers between devices, on_device(): lax.all_gather(carried_state.astype(jnp.bfloat16), 'ctx', axis=1, tiled=T...  51.9 us
    all_to_all x1, waiting for transfers between devices, on_device(): lax.all_to_all(local_grad[None], 'ctx', split_axis=2, concat_axis=0, tile...  43.2 us
    all_to_all x1, waiting for transfers between devices, later_and_total(): lax.all_to_all(later, 'ctx', split_axis=0, concat_axis=2, tiled=True)  10.4 us
    all_to_all x1, starting transfers between devices, later_and_total(): lax.all_to_all(later, 'ctx', split_axis=0, concat_axis=2, tiled=True)  6.28 us
    dot_general x1, matrix products, on_device(): jnp.einsum('thd,hde->the', query_heads, prior_bf, preferred_element_type=...  5.49 us
    all_to_all x1, starting transfers between devices, on_device(): lax.all_to_all(local_grad[None], 'ctx', split_axis=2, concat_axis=0, tile...  5.23 us
  transfers between devices with their start and end apart: 4, of which 3 were waited for; matrix products, arithmetic and copies ran while one was open for 8% of the time, Pallas kernels for 0%

commit v1 on v0

v1 whole, which is shorter than its diff:
```python
import functools

import jax
import jax.numpy as jnp
from jax import lax
from jax.experimental import pallas as pl
from jax.experimental.pallas import tpu as pltpu
from jax.sharding import PartitionSpec as P

BF16 = jnp.bfloat16
F32 = jnp.float32
CHUNKS = 1
HEAD_BLOCK = 4


def causal_mask(count):
    row_ids = lax.broadcasted_iota(jnp.int32, (count, count), 0)
    col_ids = lax.broadcasted_iota(jnp.int32, (count, count), 1)
    return col_ids <= row_ids


def plain_on_device(queries, keys, values, carried_state, gain, out_grad):
    tokens = queries.shape[0]
    heads = carried_state.shape[0]
    head_dim = carried_state.shape[2]
    f32 = dict(preferred_element_type=F32)
    split = lambda a: a.reshape(tokens, heads, head_dim)
    spread = functools.partial(
        lax.all_to_all, axis_name="ctx", split_axis=2, concat_axis=0, tiled=True
    )
    collect = functools.partial(
        lax.all_to_all, axis_name="ctx", split_axis=0, concat_axis=2, tiled=True
    )
    q, k, v = split(queries), split(keys), split(values)
    blocks = spread(jnp.einsum("thd,the->hde", k, v, **f32)[None])
    earlier = jnp.cumsum(blocks, axis=0) - blocks + carried_state[None]
    prior_bf = collect(earlier)[0].astype(BF16)
    causal = causal_mask(tokens)[None]
    scores = jnp.where(causal, jnp.einsum("thd,shd->hts", q, k, **f32), 0.0).astype(BF16)
    mixed = jnp.einsum("hts,she->the", scores, v, **f32)
    mixed = mixed + jnp.einsum("thd,hde->the", q, prior_bf, **f32)
    inv_rms = lax.rsqrt(jnp.mean(mixed * mixed, axis=2, keepdims=True) + 1e-06)
    gain_heads = gain.reshape(1, heads, head_dim)
    attended = (gain_heads * mixed * inv_rms).astype(BF16)
    scaled = gain_heads * split(out_grad).astype(F32)
    grad_mixed = (
        inv_rms * scaled
        - mixed * (inv_rms * inv_rms * inv_rms) * jnp.mean(scaled * mixed, axis=2, keepdims=True)
    ).astype(BF16)
    grads = spread(jnp.einsum("thd,the->hde", q, grad_mixed, **f32)[None])
    inclusive = jnp.cumsum(grads, axis=0)
    total = inclusive[-1:]
    later_bf = collect((total - inclusive).astype(BF16))[0]
    grad_scores = jnp.einsum("the,she->hts", grad_mixed, v, **f32)
    grad_scores = jnp.where(causal, grad_scores, 0.0).astype(BF16)
    q_grad = jnp.einsum("hts,shd->thd", grad_scores, k, **f32)
    q_grad = q_grad + jnp.einsum("the,hde->thd", grad_mixed, prior_bf, **f32)
    k_grad = jnp.einsum("hts,thd->shd", grad_scores, q, **f32)
    k_grad = k_grad + jnp.einsum("she,hde->shd", v, later_bf, **f32)
    v_grad = jnp.einsum("hts,the->she", scores, grad_mixed, **f32)
    v_grad = v_grad + jnp.einsum("shd,hde->she", k, later_bf, **f32)
    flat = lambda a: a.astype(BF16).reshape(tokens, heads * head_dim)
    return flat(attended), flat(q_grad), flat(k_grad), flat(v_grad), total[0]


def dot(a, b, dims):
    return lax.dot_general(a, b, (dims, ((), ())), preferred_element_type=F32)


NN = ((1,), (0,))
NT = ((1,), (1,))
TN = ((0,), (0,))


def put_halves(core, state, h, mine_ref, theirs_ref):
    slabs = mine_ref.shape[2] // 8
    for slab in range(slabs):
        for pair in range(2):
            at = 8 * (4 * slab + 2 * pair)
            even, odd = state[at : at + 8], state[at + 8 : at + 16]
            rows = slice(8 * slab, 8 * slab + 8)
            mine_ref[pair, h, rows, :] = jnp.where(core == 0, even, odd)
            theirs_ref[pair, h, rows, :] = jnp.where(core == 0, odd, even).astype(BF16)


def whole_state(core, own_ref, got_ref, h):
    slabs = own_ref.shape[2] // 8
    own = [own_ref[pair, h].astype(F32) for pair in range(2)]
    got = [got_ref[pair, h].astype(F32) for pair in range(2)]
    even = [jnp.where(core == 0, own[pair], got[pair]) for pair in range(2)]
    odd = [jnp.where(core == 0, got[pair], own[pair]) for pair in range(2)]
    tiles = []
    for slab in range(slabs):
        for pair in range(2):
            rows = slice(8 * slab, 8 * slab + 8)
            tiles += [even[pair][rows], odd[pair][rows]]
    return jnp.concatenate(tiles, axis=0).astype(BF16)


def cols(h, dim):
    return slice(h * dim, (h + 1) * dim)


def state_kernel(core_ref, k_ref, v_ref, mine_ref, theirs_ref):
    core = core_ref[0]
    dim = mine_ref.shape[3]
    for h in range(mine_ref.shape[1]):
        state = dot(k_ref[:, cols(h, dim)], v_ref[:, cols(h, dim)], TN)
        put_halves(core, state, h, mine_ref, theirs_ref)


def intra_kernel(q_ref, k_ref, v_ref, scores_ref, intra_ref):
    tokens = q_ref.shape[0]
    heads = scores_ref.shape[0]
    dim = q_ref.shape[1] // heads
    causal = causal_mask(tokens)
    for h in range(heads):
        at = cols(h, dim)
        scores = jnp.where(causal, dot(q_ref[:, at], k_ref[:, at], NT), 0.0).astype(BF16)
        scores_ref[h] = scores
        intra_ref[:, at] = dot(scores, v_ref[:, at], NN)


def mix_kernel(core_ref, q_ref, intra_ref, own_ref, got_ref, gain_ref, do_ref, *rest):
    att_ref, gm_ref, prior_ref, mine_ref, theirs_ref = rest[-5:]
    core = core_ref[0]
    heads, dim = own_ref.shape[1], own_ref.shape[3]
    for h in range(heads):
        at = cols(h, dim)
        prior = whole_state(core, own_ref, got_ref, h)
        prior_ref[h] = prior
        q = q_ref[:, at]
        mixed = intra_ref[:, at] + dot(q, prior, NN)
        gain = gain_ref[:, at]
        inv = lax.rsqrt(jnp.mean(mixed * mixed, axis=1, keepdims=True) + 1e-06)
        att_ref[:, at] = (gain * mixed * inv).astype(BF16)
        scaled = gain * do_ref[:, at].astype(F32)
        along = jnp.mean(scaled * mixed, axis=1, keepdims=True)
        gm = (inv * scaled - mixed * (inv * inv * inv * along)).astype(BF16)
        gm_ref[:, at] = gm
        put_halves(core, dot(q, gm, TN), h, mine_ref, theirs_ref)


def local_grad_kernel(q_ref, k_ref, v_ref, gm_ref, scores_ref, prior_ref, *rest):
    qg_ref, kpart_ref, vpart_ref = rest[-3:]
    tokens = q_ref.shape[0]
    heads = scores_ref.shape[0]
    dim = q_ref.shape[1] // heads
    causal = causal_mask(tokens)
    for h in range(heads):
        at = cols(h, dim)
        gm = gm_ref[:, at]
        gs = jnp.where(causal, dot(gm, v_ref[:, at], NT), 0.0).astype(BF16)
        qg = dot(gs, k_ref[:, at], NN) + dot(gm, prior_ref[h], NT)
        qg_ref[:, at] = qg.astype(BF16)
        kpart_ref[:, at] = dot(gs, q_ref[:, at], TN)
        vpart_ref[:, at] = dot(scores_ref[h], gm, TN)


def final_kernel(core_ref, k_ref, v_ref, kpart_ref, vpart_ref, own_ref, got_ref, *rest):
    kg_ref, vg_ref = rest[-2:]
    core = core_ref[0]
    heads, dim = own_ref.shape[1], own_ref.shape[3]
    for h in range(heads):
        at = cols(h, dim)
        later = whole_state(core, own_ref, got_ref, h)
        kg_ref[:, at] = (kpart_ref[:, at] + dot(v_ref[:, at], later, NT)).astype(BF16)
        vg_ref[:, at] = (vpart_ref[:, at] + dot(k_ref[:, at], later, NN)).astype(BF16)


def fused_on_device(n, queries, keys, values, carried_state, gain, out_grad):
    tokens, width = queries.shape
    heads, owned, dim = carried_state.shape
    slab_rows = dim // 4
    part = heads // CHUNKS
    hb = HEAD_BLOCK
    steps = part // hb
    rank = lax.axis_index("ctx")
    core, pair, slab = rank % 2, (rank // 2) % 2, rank // 4
    core_arg = core.reshape(1).astype(jnp.int32)
    gain_row = gain.reshape(1, width)

    def swap(x, bit):
        return lax.ppermute(x, "ctx", [(i, i ^ bit) for i in range(n)])

    def call(body, chunk, ins, outs, flops, with_core=True, keep=()):
        off = chunk * steps
        specs = {
            "flat": lambda o: pl.BlockSpec((tokens, hb * dim), lambda i, *_: (0, i + o)),
            "row": lambda o: pl.BlockSpec((1, hb * dim), lambda i, *_: (0, i + o)),
            "half": lambda o: pl.BlockSpec((2, hb, slab_rows, dim), lambda i, *_: (0, i, 0, 0)),
            "sq": lambda o: pl.BlockSpec((hb, tokens, tokens), lambda i, *_: (i, 0, 0)),
            "state": lambda o: pl.BlockSpec((hb, dim, dim), lambda i, *_: (i, 0, 0)),
            "local": lambda o: pl.BlockSpec((tokens, hb * dim), lambda i, *_: (0, i)),
        }
        shapes = {
            "flat": (tokens, width),
            "half": (2, part, slab_rows, dim),
            "sq": (part, tokens, tokens),
            "state": (part, dim, dim),
            "local": (tokens, part * dim),
        }
        scalars = 1 if with_core else 0
        args = [a for _, a in ins]
        in_specs = [specs[kind](off) for kind, _ in ins]
        aliases = {}
        for at, array in keep:
            aliases[scalars + len(args)] = at
            args.append(array)
            in_specs.append(pl.BlockSpec(memory_space=pl.ANY))
        out_shape = [jax.ShapeDtypeStruct(shapes[kind], t) for kind, t in outs]
        moved = sum(a.size * a.dtype.itemsize for _, a in ins) // CHUNKS
        moved += sum(s.size * s.dtype.itemsize for s in out_shape)
        return pl.pallas_call(
            body,
            out_shape=out_shape,
            grid_spec=pltpu.PrefetchScalarGridSpec(
                num_scalar_prefetch=scalars,
                grid=(steps,),
                in_specs=in_specs,
                out_specs=[specs[kind](off) for kind, _ in outs],
            ),
            input_output_aliases=aliases,
            cost_estimate=pl.CostEstimate(
                flops=int(flops * part), bytes_accessed=int(moved), transcendentals=0
            ),
            compiler_params=pltpu.CompilerParams(vmem_limit_bytes=32 * 1024 * 1024),
        )(*([core_arg] if with_core else []), *args)

    def scan_out(mine, theirs, start, later):
        bit = lambda x: (x == 0) if later else (x == 1)
        from_core = swap(theirs, 1).astype(F32)
        chip = mine + from_core
        kept = jnp.where(pair == 0, chip[0], chip[1])
        from_pair = swap(jnp.where(pair == 0, chip[1], chip[0]).astype(BF16), 2).astype(F32)
        total = kept + from_pair
        before = start
        step = 1
        while 4 * step < n:
            got = swap(total.astype(BF16), 4 * step).astype(F32)
            before = before + jnp.where(bit((slab // step) % 2), got, 0.0)
            total = total + got
            step *= 2
        for_pair = before + jnp.where(bit(1 - pair), kept, 0.0)
        here = before + jnp.where(bit(pair), from_pair, 0.0)
        there = swap(for_pair.astype(BF16), 2).astype(F32)
        ours = jnp.stack([jnp.where(pair == 0, here, there), jnp.where(pair == 0, there, here)])
        got_half = swap((ours + jnp.where(bit(1 - core), mine, 0.0)).astype(BF16), 1)
        own_half = ours + jnp.where(bit(core), from_core, 0.0)
        return own_half.astype(BF16), got_half, total

    carried = carried_state.astype(BF16)[:, None]
    step = 1
    while 4 * step < n:
        other = swap(carried, 4 * step)
        upper = (slab // step) % 2 == 1
        carried = jnp.concatenate(
            [jnp.where(upper, other, carried), jnp.where(upper, carried, other)], axis=1
        )
        step *= 2
    carried = carried.reshape(heads, slab_rows, dim).astype(F32)

    mac = 2 * tokens * dim
    states, intras, priors, mixes, locals_ = [], [], [], [], []
    for g in range(CHUNKS):
        ins = [("flat", keys), ("flat", values)]
        states.append(call(state_kernel, g, ins, [("half", F32), ("half", BF16)], mac * dim))
    for g in range(CHUNKS):
        ins = [("flat", queries), ("flat", keys), ("flat", values)]
        outs = [("sq", BF16), ("local", F32)]
        intras.append(call(intra_kernel, g, ins, outs, 2 * mac * tokens, with_core=False))
    for g in range(CHUNKS):
        start = carried[g * part : (g + 1) * part]
        priors.append(scan_out(*states[g], start, False))
    attended = None
    for g in range(CHUNKS):
        ins = [
            ("flat", queries),
            ("local", intras[g][1]),
            ("half", priors[g][0]),
            ("half", priors[g][1]),
            ("row", gain_row),
            ("flat", out_grad),
        ]
        outs = [("flat", BF16), ("local", BF16), ("state", BF16), ("half", F32), ("half", BF16)]
        keep = [] if attended is None else [(0, attended)]
        mixes.append(call(mix_kernel, g, ins, outs, 2 * mac * dim, keep=keep))
        attended = mixes[g][0]
    q_grad = None
    for g in range(CHUNKS):
        ins = [
            ("flat", queries),
            ("flat", keys),
            ("flat", values),
            ("local", mixes[g][1]),
            ("sq", intras[g][0]),
            ("state", mixes[g][2]),
        ]
        outs = [("flat", BF16), ("local", F32), ("local", F32)]
        keep = [] if q_grad is None else [(0, q_grad)]
        flops = 4 * mac * tokens + mac * dim
        locals_.append(call(local_grad_kernel, g, ins, outs, flops, with_core=False, keep=keep))
        q_grad = locals_[g][0]
    laters = [scan_out(mixes[g][3], mixes[g][4], jnp.zeros((), F32), True) for g in range(CHUNKS)]
    finals = None
    for g in range(CHUNKS):
        ins = [
            ("flat", keys),
            ("flat", values),
            ("local", locals_[g][1]),
            ("local", locals_[g][2]),
            ("half", laters[g][0]),
            ("half", laters[g][1]),
        ]
        keep = [] if finals is None else [(0, finals[0]), (1, finals[1])]
        finals = call(final_kernel, g, ins, [("flat", BF16)] * 2, 2 * mac * dim, keep=keep)
    total = jnp.concatenate([later[2] for later in laters], axis=0)
    state_grad = lax.dynamic_slice_in_dim(total, slab * owned, owned, axis=1)
    return attended, q_grad, finals[0], finals[1], state_grad


def on_device(n, queries, keys, values, carried_state, gain, out_grad):
    heads, owned, dim = carried_state.shape
    power = n >= 4 and (n & (n - 1)) == 0
    fits = power and owned % 8 == 0 and owned == 8 and dim % 128 == 0
    if fits and heads % (CHUNKS * HEAD_BLOCK) == 0 and queries.shape[0] % 16 == 0:
        return fused_on_device(n, queries, keys, values, carried_state, gain, out_grad)
    return plain_on_device(queries, keys, values, carried_state, gain, out_grad)


def solution(mesh):
    rows = P(("groups", "ctx"), None)
    state = P("groups", "ctx", None)
    return jax.shard_map(
        functools.partial(on_device, mesh.shape["ctx"]),
        mesh=mesh,
        in_specs=(rows, rows, rows, state, P(), rows),
        out_specs=(rows, rows, rows, rows, state),
        check_vma=False,
    )
```

time: 248 us -> 142 us (0.57)
  blocking collectives: 54.2 us -> 0 us
  waiting for transfers between devices: 106 us -> 61.4 us
  Pallas kernels: 0 us -> 33.8 us
  matrix products: 30.9 us -> 0 us
  between operations: 14.2 us -> 0.89 us
  starting transfers between devices: 16.2 us -> 20.9 us
    ppermute x0 -> x14, waiting for transfers between devices: none -> 61.4 us  [swap(): return lax.ppermute(x, 'ctx', [(i, i ^ bit) for i in range(n)])]
    all_to_all x1 -> x0, blocking collectives: 54.2 us -> none  [on_device(): lax.all_to_all(local_state[None], 'ctx', split_axis=2, concat_axis=0, til...]
    all_to_all x3 -> x0, waiting for transfers between devices: 53.6 us -> none  [the longest x1 43.2 us: on_device(): lax.all_to_all(local_grad[None], 'ctx', split_axis=2, concat_axis=0, tile...]
    all_gather x1 -> x0, waiting for transfers between devices: 51.9 us -> none  [on_device(): lax.all_gather(carried_state.astype(jnp.bfloat16), 'ctx', axis=1, tiled=T...]
    pallas_call x0 -> x5, Pallas kernels: none -> 33.8 us  [call(): pl.pallas_call(body, out_shape=out_shape, grid_spec=pltpu.PrefetchScalarG...]
    dot_general x12 -> x0, matrix products: 30.9 us -> none  [the longest x1 5.49 us: on_device(): jnp.einsum('thd,hde->the', query_heads, prior_bf, preferred_element_type=...]
    ppermute x0 -> x14, starting transfers between devices: none -> 20.9 us  [swap(): return lax.ppermute(x, 'ctx', [(i, i ^ bit) for i in range(n)])]
    all_to_all x3 -> x0, starting transfers between devices: 16.1 us -> none  [the longest x1 6.28 us: later_and_total(): lax.all_to_all(later, 'ctx', split_axis=0, concat_axis=2, tiled=True)]
  transfers between devices with their start and end apart: 4 -> 14, of which waited for: 3 -> 10; matrix products, arithmetic and copies ran while one was open for 8% -> 2% of each run, Pallas kernels for 0% -> 12%
where the time goes in v1:
time: 142 us; the launch traced here: 140 us
  waiting for transfers between devices  61.4 us (43%)
  Pallas kernels  33.8 us (24%)
  starting transfers between devices  20.9 us (15%)
  local copies, waits for them, and re-layouts  12.5 us (9%)
  other arithmetic  10.9 us (8%)
    ppermute x14, waiting for transfers between devices, swap(): return lax.ppermute(x, 'ctx', [(i, i ^ bit) for i in range(n)])  61.4 us
    pallas_call x5, Pallas kernels, call(): pl.pallas_call(body, out_shape=out_shape, grid_spec=pltpu.PrefetchScalarG...  33.8 us
    ppermute x14, starting transfers between devices, swap(): return lax.ppermute(x, 'ctx', [(i, i ^ bit) for i in range(n)])  20.9 us
    unnamed x48, local copies, waits for them, and re-layouts  12.5 us
  transfers between devices with their start and end apart: 14, of which 10 were waited for; matrix products, arithmetic and copies ran while one was open for 2% of the time, Pallas kernels for 12%

profile of v1, /device:TPU:9, one launch (start us, length us, event | category | flops | bytes accessed | tf_op | source)
XLA Modules:
  0.0 140.4 jit_solution(6688013798696630625)
XLA Ops:
  0.6 0.0 copy-start
  0.7 1.4 copy-done
  2.1 1.4 %copy-done.2 = bf16[192,4096]{1,0:T(8,128)(2,1)S(1)} copy-done((bf16[192,4096]{1,0:T(8,128)(2,1)S(1)}, bf16[192,4096]{1,0:T(8,128)(2,1)}, u32[]{:S(2)}) %copy-start.2) | copy-done | bytes 1572888
  3.5 2.6 %shard_map.102 = (f32[2,32,32,128]{3,2,1,0:T(8,128)S(1)}, bf16[2,32,32,128]{3,2,1,0:T(8,128)(2,1)S(1)}) custom-call(s32[1]{0:T(128)} %bitcast.core_ref, bf16[192,4096]{1,0:T(8,128)(2,1)S(1)} %copy-done, bf16[192,4096]{1,0:T(8,128)(2,1)S(1)} %copy-done.2), custom_call_target="tpu_custom_call" | custom-call | flops 201326592 | bytes 4718592 | tf_op jit(solution)/shard_map/pallas_call | solution.py:214
  6.1 0.0 copy-start.6
  6.1 0.7 collective-permute-start.2
  6.8 1.5 %collective-permute-done.2 = bf16[2,32,32,128]{3,2,1,0:T(8,128)(2,1)S(1)} collective-permute-done((bf16[2,32,32,128]{3,2,1,0:T(8,128)(2,1)S(1)}, bf16[2,32,32,128]{3,2,1,0:T(8,128)(2,1)S(1)}, u32[]{:S(2)}, u32[]{:S(2)}) %collective-permute-start.2) | collective-permute-done | bytes 524320 | tf_op jit(solution)/shard_map/ppermute | solution.py:184
  8.4 0.2 convert_add_fusion.1
  8.6 0.1 fusion.20
  8.6 0.5 copy-done.20
  9.2 1.2 collective-permute-start.3
  10.4 0.2 collective-permute-start
  10.7 6.0 %collective-permute-done.3 = bf16[32,32,128]{2,1,0:T(8,128)(2,1)S(1)} collective-permute-done((bf16[32,32,128]{2,1,0:T(8,128)(2,1)S(1)}, bf16[32,32,128]{2,1,0:T(8,128)(2,1)S(1)}, u32[]{:S(2)}, u32[]{:S(2)}) %collective-permute-start.3) | collective-permute-done | bytes 262176 | tf_op jit(solution)/shard_map/ppermute | solution.py:184
  16.7 0.1 fusion.18
  16.8 0.3 collective-permute-start.4
  17.1 2.3 %collective-permute-start.1 = (bf16[32,2,8,128]{3,2,0,1:T(8,128)(2,1)S(1)}, bf16[32,2,8,128]{3,2,0,1:T(8,128)(2,1)S(1)}, u32[]{:S(2)}, u32[]{:S(2)}) collective-permute-start(bf16[32,2,8,128]{3,2,0,1:T(8,128)(2,1)S(1)} %pad_maximum_fusion.2), channel_id=1, source_target_pairs={{0,8},{1,9},{2,10},{3,11},{4,12},{5,13},{6,14},{7,15},{8,0},{9,1},... | collective-permute-start | bytes 393224 | tf_op jit(solution)/shard_map/ppermute | solution.py:184
  19.4 5.2 %collective-permute-done.4 = bf16[32,32,128]{2,1,0:T(8,128)(2,1)S(1)} collective-permute-done((bf16[32,32,128]{2,1,0:T(8,128)(2,1)S(1)}, bf16[32,32,128]{2,1,0:T(8,128)(2,1)S(1)}, u32[]{:S(2)}, u32[]{:S(2)}) %collective-permute-start.4) | collective-permute-done | bytes 262176 | tf_op jit(solution)/shard_map/ppermute | solution.py:184
  24.6 0.1 fusion.7
  24.7 4.5 %collective-permute-start.5 = (bf16[32,32,128]{2,1,0:T(8,128)(2,1)S(1)}, bf16[32,32,128]{2,1,0:T(8,128)(2,1)S(1)}, u32[]{:S(2)}, u32[]{:S(2)}) collective-permute-start(bf16[32,32,128]{2,1,0:T(8,128)(2,1)S(1)} %fusion.7), channel_id=1, source_target_pairs={{0,8},{1,9},{2,10},{3,11},{4,12},{5,13},{6,14},{7,15},{8,0},{9,1},... | collective-permute-start | bytes 786440 | tf_op jit(solution)/shard_map/ppermute | solution.py:184
  29.2 0.0 collective-permute-done.1
  29.2 10.6 %collective-permute-done.5 = bf16[32,32,128]{2,1,0:T(8,128)(2,1)S(1)} collective-permute-done((bf16[32,32,128]{2,1,0:T(8,128)(2,1)S(1)}, bf16[32,32,128]{2,1,0:T(8,128)(2,1)S(1)}, u32[]{:S(2)}, u32[]{:S(2)}) %collective-permute-start.5) | collective-permute-done | bytes 262176 | tf_op jit(solution)/shard_map/ppermute | solution.py:184
  39.8 0.2 fusion.17
  40.0 1.3 collective-permute-start.6
  41.3 6.1 %collective-permute-done.6 = bf16[32,32,128]{2,1,0:T(8,128)(2,1)S(1)} collective-permute-done((bf16[32,32,128]{2,1,0:T(8,128)(2,1)S(1)}, bf16[32,32,128]{2,1,0:T(8,128)(2,1)S(1)}, u32[]{:S(2)}, u32[]{:S(2)}) %collective-permute-start.6) | collective-permute-done | bytes 262176 | tf_op jit(solution)/shard_map/ppermute | solution.py:184
  47.4 0.1 fusion.8
  47.6 0.0 copy-start.1
  47.6 0.0 copy-start.3
  47.6 1.5 %add_convert_fusion.1 = (bf16[2,32,32,128]{3,2,1,0:T(8,128)(2,1)S(1)}, bf16[2,32,32,128]{3,2,1,0:T(8,128)(2,1)S(1)}) fusion(f32[2,32,32,128]{3,2,1,0:T(8,128)} %copy-done.6, f32[1,32,32,128]{3,2,1,0:T(8,128)S(1)} %get-tuple-element.48, f32[1,32,32,128]{3,2,1,0:T(8,128)S(1)} %get-tuple-element.47, pred[]{:T(512)S(6)} %eq.61, ...), kind=kLoop, calls=%fused_computation.11 | loop fusion | flops 2097152 | bytes 3670018 | tf_op jit(solution)/shard_map/convert_element_type | solution.py:248
  49.1 0.0 copy-start.14
  49.2 0.0 copy-start.17
  49.2 1.7 %collective-permute-start.7 = (bf16[2,32,32,128]{3,2,1,0:T(8,128)(2,1)S(1)}, bf16[2,32,32,128]{3,2,1,0:T(8,128)(2,1)S(1)}, u32[]{:S(2)}, u32[]{:S(2)}) collective-permute-start(bf16[2,32,32,128]{3,2,1,0:T(8,128)(2,1)S(1)} %get-tuple-element.45), channel_id=1, source_target_pairs={{0,1},{1,0},{2,3},{3,2},{4,5},{5,4},{6,7},{7,6},{8,9},{9,8},{10,11... | collective-permute-start | bytes 1572872 | tf_op jit(solution)/shard_map/ppermute | solution.py:184
  50.9 5.4 %shard_map.101 = (bf16[32,192,192]{2,1,0:T(8,128)(2,1)S(1)}, f32[192,4096]{1,0:T(8,128)S(1)}) custom-call(bf16[192,4096]{1,0:T(8,128)(2,1)S(1)} %copy-done.4, bf16[192,4096]{1,0:T(8,128)(2,1)S(1)} %copy-done.1, bf16[192,4096]{1,0:T(8,128)(2,1)S(1)} %copy-done.3), custom_call_target="tpu_custom_call" | custom-call | flops 603979776 | bytes 10223616 | tf_op jit(solution)/shard_map/pallas_call | solution.py:214
  56.3 1.6 %copy-done.9 = bf16[32,192,192]{2,1,0:T(8,128)(2,1)} copy-done((bf16[32,192,192]{2,1,0:T(8,128)(2,1)}, bf16[32,192,192]{2,1,0:T(8,128)(2,1)S(1)}, u32[]{:S(2)}) %copy-start.9) | copy-done | bytes 2359320
  57.9 0.0 collective-permute-done.7.got_ref
  58.0 7.6 %shard_map.103 = (bf16[192,4096]{1,0:T(8,128)(2,1)}, bf16[192,4096]{1,0:T(8,128)(2,1)S(1)}, bf16[32,128,128]{2,1,0:T(8,128)(2,1)S(1)}, f32[2,32,32,128]{3,2,1,0:T(8,128)S(1)}, bf16[2,32,32,128]{3,2,1,0:T(8,128)(2,1)S(1)}) custom-call(s32[1]{0:T(128)} %bitcast.core_ref, bf16[192,4096]{1,0:T(8,128)(2,1)S(1)} %copy-done.4, ...), custom_call_target="tpu_custom_call" | custom-call | flops 402653184 | bytes 13123584 | tf_op jit(solution)/shard_map/pallas_call | solution.py:214
  65.6 1.0 copy-done.15
  66.5 0.7 collective-permute-start.8
  67.3 1.5 %collective-permute-done.8 = bf16[2,32,32,128]{3,2,1,0:T(8,128)(2,1)S(1)} collective-permute-done((bf16[2,32,32,128]{3,2,1,0:T(8,128)(2,1)S(1)}, bf16[2,32,32,128]{3,2,1,0:T(8,128)(2,1)S(1)}, u32[]{:S(2)}, u32[]{:S(2)}) %collective-permute-start.8) | collective-permute-done | bytes 524320 | tf_op jit(solution)/shard_map/ppermute | solution.py:184
  68.8 0.2 convert_add_fusion
  69.0 0.1 fusion.21
  69.1 0.5 copy-done.21
  69.6 1.2 collective-permute-start.9
  70.9 6.3 %collective-permute-done.9 = bf16[32,32,128]{2,1,0:T(8,128)(2,1)S(1)} collective-permute-done((bf16[32,32,128]{2,1,0:T(8,128)(2,1)S(1)}, bf16[32,32,128]{2,1,0:T(8,128)(2,1)S(1)}, u32[]{:S(2)}, u32[]{:S(2)}) %collective-permute-start.9) | collective-permute-done | bytes 262176 | tf_op jit(solution)/shard_map/ppermute | solution.py:184
  77.1 0.1 fusion.19
  77.3 0.9 collective-permute-start.10
  78.2 5.8 %collective-permute-done.10 = bf16[32,32,128]{2,1,0:T(8,128)(2,1)S(1)} collective-permute-done((bf16[32,32,128]{2,1,0:T(8,128)(2,1)S(1)}, bf16[32,32,128]{2,1,0:T(8,128)(2,1)S(1)}, u32[]{:S(2)}, u32[]{:S(2)}) %collective-permute-start.10) | collective-permute-done | bytes 262176 | tf_op jit(solution)/shard_map/ppermute | solution.py:184
  84.0 1.0 fusion.22
  85.0 3.1 %collective-permute-start.11 = (bf16[32,32,128]{2,1,0:T(8,128)(2,1)}, bf16[32,32,128]{2,1,0:T(8,128)(2,1)}, u32[]{:S(2)}, u32[]{:S(2)}) collective-permute-start(bf16[32,32,128]{2,1,0:T(8,128)(2,1)} %get-tuple-element.33), channel_id=1, source_target_pairs={{0,8},{1,9},{2,10},{3,11},{4,12},{5,13},{6,14},{7,15},{8,0},{9,1},... | collective-permute-start | bytes 786440 | tf_op jit(solution)/shard_map/ppermute | solution.py:184
  88.1 12.0 %collective-permute-done.11 = bf16[32,32,128]{2,1,0:T(8,128)(2,1)} collective-permute-done((bf16[32,32,128]{2,1,0:T(8,128)(2,1)}, bf16[32,32,128]{2,1,0:T(8,128)(2,1)}, u32[]{:S(2)}, u32[]{:S(2)}) %collective-permute-start.11) | collective-permute-done | bytes 262176 | tf_op jit(solution)/shard_map/ppermute | solution.py:184
  100.0 2.0 %fusion.15 = bf16[32,32,128]{2,1,0:T(8,128)(2,1)} fusion(f32[1,32,32,128]{3,2,1,0:T(8,128)} %copy-done.18, pred[]{:T(512)S(6)} %eq.64, bf16[32,32,128]{2,1,0:T(8,128)(2,1)} %collective-permute-done.11, pred[]{:T(512)S(6)} %eq.63, bf16[32,32,128]{2,1,0:T(8,128)(2,1)} %copy-done.19, pred[]{:T(512)S(6)} %eq.62), kind=kLoop, calls=%fused_computation.36 | loop fusion | flops 1048576 | bytes 1310723 | tf_op jit(solution)/shard_map/convert_element_type | solution.py:246
  102.1 1.2 collective-permute-start.12
  103.3 6.4 %collective-permute-done.12 = bf16[32,32,128]{2,1,0:T(8,128)(2,1)} collective-permute-done((bf16[32,32,128]{2,1,0:T(8,128)(2,1)}, bf16[32,32,128]{2,1,0:T(8,128)(2,1)}, u32[]{:S(2)}, u32[]{:S(2)}) %collective-permute-start.12) | collective-permute-done | bytes 262176 | tf_op jit(solution)/shard_map/ppermute | solution.py:184
  109.7 1.3 fusion.12
  111.1 1.3 add_convert_fusion
  112.4 1.4 collective-permute-start.13
  113.7 1.4 %copy-done.5 = bf16[192,4096]{1,0:T(8,128)(2,1)S(1)} copy-done((bf16[192,4096]{1,0:T(8,128)(2,1)S(1)}, bf16[192,4096]{1,0:T(8,128)(2,1)}, u32[]{:S(2)}) %copy-start.5) | copy-done | bytes 1572888
  115.1 1.9 %copy-done.10 = bf16[32,192,192]{2,1,0:T(8,128)(2,1)S(1)} copy-done((bf16[32,192,192]{2,1,0:T(8,128)(2,1)S(1)}, bf16[32,192,192]{2,1,0:T(8,128)(2,1)}, u32[]{:S(2)}) %copy-start.10) | copy-done | bytes 2359320
  117.0 1.4 %copy-done.13 = bf16[192,4096]{1,0:T(8,128)(2,1)S(1)} copy-done((bf16[192,4096]{1,0:T(8,128)(2,1)S(1)}, bf16[192,4096]{1,0:T(8,128)(2,1)}, u32[]{:S(2)}) %copy-start.13) | copy-done | bytes 1572888
  118.4 1.2 copy-done.16
  119.7 11.7 %shard_map.104 = (bf16[192,4096]{1,0:T(8,128)(2,1)}, f32[192,4096]{1,0:T(8,128)S(1)}, f32[192,4096]{1,0:T(8,128)S(1)}) custom-call(bf16[192,4096]{1,0:T(8,128)(2,1)S(1)} %copy-done.5, bf16[192,4096]{1,0:T(8,128)(2,1)S(1)} %copy-done.1, bf16[192,4096]{1,0:T(8,128)(2,1)S(1)} %copy-done.3, bf16[192,4096]{1,0:T(8,128)(2,1)S(1)} %copy-done.13, ...), custom_call_target="tpu_custom_call" | custom-call | flops 1409286144 | bytes 17563648 | tf_op jit(solution)/shard_map/pallas_call | solution.py:214
  131.3 1.0 convert_element_type.103
  132.4 1.6 %dynamic-slice_add_fusion = f32[32,8,128]{2,1,0:T(8,128)} fusion(f32[32,32,128]{2,1,0:T(8,128)S(1)} %convert_element_type.103, s32[]{:T(128)S(6)} %select_n.237, f32[32,32,128]{2,1,0:T(8,128)} %get-tuple-element.34), kind=kLoop, calls=%fused_computation.49 | loop fusion | flops 32768 | bytes 393220 | tf_op jit(solution)/shard_map/add | solution.py:242
  133.9 0.0 collective-permute-done.13.got_ref
  133.9 6.4 %shard_map.105 = (bf16[192,4096]{1,0:T(8,128)(2,1)}, bf16[192,4096]{1,0:T(8,128)(2,1)}) custom-call(s32[1]{0:T(128)} %bitcast.core_ref, bf16[192,4096]{1,0:T(8,128)(2,1)S(1)} %copy-done.1, bf16[192,4096]{1,0:T(8,128)(2,1)S(1)} %copy-done.3, f32[192,4096]{1,0:T(8,128)S(1)} %get-tuple-element.27.kpart_ref, f32[192,4096]{1,0:T(8,128)S(1)} %get-tuple-element.28.vpart_ref, ...), custom_call_target="tpu_custom_call" | custom-call | flops 402653184 | bytes 13631488 | tf_op jit(solution)/shard_map/pallas_call | solution.py:214
  (37 shorter events, 0.1 us)
Async XLA Ops:
  0.6 1.4 %copy-start = (bf16[192,4096]{1,0:T(8,128)(2,1)S(1)}, bf16[192,4096]{1,0:T(8,128)(2,1)}, u32[]{:S(2)}) copy-start(bf16[192,4096]{1,0:T(8,128)(2,1)} %k_ref.7) | copy-start | bytes 4718596
  2.1 1.4 %copy-start.2 = (bf16[192,4096]{1,0:T(8,128)(2,1)S(1)}, bf16[192,4096]{1,0:T(8,128)(2,1)}, u32[]{:S(2)}) copy-start(bf16[192,4096]{1,0:T(8,128)(2,1)} %v_ref.7) | copy-start | bytes 4718596
  6.1 2.5 %copy-start.6 = (f32[2,32,32,128]{3,2,1,0:T(8,128)}, f32[2,32,32,128]{3,2,1,0:T(8,128)S(1)}, u32[]{:S(2)}) copy-start(f32[2,32,32,128]{3,2,1,0:T(8,128)S(1)} %get-tuple-element.20) | copy-start | bytes 3145732
  6.1 2.3 %collective-permute-start.2 = (bf16[2,32,32,128]{3,2,1,0:T(8,128)(2,1)S(1)}, bf16[2,32,32,128]{3,2,1,0:T(8,128)(2,1)S(1)}, u32[]{:S(2)}, u32[]{:S(2)}) collective-permute-start(bf16[2,32,32,128]{3,2,1,0:T(8,128)(2,1)S(1)} %get-tuple-element.21), channel_id=1, source_target_pairs={{0,1},{1,0},{2,3},{3,2},{4,5},{5,4},{6,7},{7,6},{8,9},{9,8},{10,11... | collective-permute-start | bytes 1572872 | tf_op jit(solution)/shard_map/ppermute | solution.py:184
  8.4 0.8 copy-start.20
  8.4 2.0 %copy-start.23 = (f32[32,8,128]{2,1,0:T(8,128)S(1)}, f32[32,8,128]{2,1,0:T(8,128)}, u32[]{:S(2)}) copy-start(f32[32,8,128]{2,1,0:T(8,128)} %param.9) | copy-start | bytes 393220
  9.2 7.5 %collective-permute-start.3 = (bf16[32,32,128]{2,1,0:T(8,128)(2,1)S(1)}, bf16[32,32,128]{2,1,0:T(8,128)(2,1)S(1)}, u32[]{:S(2)}, u32[]{:S(2)}) collective-permute-start(bf16[32,32,128]{2,1,0:T(8,128)(2,1)S(1)} %fusion.20), channel_id=1, source_target_pairs={{0,2},{1,3},{2,0},{3,1},{4,6},{5,7},{6,4},{7,5},{8,10},{9,11},{10,... | collective-permute-start | bytes 786440 | tf_op jit(solution)/shard_map/ppermute | solution.py:184
  10.4 6.7 %collective-permute-start = (bf16[32,1,8,128]{3,2,0,1:T(8,128)(2,1)S(1)}, bf16[32,1,8,128]{3,2,0,1:T(8,128)(2,1)S(1)}, u32[]{:S(2)}, u32[]{:S(2)}) collective-permute-start(bf16[32,1,8,128]{3,2,0,1:T(8,128)(2,1)S(1)} %convert_bitcast_fusion), channel_id=1, source_target_pairs={{0,4},{1,5},{2,6},{3,7},{4,0},{5,1},{6,2},{7,3},{8,12},{9,13},{10,... | collective-permute-start | bytes 196616 | tf_op jit(solution)/shard_map/ppermute | solution.py:184
  16.8 7.8 %collective-permute-start.4 = (bf16[32,32,128]{2,1,0:T(8,128)(2,1)S(1)}, bf16[32,32,128]{2,1,0:T(8,128)(2,1)S(1)}, u32[]{:S(2)}, u32[]{:S(2)}) collective-permute-start(bf16[32,32,128]{2,1,0:T(8,128)(2,1)S(1)} %get-tuple-element.39), channel_id=1, source_target_pairs={{0,4},{1,5},{2,6},{3,7},{4,0},{5,1},{6,2},{7,3},{8,12},{9,13},{10,... | collective-permute-start | bytes 786440 | tf_op jit(solution)/shard_map/ppermute | solution.py:184
  17.1 12.1 %collective-permute-start.1 = (bf16[32,2,8,128]{3,2,0,1:T(8,128)(2,1)S(1)}, bf16[32,2,8,128]{3,2,0,1:T(8,128)(2,1)S(1)}, u32[]{:S(2)}, u32[]{:S(2)}) collective-permute-start(bf16[32,2,8,128]{3,2,0,1:T(8,128)(2,1)S(1)} %pad_maximum_fusion.2), channel_id=1, source_target_pairs={{0,8},{1,9},{2,10},{3,11},{4,12},{5,13},{6,14},{7,15},{8,0},{9,1},... | collective-permute-start | bytes 393224 | tf_op jit(solution)/shard_map/ppermute | solution.py:184
  24.7 15.1 %collective-permute-start.5 = (bf16[32,32,128]{2,1,0:T(8,128)(2,1)S(1)}, bf16[32,32,128]{2,1,0:T(8,128)(2,1)S(1)}, u32[]{:S(2)}, u32[]{:S(2)}) collective-permute-start(bf16[32,32,128]{2,1,0:T(8,128)(2,1)S(1)} %fusion.7), channel_id=1, source_target_pairs={{0,8},{1,9},{2,10},{3,11},{4,12},{5,13},{6,14},{7,15},{8,0},{9,1},... | collective-permute-start | bytes 786440 | tf_op jit(solution)/shard_map/ppermute | solution.py:184
  40.0 7.4 %collective-permute-start.6 = (bf16[32,32,128]{2,1,0:T(8,128)(2,1)S(1)}, bf16[32,32,128]{2,1,0:T(8,128)(2,1)S(1)}, u32[]{:S(2)}, u32[]{:S(2)}) collective-permute-start(bf16[32,32,128]{2,1,0:T(8,128)(2,1)S(1)} %get-tuple-element.37), channel_id=1, source_target_pairs={{0,2},{1,3},{2,0},{3,1},{4,6},{5,7},{6,4},{7,5},{8,10},{9,11},{10,... | collective-permute-start | bytes 786440 | tf_op jit(solution)/shard_map/ppermute | solution.py:184
  47.4 3.5 %copy-start.4 = (bf16[192,4096]{1,0:T(8,128)(2,1)S(1)}, bf16[192,4096]{1,0:T(8,128)(2,1)}, u32[]{:S(2)}) copy-start(bf16[192,4096]{1,0:T(8,128)(2,1)} %q_ref.5) | copy-start | bytes 4718596
  47.6 3.3 %copy-start.1 = (bf16[192,4096]{1,0:T(8,128)(2,1)S(1)}, bf16[192,4096]{1,0:T(8,128)(2,1)}, u32[]{:S(2)}) copy-start(bf16[192,4096]{1,0:T(8,128)(2,1)} %k_ref.7) | copy-start | bytes 4718596
  47.6 3.3 %copy-start.3 = (bf16[192,4096]{1,0:T(8,128)(2,1)S(1)}, bf16[192,4096]{1,0:T(8,128)(2,1)}, u32[]{:S(2)}) copy-start(bf16[192,4096]{1,0:T(8,128)(2,1)} %v_ref.7) | copy-start | bytes 4718596
  49.1 8.8 %copy-start.14 = (bf16[192,4096]{1,0:T(8,128)(2,1)S(1)}, bf16[192,4096]{1,0:T(8,128)(2,1)}, u32[]{:S(2)}) copy-start(bf16[192,4096]{1,0:T(8,128)(2,1)} %do_ref.1) | copy-start | bytes 4718596
  49.2 8.8 %copy-start.17 = (f32[4096]{0:T(1024)S(1)}, f32[4096]{0:T(1024)}, u32[]{:S(2)}) copy-start(f32[4096]{0:T(1024)} %param.10) | copy-start | bytes 49156
  49.2 8.8 %collective-permute-start.7 = (bf16[2,32,32,128]{3,2,1,0:T(8,128)(2,1)S(1)}, bf16[2,32,32,128]{3,2,1,0:T(8,128)(2,1)S(1)}, u32[]{:S(2)}, u32[]{:S(2)}) collective-permute-start(bf16[2,32,32,128]{3,2,1,0:T(8,128)(2,1)S(1)} %get-tuple-element.45), channel_id=1, source_target_pairs={{0,1},{1,0},{2,3},{3,2},{4,5},{5,4},{6,7},{7,6},{8,9},{9,8},{10,11... | collective-permute-start | bytes 1572872 | tf_op jit(solution)/shard_map/ppermute | solution.py:184
  56.3 1.6 %copy-start.9 = (bf16[32,192,192]{2,1,0:T(8,128)(2,1)}, bf16[32,192,192]{2,1,0:T(8,128)(2,1)S(1)}, u32[]{:S(2)}) copy-start(bf16[32,192,192]{2,1,0:T(8,128)(2,1)S(1)} %get-tuple-element.24.scores_ref) | copy-start | bytes 7077892
  65.6 1.0 copy-start.15
  66.5 2.5 %copy-start.7 = (f32[2,32,32,128]{3,2,1,0:T(8,128)}, f32[2,32,32,128]{3,2,1,0:T(8,128)S(1)}, u32[]{:S(2)}) copy-start(f32[2,32,32,128]{3,2,1,0:T(8,128)S(1)} %get-tuple-element.29) | copy-start | bytes 3145732
  66.5 2.5 %copy-start.12 = (bf16[192,4096]{1,0:T(8,128)(2,1)}, bf16[192,4096]{1,0:T(8,128)(2,1)S(1)}, u32[]{:S(2)}) copy-start(bf16[192,4096]{1,0:T(8,128)(2,1)S(1)} %get-tuple-element.23.gm_ref) | copy-start | bytes 4718596
  66.5 2.3 %collective-permute-start.8 = (bf16[2,32,32,128]{3,2,1,0:T(8,128)(2,1)S(1)}, bf16[2,32,32,128]{3,2,1,0:T(8,128)(2,1)S(1)}, u32[]{:S(2)}, u32[]{:S(2)}) collective-permute-start(bf16[2,32,32,128]{3,2,1,0:T(8,128)(2,1)S(1)} %get-tuple-element.30), channel_id=1, source_target_pairs={{0,1},{1,0},{2,3},{3,2},{4,5},{5,4},{6,7},{7,6},{8,9},{9,8},{10,11... | collective-permute-start | bytes 1572872 | tf_op jit(solution)/shard_map/ppermute | solution.py:184
  68.8 0.8 copy-start.21
  69.6 7.5 %collective-permute-start.9 = (bf16[32,32,128]{2,1,0:T(8,128)(2,1)S(1)}, bf16[32,32,128]{2,1,0:T(8,128)(2,1)S(1)}, u32[]{:S(2)}, u32[]{:S(2)}) collective-permute-start(bf16[32,32,128]{2,1,0:T(8,128)(2,1)S(1)} %fusion.21), channel_id=1, source_target_pairs={{0,2},{1,3},{2,0},{3,1},{4,6},{5,7},{6,4},{7,5},{8,10},{9,11},{10,... | collective-permute-start | bytes 786440 | tf_op jit(solution)/shard_map/ppermute | solution.py:184
  77.3 6.7 %copy-start.18 = (f32[1,32,32,128]{3,2,1,0:T(8,128)}, f32[1,32,32,128]{3,2,1,0:T(8,128)S(1)}, u32[]{:S(2)}) copy-start(f32[1,32,32,128]{3,2,1,0:T(8,128)S(1)} %get-tuple-element.36) | copy-start | bytes 1572868
  77.3 6.7 %collective-permute-start.10 = (bf16[32,32,128]{2,1,0:T(8,128)(2,1)S(1)}, bf16[32,32,128]{2,1,0:T(8,128)(2,1)S(1)}, u32[]{:S(2)}, u32[]{:S(2)}) collective-permute-start(bf16[32,32,128]{2,1,0:T(8,128)(2,1)S(1)} %get-tuple-element.35), channel_id=1, source_target_pairs={{0,4},{1,5},{2,6},{3,7},{4,0},{5,1},{6,2},{7,3},{8,12},{9,13},{10,... | collective-permute-start | bytes 786440 | tf_op jit(solution)/shard_map/ppermute | solution.py:184
  84.0 1.0 copy-start.19
  85.0 15.1 %collective-permute-start.11 = (bf16[32,32,128]{2,1,0:T(8,128)(2,1)}, bf16[32,32,128]{2,1,0:T(8,128)(2,1)}, u32[]{:S(2)}, u32[]{:S(2)}) collective-permute-start(bf16[32,32,128]{2,1,0:T(8,128)(2,1)} %get-tuple-element.33), channel_id=1, source_target_pairs={{0,8},{1,9},{2,10},{3,11},{4,12},{5,13},{6,14},{7,15},{8,0},{9,1},... | collective-permute-start | bytes 786440 | tf_op jit(solution)/shard_map/ppermute | solution.py:184
  102.1 7.7 %collective-permute-start.12 = (bf16[32,32,128]{2,1,0:T(8,128)(2,1)}, bf16[32,32,128]{2,1,0:T(8,128)(2,1)}, u32[]{:S(2)}, u32[]{:S(2)}) collective-permute-start(bf16[32,32,128]{2,1,0:T(8,128)(2,1)} %fusion.15), channel_id=1, source_target_pairs={{0,2},{1,3},{2,0},{3,1},{4,6},{5,7},{6,4},{7,5},{8,10},{9,11},{10,... | collective-permute-start | bytes 786440 | tf_op jit(solution)/shard_map/ppermute | solution.py:184
  103.3 7.7 %copy-start.8 = (f32[2,32,32,128]{3,2,1,0:T(8,128)S(1)}, f32[2,32,32,128]{3,2,1,0:T(8,128)}, u32[]{:S(2)}) copy-start(f32[2,32,32,128]{3,2,1,0:T(8,128)} %copy-done.7) | copy-start | bytes 3145732
  103.3 7.8 %copy-start.22 = (bf16[2,32,32,128]{3,2,1,0:T(8,128)(2,1)S(1)}, bf16[2,32,32,128]{3,2,1,0:T(8,128)(2,1)}, u32[]{:S(2)}) copy-start(bf16[2,32,32,128]{3,2,1,0:T(8,128)(2,1)} %copy-done.21) | copy-start | bytes 1572868
  112.4 21.6 %collective-permute-start.13 = (bf16[2,32,32,128]{3,2,1,0:T(8,128)(2,1)}, bf16[2,32,32,128]{3,2,1,0:T(8,128)(2,1)}, u32[]{:S(2)}, u32[]{:S(2)}) collective-permute-start(bf16[2,32,32,128]{3,2,1,0:T(8,128)(2,1)} %get-tuple-element.41), channel_id=1, source_target_pairs={{0,1},{1,0},{2,3},{3,2},{4,5},{5,4},{6,7},{7,6},{8,9},{9,8},{10,11... | collective-permute-start | bytes 1572872 | tf_op jit(solution)/shard_map/ppermute | solution.py:184
  113.7 1.4 %copy-start.5 = (bf16[192,4096]{1,0:T(8,128)(2,1)S(1)}, bf16[192,4096]{1,0:T(8,128)(2,1)}, u32[]{:S(2)}) copy-start(bf16[192,4096]{1,0:T(8,128)(2,1)} %q_ref.5) | copy-start | bytes 4718596
  115.1 1.9 %copy-start.10 = (bf16[32,192,192]{2,1,0:T(8,128)(2,1)S(1)}, bf16[32,192,192]{2,1,0:T(8,128)(2,1)}, u32[]{:S(2)}) copy-start(bf16[32,192,192]{2,1,0:T(8,128)(2,1)} %copy-done.9) | copy-start | bytes 7077892
  117.0 1.4 %copy-start.13 = (bf16[192,4096]{1,0:T(8,128)(2,1)S(1)}, bf16[192,4096]{1,0:T(8,128)(2,1)}, u32[]{:S(2)}) copy-start(bf16[192,4096]{1,0:T(8,128)(2,1)} %copy-done.12) | copy-start | bytes 4718596
  118.4 1.2 copy-start.16
  119.6 14.3 %copy-start.11 = (bf16[2,32,32,128]{3,2,1,0:T(8,128)(2,1)S(1)}, bf16[2,32,32,128]{3,2,1,0:T(8,128)(2,1)}, u32[]{:S(2)}) copy-start(bf16[2,32,32,128]{3,2,1,0:T(8,128)(2,1)} %get-tuple-element.42.own_ref) | copy-start | bytes 1572868

commit v2 on v1

v2 whole, which is shorter than its diff:
```python
import functools
import math

import jax
import jax.numpy as jnp
from jax import lax
from jax.experimental import pallas as pl
from jax.experimental.pallas import tpu as pltpu
from jax.sharding import PartitionSpec as P


BF16 = jnp.bfloat16
F32 = jnp.float32
CHUNKS = 2
HEAD_BLOCK = 4
LOCAL_SPLIT = 2
VMEM_LIMIT = 6 * 1024 * 1024


def causal_mask(count):
    row_ids = lax.broadcasted_iota(jnp.int32, (count, count), 0)
    col_ids = lax.broadcasted_iota(jnp.int32, (count, count), 1)
    return col_ids <= row_ids


def plain_on_device(queries, keys, values, carried_state, gain, out_grad):
    tokens = queries.shape[0]
    heads = carried_state.shape[0]
    head_dim = carried_state.shape[2]
    f32 = dict(preferred_element_type=F32)
    split = lambda a: a.reshape(tokens, heads, head_dim)
    spread = functools.partial(
        lax.all_to_all, axis_name="ctx", split_axis=2, concat_axis=0, tiled=True
    )
    collect = functools.partial(
        lax.all_to_all, axis_name="ctx", split_axis=0, concat_axis=2, tiled=True
    )
    q, k, v = split(queries), split(keys), split(values)
    blocks = spread(jnp.einsum("thd,the->hde", k, v, **f32)[None])
    earlier = jnp.cumsum(blocks, axis=0) - blocks + carried_state[None]
    prior_bf = collect(earlier)[0].astype(BF16)
    causal = causal_mask(tokens)[None]
    scores = jnp.where(causal, jnp.einsum("thd,shd->hts", q, k, **f32), 0.0).astype(BF16)
    mixed = jnp.einsum("hts,she->the", scores, v, **f32)
    mixed = mixed + jnp.einsum("thd,hde->the", q, prior_bf, **f32)
    inv_rms = lax.rsqrt(jnp.mean(mixed * mixed, axis=2, keepdims=True) + 1e-06)
    gain_heads = gain.reshape(1, heads, head_dim)
    attended = (gain_heads * mixed * inv_rms).astype(BF16)
    scaled = gain_heads * split(out_grad).astype(F32)
    grad_mixed = (
        inv_rms * scaled
        - mixed * (inv_rms * inv_rms * inv_rms) * jnp.mean(scaled * mixed, axis=2, keepdims=True)
    ).astype(BF16)
    grads = spread(jnp.einsum("thd,the->hde", q, grad_mixed, **f32)[None])
    inclusive = jnp.cumsum(grads, axis=0)
    total = inclusive[-1:]
    later_bf = collect((total - inclusive).astype(BF16))[0]
    grad_scores = jnp.einsum("the,she->hts", grad_mixed, v, **f32)
    grad_scores = jnp.where(causal, grad_scores, 0.0).astype(BF16)
    q_grad = jnp.einsum("hts,shd->thd", grad_scores, k, **f32)
    q_grad = q_grad + jnp.einsum("the,hde->thd", grad_mixed, prior_bf, **f32)
    k_grad = jnp.einsum("hts,thd->shd", grad_scores, q, **f32)
    k_grad = k_grad + jnp.einsum("she,hde->shd", v, later_bf, **f32)
    v_grad = jnp.einsum("hts,the->she", scores, grad_mixed, **f32)
    v_grad = v_grad + jnp.einsum("shd,hde->she", k, later_bf, **f32)
    flat = lambda a: a.astype(BF16).reshape(tokens, heads * head_dim)
    return flat(attended), flat(q_grad), flat(k_grad), flat(v_grad), total[0]


def dot(a, b, dims):
    return lax.dot_general(a, b, (dims, ((), ())), preferred_element_type=F32)


NN = ((1,), (0,))
NT = ((1,), (1,))
TN = ((0,), (0,))


def put_halves(core, state, h, mine_ref, theirs_ref):
    slabs = mine_ref.shape[2] // 8
    for slab in range(slabs):
        for pair in range(2):
            at = 8 * (4 * slab + 2 * pair)
            even, odd = state[at : at + 8], state[at + 8 : at + 16]
            rows = slice(8 * slab, 8 * slab + 8)
            mine_ref[pair, h, rows, :] = jnp.where(core == 0, even, odd)
            theirs_ref[pair, h, rows, :] = jnp.where(core == 0, odd, even).astype(BF16)


def whole_state(core, own_ref, got_ref, h):
    slabs = own_ref.shape[2] // 8
    own = [own_ref[pair, h].astype(F32) for pair in range(2)]
    got = [got_ref[pair, h].astype(F32) for pair in range(2)]
    even = [jnp.where(core == 0, own[pair], got[pair]) for pair in range(2)]
    odd = [jnp.where(core == 0, got[pair], own[pair]) for pair in range(2)]
    tiles = []
    for slab in range(slabs):
        for pair in range(2):
            rows = slice(8 * slab, 8 * slab + 8)
            tiles += [even[pair][rows], odd[pair][rows]]
    return jnp.concatenate(tiles, axis=0).astype(BF16)


def cols(h, dim):
    return slice(h * dim, (h + 1) * dim)


def state_kernel(core_ref, k_ref, v_ref, mine_ref, theirs_ref):
    core = core_ref[0]
    dim = mine_ref.shape[3]
    ats = [cols(h, dim) for h in range(mine_ref.shape[1])]
    states = [dot(k_ref[:, at], v_ref[:, at], TN) for at in ats]
    for h, state in enumerate(states):
        put_halves(core, state, h, mine_ref, theirs_ref)


def intra_kernel(q_ref, k_ref, v_ref, scores_ref, intra_ref):
    heads = scores_ref.shape[0]
    dim = q_ref.shape[1] // heads
    causal = causal_mask(q_ref.shape[0])
    ats = [cols(h, dim) for h in range(heads)]
    scores = [
        jnp.where(causal, dot(q_ref[:, at], k_ref[:, at], NT), 0.0).astype(BF16) for at in ats
    ]
    for h, at in enumerate(ats):
        scores_ref[h] = scores[h]
        intra_ref[:, at] = dot(scores[h], v_ref[:, at], NN)


def mix_kernel(core_ref, q_ref, intra_ref, own_ref, got_ref, gain_ref, do_ref, *rest):
    att_ref, gm_ref, prior_ref, mine_ref, theirs_ref = rest[-5:]
    core = core_ref[0]
    heads, dim = own_ref.shape[1], own_ref.shape[3]
    ats = [cols(h, dim) for h in range(heads)]
    for h in range(heads):
        prior_ref[h] = whole_state(core, own_ref, got_ref, h)
    crosses = [dot(q_ref[:, at], prior_ref[h], NN) for h, at in enumerate(ats)]
    for at, cross in zip(ats, crosses):
        mixed = intra_ref[:, at] + cross
        gain = gain_ref[:, at]
        inv = lax.rsqrt(jnp.mean(mixed * mixed, axis=1, keepdims=True) + 1e-06)
        att_ref[:, at] = (gain * mixed * inv).astype(BF16)
        scaled = gain * do_ref[:, at].astype(F32)
        along = jnp.mean(scaled * mixed, axis=1, keepdims=True)
        gm_ref[:, at] = (inv * scaled - mixed * (inv * inv * inv * along)).astype(BF16)
    grads = [dot(q_ref[:, at], gm_ref[:, at], TN) for at in ats]
    for h, grad in enumerate(grads):
        put_halves(core, grad, h, mine_ref, theirs_ref)


def local_grad_kernel(q_ref, k_ref, v_ref, gm_ref, scores_ref, prior_ref, *rest):
    qg_ref, kpart_ref, vpart_ref = rest[-3:]
    heads = scores_ref.shape[0]
    dim = q_ref.shape[1] // heads
    causal = causal_mask(q_ref.shape[0])
    ats = [cols(h, dim) for h in range(heads)]
    grads = [
        jnp.where(causal, dot(gm_ref[:, at], v_ref[:, at], NT), 0.0).astype(BF16) for at in ats
    ]
    for h, at in enumerate(ats):
        qg = dot(grads[h], k_ref[:, at], NN) + dot(gm_ref[:, at], prior_ref[h], NT)
        qg_ref[:, at] = qg.astype(BF16)
    for h, at in enumerate(ats):
        kpart_ref[:, at] = dot(grads[h], q_ref[:, at], TN)
    for h, at in enumerate(ats):
        vpart_ref[:, at] = dot(scores_ref[h], gm_ref[:, at], TN)


def final_kernel(core_ref, k_ref, v_ref, kpart_ref, vpart_ref, own_ref, got_ref, *rest):
    kg_ref, vg_ref = rest[-2:]
    core = core_ref[0]
    heads, dim = own_ref.shape[1], own_ref.shape[3]
    laters = [whole_state(core, own_ref, got_ref, h) for h in range(heads)]
    for h, later in enumerate(laters):
        at = cols(h, dim)
        kg_ref[:, at] = (kpart_ref[:, at] + dot(v_ref[:, at], later, NT)).astype(BF16)
    for h, later in enumerate(laters):
        at = cols(h, dim)
        vg_ref[:, at] = (vpart_ref[:, at] + dot(k_ref[:, at], later, NN)).astype(BF16)


def fused_on_device(n, queries, keys, values, carried_state, gain, out_grad):
    tokens, width = queries.shape
    heads, owned, dim = carried_state.shape
    slab_rows = dim // 4
    part = heads // CHUNKS
    hb = HEAD_BLOCK
    rank = lax.axis_index("ctx").astype(jnp.int32)
    core_arg = (rank & 1).reshape(1)
    odd_core, odd_pair = (rank & 1) == 1, (rank & 2) == 2
    odd_slab = {}
    step = 1
    while 4 * step < n:
        odd_slab[step] = (rank & (4 * step)) != 0
        step *= 2
    owned_at = (lax.axis_index("ctx").astype(jnp.uint32) >> 2) * jnp.uint32(owned)
    scalars = (core_arg, odd_core, odd_pair, odd_slab, owned_at)
    scalars, (keys, values, carried_state) = lax.optimization_barrier(
        (scalars, (keys, values, carried_state))
    )
    core_arg, odd_core, odd_pair, odd_slab, owned_at = scalars
    gain_row = gain.reshape(1, width)

    def swap(x, bit):
        return lax.ppermute(x, "ctx", [(i, i ^ bit) for i in range(n)])

    def call(body, chunk, ins, outs, flops, with_core=True, keep=(), sub=0, subs=1):
        count = part // hb // subs
        first = sub * count
        off = chunk * (part // hb) + first
        specs = {
            "flat": pl.BlockSpec((tokens, hb * dim), lambda i, *_: (0, i + off)),
            "row": pl.BlockSpec((1, hb * dim), lambda i, *_: (0, i + off)),
            "half": pl.BlockSpec((2, hb, slab_rows, dim), lambda i, *_: (0, i + first, 0, 0)),
            "sq": pl.BlockSpec((hb, tokens, tokens), lambda i, *_: (i + first, 0, 0)),
            "state": pl.BlockSpec((hb, dim, dim), lambda i, *_: (i + first, 0, 0)),
            "local": pl.BlockSpec((tokens, hb * dim), lambda i, *_: (0, i + first)),
        }
        shapes = {
            "flat": (tokens, width),
            "half": (2, part, slab_rows, dim),
            "sq": (part, tokens, tokens),
            "state": (part, dim, dim),
            "local": (tokens, part * dim),
        }
        scalar_args = [core_arg] if with_core else []
        args = [a for _, a in ins]
        in_specs = [specs[kind] for kind, _ in ins]
        aliases = {}
        for at, array in keep:
            aliases[len(scalar_args) + len(args)] = at
            args.append(array)
            in_specs.append(pl.BlockSpec(memory_space=pl.ANY))
        block = lambda kind: math.prod(specs[kind].block_shape)
        moved = sum(block(kind) * a.dtype.itemsize for kind, a in ins)
        moved += sum(block(kind) * jnp.dtype(t).itemsize for kind, t in outs)
        return pl.pallas_call(
            body,
            out_shape=[jax.ShapeDtypeStruct(shapes[kind], t) for kind, t in outs],
            grid_spec=pltpu.PrefetchScalarGridSpec(
                num_scalar_prefetch=len(scalar_args),
                grid=(count,),
                in_specs=in_specs,
                out_specs=[specs[kind] for kind, _ in outs],
            ),
            input_output_aliases=aliases,
            cost_estimate=pl.CostEstimate(
                flops=flops * count * hb, bytes_accessed=moved * count, transcendentals=0
            ),
            compiler_params=pltpu.CompilerParams(vmem_limit_bytes=VMEM_LIMIT),
        )(*scalar_args, *args)

    def scan_out(mine, theirs, carried=None):
        later = carried is None

        def if_after(odd, x):
            return jnp.where(odd, 0.0, x) if later else jnp.where(odd, x, 0.0)

        def if_before(odd, x):
            return jnp.where(odd, x, 0.0) if later else jnp.where(odd, 0.0, x)

        from_core = swap(theirs, 1).astype(F32)
        chip = mine + from_core
        kept = jnp.where(odd_pair, chip[1], chip[0])
        sent = jnp.where(odd_pair, chip[0], chip[1]).astype(BF16)
        from_pair = swap(sent, 2).astype(F32)
        total = kept + from_pair
        before = 0.0
        last = max(odd_slab)
        for step, odd in odd_slab.items():
            if later:
                got = swap(total.astype(BF16), 4 * step).astype(F32)
                before = before + if_after(odd, got)
                total = total + got
            elif step < last:
                rows = jnp.concatenate([total.astype(BF16), carried], axis=1)
                rows = swap(rows, 4 * step)
                got, other = rows[:, :slab_rows].astype(F32), rows[:, slab_rows:]
                before = before + if_after(odd, got)
                total = total + got
                lower, upper = jnp.where(odd, other, carried), jnp.where(odd, carried, other)
                carried = jnp.concatenate([lower, upper], axis=1)
            else:
                blank = jnp.zeros_like(carried)
                lower, upper = jnp.where(odd, blank, carried), jnp.where(odd, carried, blank)
                known = jnp.concatenate([lower, upper], axis=1).astype(F32)
                sent = (known + if_before(odd, total)).astype(BF16)
                before = before + known + swap(sent, 4 * step).astype(F32)
        for_pair = (before + if_before(odd_pair, kept)).astype(BF16)
        here = before + if_after(odd_pair, from_pair)
        there = swap(for_pair, 2).astype(F32)
        ours = jnp.stack([jnp.where(odd_pair, there, here), jnp.where(odd_pair, here, there)])
        for_core = (ours + if_before(odd_core, mine)).astype(BF16)
        got_half = swap(for_core, 1)
        own_half = (ours + if_after(odd_core, from_core)).astype(BF16)
        return own_half, got_half, total

    mac = 2 * tokens * dim
    chunks = range(CHUNKS)
    states, intras, priors, mixes, locals_ = [], [], [], [], []
    for g in chunks:
        pair = (keys, values)
        if g == 0:
            pair = [pltpu.with_memory_space_constraint(x, pltpu.HBM) for x in pair]
        ins = [("flat", x) for x in pair]
        outs = [("half", F32), ("half", BF16)]
        states.append(call(state_kernel, g, ins, outs, mac * dim))
    for g in chunks:
        ins = [("flat", queries), ("flat", keys), ("flat", values)]
        outs = [("sq", BF16), ("local", F32)]
        intras.append(call(intra_kernel, g, ins, outs, 2 * mac * tokens, with_core=False))
    for g in chunks:
        carried = carried_state[g * part : (g + 1) * part].astype(BF16)
        priors.append(scan_out(*states[g], carried))
    keep = []
    for g in chunks:
        ins = [
            ("flat", queries),
            ("local", intras[g][1]),
            ("half", priors[g][0]),
            ("half", priors[g][1]),
            ("row", gain_row),
            ("flat", out_grad),
        ]
        outs = [("flat", BF16), ("local", BF16), ("state", BF16), ("half", F32), ("half", BF16)]
        mixes.append(call(mix_kernel, g, ins, outs, 2 * mac * dim, keep=keep))
        keep = [(0, mixes[g][0])]
    keep = []
    for g in chunks:
        ins = [
            ("flat", queries),
            ("flat", keys),
            ("flat", values),
            ("local", mixes[g][1]),
            ("sq", intras[g][0]),
            ("state", mixes[g][2]),
        ]
        outs = [("flat", BF16), ("local", F32), ("local", F32)]
        flops = 4 * mac * tokens + mac * dim
        for sub in range(LOCAL_SPLIT):
            at = dict(sub=sub, subs=LOCAL_SPLIT)
            made = call(local_grad_kernel, g, ins, outs, flops, False, keep, **at)
            keep = list(enumerate(made))
        locals_.append(made)
        keep = [(0, made[0])]
    laters = [scan_out(mixes[g][3], mixes[g][4]) for g in chunks]
    keep = []
    for g in chunks:
        ins = [
            ("flat", keys),
            ("flat", values),
            ("local", locals_[g][1]),
            ("local", locals_[g][2]),
            ("half", laters[g][0]),
            ("half", laters[g][1]),
        ]
        made = call(final_kernel, g, ins, [("flat", BF16)] * 2, 2 * mac * dim, keep=keep)
        keep = list(enumerate(made))
    zero = jnp.uint32(0)
    owned_rows = [
        lax.dynamic_slice(later, (zero, owned_at, zero), (part, owned, dim)) for _, _, later in laters
    ]
    state_grad = jnp.concatenate(owned_rows, axis=0)
    return mixes[-1][0], locals_[-1][0], made[0], made[1], state_grad


def on_device(n, queries, keys, values, carried_state, gain, out_grad):
    heads, owned, dim = carried_state.shape
    power = n >= 4 and (n & (n - 1)) == 0
    fits = power and owned % 8 == 0 and owned == 8 and dim % 128 == 0
    if fits and heads % (CHUNKS * HEAD_BLOCK) == 0 and queries.shape[0] % 16 == 0:
        return fused_on_device(n, queries, keys, values, carried_state, gain, out_grad)
    return plain_on_device(queries, keys, values, carried_state, gain, out_grad)


def solution(mesh):
    rows = P(("groups", "ctx"), None)
    state = P("groups", "ctx", None)
    return jax.shard_map(
        functools.partial(on_device, mesh.shape["ctx"]),
        mesh=mesh,
        in_specs=(rows, rows, rows, state, P(), rows),
        out_specs=(rows, rows, rows, rows, state),
        check_vma=False,
    )
```

time: 142 us -> 94.7 us (0.67)
  the two profiles are of different devices: /device:TPU:9 before, /device:TPU:1 now
where the time goes in v2:
time: 94.7 us; the launch traced here: 94.5 us
  waiting for transfers between devices  35 us (37%)
  Pallas kernels  29 us (31%)
  starting transfers between devices  26.4 us (28%)
  other arithmetic  3.06 us (3%)
  between operations  1.07 us (1%)
    ppermute x24, waiting for transfers between devices, swap(): return lax.ppermute(x, 'ctx', [(i, i ^ bit) for i in range(n)])  35 us
    pallas_call x12, Pallas kernels, call(): pl.pallas_call(body, out_shape=[jax.ShapeDtypeStruct(shapes[kind], t) for...  29 us
    ppermute x24, starting transfers between devices, swap(): return lax.ppermute(x, 'ctx', [(i, i ^ bit) for i in range(n)])  26.4 us
  transfers between devices with their start and end apart: 24, of which 11 were waited for; matrix products, arithmetic and copies ran while one was open for 3% of the time, Pallas kernels for 25%

profile of v2, /device:TPU:1, one launch (start us, length us, event | category | flops | bytes accessed | tf_op | source)
XLA Modules:
  0.0 94.5 jit_solution(7884919088365499699)
XLA Ops:
  0.7 3.2 %shard_map.104 = (f32[2,16,32,128]{3,2,1,0:T(8,128)S(1)}, bf16[2,16,32,128]{3,2,1,0:T(8,128)(2,1)S(1)}) custom-call(s32[1]{0:T(128)} %bitcast.core_ref, bf16[192,4096]{1,0:T(8,128)(2,1)} %k_ref.9, bf16[192,4096]{1,0:T(8,128)(2,1)} %v_ref.9), custom_call_target="tpu_custom_call" | custom-call | flops 100663296 | bytes 2359296 | tf_op jit(solution)/shard_map/pallas_call | solution.py:237
  3.8 0.1 collective-permute-start.6
  3.9 1.4 %shard_map.102 = (f32[2,16,32,128]{3,2,1,0:T(8,128)S(1)}, bf16[2,16,32,128]{3,2,1,0:T(8,128)(2,1)S(1)}) custom-call(s32[1]{0:T(128)} %bitcast.core_ref, bf16[192,4096]{1,0:T(8,128)(2,1)S(1)} %copy-done, bf16[192,4096]{1,0:T(8,128)(2,1)S(1)} %copy-done.1), custom_call_target="tpu_custom_call" | custom-call | flops 100663296 | bytes 2359296 | tf_op jit(solution)/shard_map/pallas_call | solution.py:237
  5.3 0.5 collective-permute-start
  5.9 0.1 convert_add_fusion.2
  6.0 2.3 %collective-permute-start.7 = (bf16[16,32,128]{2,1,0:T(8,128)(2,1)S(1)}, bf16[16,32,128]{2,1,0:T(8,128)(2,1)S(1)}, u32[]{:S(2)}, u32[]{:S(2)}) collective-permute-start(bf16[16,32,128]{2,1,0:T(8,128)(2,1)S(1)} %fusion.41), channel_id=1, source_target_pairs={{0,2},{1,3},{2,0},{3,1},{4,6},{5,7},{6,4},{7,5},{8,10},{9,11},{10,... | collective-permute-start | bytes 393224 | tf_op jit(solution)/shard_map/ppermute | solution.py:205
  8.3 0.1 convert_add_fusion.3
  8.4 3.3 %collective-permute-done.7 = bf16[16,32,128]{2,1,0:T(8,128)(2,1)S(1)} collective-permute-done((bf16[16,32,128]{2,1,0:T(8,128)(2,1)S(1)}, bf16[16,32,128]{2,1,0:T(8,128)(2,1)S(1)}, u32[]{:S(2)}, u32[]{:S(2)}) %collective-permute-start.7) | collective-permute-done | bytes 131104 | tf_op jit(solution)/shard_map/ppermute | solution.py:205
  11.8 1.3 %collective-permute-start.8 = (bf16[16,40,128]{2,1,0:T(8,128)(2,1)S(1)}, bf16[16,40,128]{2,1,0:T(8,128)(2,1)S(1)}, u32[]{:S(2)}, u32[]{:S(2)}) collective-permute-start(bf16[16,40,128]{2,1,0:T(8,128)(2,1)S(1)} %pad_maximum_fusion.5), channel_id=1, source_target_pairs={{0,4},{1,5},{2,6},{3,7},{4,0},{5,1},{6,2},{7,3},{8,12},{9,13},{10,... | collective-permute-start | bytes 491528 | tf_op jit(solution)/shard_map/ppermute | solution.py:205
  13.1 1.3 %collective-permute-start.1 = (bf16[16,32,128]{2,1,0:T(8,128)(2,1)S(1)}, bf16[16,32,128]{2,1,0:T(8,128)(2,1)S(1)}, u32[]{:S(2)}, u32[]{:S(2)}) collective-permute-start(bf16[16,32,128]{2,1,0:T(8,128)(2,1)S(1)} %fusion.40), channel_id=1, source_target_pairs={{0,2},{1,3},{2,0},{3,1},{4,6},{5,7},{6,4},{7,5},{8,10},{9,11},{10,... | collective-permute-start | bytes 393224 | tf_op jit(solution)/shard_map/ppermute | solution.py:205
  14.5 2.1 %collective-permute-done.8 = bf16[16,40,128]{2,1,0:T(8,128)(2,1)S(1)} collective-permute-done((bf16[16,40,128]{2,1,0:T(8,128)(2,1)S(1)}, bf16[16,40,128]{2,1,0:T(8,128)(2,1)S(1)}, u32[]{:S(2)}, u32[]{:S(2)}) %collective-permute-start.8) | collective-permute-done | bytes 163872 | tf_op jit(solution)/shard_map/ppermute | solution.py:205
  16.6 0.1 fusion.17
  16.7 1.8 %collective-permute-start.9 = (bf16[16,32,128]{2,1,0:T(8,128)(2,1)S(1)}, bf16[16,32,128]{2,1,0:T(8,128)(2,1)S(1)}, u32[]{:S(2)}, u32[]{:S(2)}) collective-permute-start(bf16[16,32,128]{2,1,0:T(8,128)(2,1)S(1)} %fusion.17), channel_id=1, source_target_pairs={{0,8},{1,9},{2,10},{3,11},{4,12},{5,13},{6,14},{7,15},{8,0},{9,1},... | collective-permute-start | bytes 393224 | tf_op jit(solution)/shard_map/ppermute | solution.py:205
  18.6 1.4 %collective-permute-start.2 = (bf16[16,40,128]{2,1,0:T(8,128)(2,1)S(1)}, bf16[16,40,128]{2,1,0:T(8,128)(2,1)S(1)}, u32[]{:S(2)}, u32[]{:S(2)}) collective-permute-start(bf16[16,40,128]{2,1,0:T(8,128)(2,1)S(1)} %pad_maximum_fusion.4), channel_id=1, source_target_pairs={{0,4},{1,5},{2,6},{3,7},{4,0},{5,1},{6,2},{7,3},{8,12},{9,13},{10,... | collective-permute-start | bytes 491528 | tf_op jit(solution)/shard_map/ppermute | solution.py:205
  19.9 3.8 %collective-permute-done.9 = bf16[16,32,128]{2,1,0:T(8,128)(2,1)S(1)} collective-permute-done((bf16[16,32,128]{2,1,0:T(8,128)(2,1)S(1)}, bf16[16,32,128]{2,1,0:T(8,128)(2,1)S(1)}, u32[]{:S(2)}, u32[]{:S(2)}) %collective-permute-start.9) | collective-permute-done | bytes 131104 | tf_op jit(solution)/shard_map/ppermute | solution.py:205
  23.7 0.1 fusion.33
  23.8 0.1 collective-permute-start.10
  23.9 1.3 %collective-permute-done.2 = bf16[16,40,128]{2,1,0:T(8,128)(2,1)S(1)} collective-permute-done((bf16[16,40,128]{2,1,0:T(8,128)(2,1)S(1)}, bf16[16,40,128]{2,1,0:T(8,128)(2,1)S(1)}, u32[]{:S(2)}, u32[]{:S(2)}) %collective-permute-start.2) | collective-permute-done | bytes 163872 | tf_op jit(solution)/shard_map/ppermute | solution.py:205
  25.2 0.1 fusion.11
  25.3 0.1 collective-permute-start.3
  25.4 2.3 %collective-permute-done.10 = bf16[16,32,128]{2,1,0:T(8,128)(2,1)S(1)} collective-permute-done((bf16[16,32,128]{2,1,0:T(8,128)(2,1)S(1)}, bf16[16,32,128]{2,1,0:T(8,128)(2,1)S(1)}, u32[]{:S(2)}, u32[]{:S(2)}) %collective-permute-start.10) | collective-permute-done | bytes 131104 | tf_op jit(solution)/shard_map/ppermute | solution.py:205
  27.7 0.1 fusion.18
  27.8 0.1 add_convert_fusion.2
  27.9 4.1 %collective-permute-start.11 = (bf16[2,16,32,128]{3,2,1,0:T(8,128)(2,1)S(1)}, bf16[2,16,32,128]{3,2,1,0:T(8,128)(2,1)S(1)}, u32[]{:S(2)}, u32[]{:S(2)}) collective-permute-start(bf16[2,16,32,128]{3,2,1,0:T(8,128)(2,1)S(1)} %get-tuple-element.115), channel_id=1, source_target_pairs={{0,1},{1,0},{2,3},{3,2},{4,5},{5,4},{6,7},{7,6},{8,9},{9,8},{10,11... | collective-permute-start | bytes 786440 | tf_op jit(solution)/shard_map/ppermute | solution.py:205
  32.0 0.1 fusion.35
  32.1 0.8 collective-permute-start.4
  32.9 1.9 %shard_map.103 = (bf16[16,192,192]{2,1,0:T(8,128)(2,1)S(1)}, f32[192,2048]{1,0:T(8,128)S(1)}) custom-call(bf16[192,4096]{1,0:T(8,128)(2,1)S(1)} %copy-done.2, bf16[192,4096]{1,0:T(8,128)(2,1)S(1)} %copy-done, bf16[192,4096]{1,0:T(8,128)(2,1)S(1)} %copy-done.1), custom_call_target="tpu_custom_call" | custom-call | flops 301989888 | bytes 5111808 | tf_op jit(solution)/shard_map/pallas_call | solution.py:237
  34.8 1.9 %shard_map.101 = (bf16[16,192,192]{2,1,0:T(8,128)(2,1)S(1)}, f32[192,2048]{1,0:T(8,128)S(1)}) custom-call(bf16[192,4096]{1,0:T(8,128)(2,1)S(1)} %copy-done.2, bf16[192,4096]{1,0:T(8,128)(2,1)S(1)} %copy-done, bf16[192,4096]{1,0:T(8,128)(2,1)S(1)} %copy-done.1), custom_call_target="tpu_custom_call" | custom-call | flops 301989888 | bytes 5111808 | tf_op jit(solution)/shard_map/pallas_call | solution.py:237
  36.8 3.7 %shard_map.105 = (bf16[192,4096]{1,0:T(8,128)(2,1)}, bf16[192,2048]{1,0:T(8,128)(2,1)S(1)}, bf16[16,128,128]{2,1,0:T(8,128)(2,1)S(1)}, f32[2,16,32,128]{3,2,1,0:T(8,128)S(1)}, bf16[2,16,32,128]{3,2,1,0:T(8,128)(2,1)S(1)}) custom-call(s32[1]{0:T(128)} %bitcast.core_ref, bf16[192,4096]{1,0:T(8,128)(2,1)S(1)} %copy-done.2, ...), custom_call_target="tpu_custom_call" | custom-call | flops 201326592 | bytes 6561792 | tf_op jit(solution)/shard_map/pallas_call | solution.py:237
  40.5 3.4 %collective-permute-start.18 = (bf16[2,16,32,128]{3,2,1,0:T(8,128)(2,1)S(1)}, bf16[2,16,32,128]{3,2,1,0:T(8,128)(2,1)S(1)}, u32[]{:S(2)}, u32[]{:S(2)}) collective-permute-start(bf16[2,16,32,128]{3,2,1,0:T(8,128)(2,1)S(1)} %get-tuple-element.85), channel_id=1, source_target_pairs={{0,1},{1,0},{2,3},{3,2},{4,5},{5,4},{6,7},{7,6},{8,9},{9,8},{10,11... | collective-permute-start | bytes 786440 | tf_op jit(solution)/shard_map/ppermute | solution.py:205
  43.9 0.1 fusion.12
  44.0 0.1 add_convert_fusion.3
  44.2 0.1 collective-permute-start.5
  44.3 0.8 collective-permute-done.18
  45.2 0.8 collective-permute-start.19
  46.0 2.0 %shard_map.107 = (bf16[192,4096]{1,0:T(8,128)(2,1)}, f32[192,2048]{1,0:T(8,128)S(1)}, f32[192,2048]{1,0:T(8,128)S(1)}) custom-call(bf16[192,4096]{1,0:T(8,128)(2,1)S(1)} %copy-done.2, bf16[192,4096]{1,0:T(8,128)(2,1)S(1)} %copy-done, bf16[192,4096]{1,0:T(8,128)(2,1)S(1)} %copy-done.1, bf16[192,2048]{1,0:T(8,128)(2,1)S(1)} %get-tuple-element.67.gm_ref, ...), custom_call_target="tpu_custom_call" | custom-call | flops 352321536 | bytes 4390912 | tf_op jit(solution)/shard_map/pallas_call | solution.py:237
  48.0 2.0 %shard_map.108 = (bf16[192,4096]{1,0:T(8,128)(2,1)}, f32[192,2048]{1,0:T(8,128)S(1)}, f32[192,2048]{1,0:T(8,128)S(1)}) custom-call(bf16[192,4096]{1,0:T(8,128)(2,1)S(1)} %copy-done.2, bf16[192,4096]{1,0:T(8,128)(2,1)S(1)} %copy-done, bf16[192,4096]{1,0:T(8,128)(2,1)S(1)} %copy-done.1, ...), custom_call_target="tpu_custom_call", output_to_operand_aliasing={{0}: (6, {}), {1}: (7, {}), {2}: (8, {})} | custom-call | flops 352321536 | bytes 4390912 | tf_op jit(solution)/shard_map/pallas_call | solution.py:237
  50.0 3.7 %shard_map.106 = (bf16[192,4096]{1,0:T(8,128)(2,1)}, bf16[192,2048]{1,0:T(8,128)(2,1)S(1)}, bf16[16,128,128]{2,1,0:T(8,128)(2,1)S(1)}, f32[2,16,32,128]{3,2,1,0:T(8,128)S(1)}, bf16[2,16,32,128]{3,2,1,0:T(8,128)(2,1)S(1)}) custom-call(s32[1]{0:T(128)} %bitcast.core_ref, bf16[192,4096]{1,0:T(8,128)(2,1)S(1)} %copy-done.2, ...), custom_call_target="tpu_custom_call", output_to_operand_aliasing={{0}: (7, {})} | custom-call | flops 201326592 | bytes 6561792 | tf_op jit(solution)/shard_map/pallas_call | solution.py:237
  53.7 0.6 collective-permute-start.12
  54.3 2.0 %shard_map.109 = (bf16[192,4096]{1,0:T(8,128)(2,1)}, f32[192,2048]{1,0:T(8,128)S(1)}, f32[192,2048]{1,0:T(8,128)S(1)}) custom-call(bf16[192,4096]{1,0:T(8,128)(2,1)S(1)} %copy-done.2, bf16[192,4096]{1,0:T(8,128)(2,1)S(1)} %copy-done, bf16[192,4096]{1,0:T(8,128)(2,1)S(1)} %copy-done.1, ...), custom_call_target="tpu_custom_call", output_to_operand_aliasing={{0}: (6, {})} | custom-call | flops 352321536 | bytes 4390912 | tf_op jit(solution)/shard_map/pallas_call | solution.py:237
  56.4 2.0 %shard_map.110 = (bf16[192,4096]{1,0:T(8,128)(2,1)}, f32[192,2048]{1,0:T(8,128)S(1)}, f32[192,2048]{1,0:T(8,128)S(1)}) custom-call(bf16[192,4096]{1,0:T(8,128)(2,1)S(1)} %copy-done.2, bf16[192,4096]{1,0:T(8,128)(2,1)S(1)} %copy-done, bf16[192,4096]{1,0:T(8,128)(2,1)S(1)} %copy-done.1, ...), custom_call_target="tpu_custom_call", output_to_operand_aliasing={{0}: (6, {}), {1}: (7, {}), {2}: (8, {})} | custom-call | flops 352321536 | bytes 4390912 | tf_op jit(solution)/shard_map/pallas_call | solution.py:237
  58.6 0.1 convert_add_fusion.1
  58.7 0.8 collective-permute-start.13
  59.5 4.1 %collective-permute-done.20 = bf16[16,32,128]{2,1,0:T(8,128)(2,1)S(1)} collective-permute-done((bf16[16,32,128]{2,1,0:T(8,128)(2,1)S(1)}, bf16[16,32,128]{2,1,0:T(8,128)(2,1)S(1)}, u32[]{:S(2)}, u32[]{:S(2)}) %collective-permute-start.20) | collective-permute-done | bytes 131104 | tf_op jit(solution)/shard_map/ppermute | solution.py:205
  63.7 1.3 %collective-permute-start.21 = (bf16[16,32,128]{2,1,0:T(8,128)(2,1)S(1)}, bf16[16,32,128]{2,1,0:T(8,128)(2,1)S(1)}, u32[]{:S(2)}, u32[]{:S(2)}) collective-permute-start(bf16[16,32,128]{2,1,0:T(8,128)(2,1)S(1)} %get-tuple-element.91), channel_id=1, source_target_pairs={{0,8},{1,9},{2,10},{3,11},{4,12},{5,13},{6,14},{7,15},{8,0},{9,1},... | collective-permute-start | bytes 393224 | tf_op jit(solution)/shard_map/ppermute | solution.py:205
  65.0 1.2 %collective-permute-start.14 = (bf16[16,32,128]{2,1,0:T(8,128)(2,1)S(1)}, bf16[16,32,128]{2,1,0:T(8,128)(2,1)S(1)}, u32[]{:S(2)}, u32[]{:S(2)}) collective-permute-start(bf16[16,32,128]{2,1,0:T(8,128)(2,1)S(1)} %get-tuple-element.97), channel_id=1, source_target_pairs={{0,4},{1,5},{2,6},{3,7},{4,0},{5,1},{6,2},{7,3},{8,12},{9,13},{10,... | collective-permute-start | bytes 393224 | tf_op jit(solution)/shard_map/ppermute | solution.py:205
  66.3 6.7 %collective-permute-done.21 = bf16[16,32,128]{2,1,0:T(8,128)(2,1)S(1)} collective-permute-done((bf16[16,32,128]{2,1,0:T(8,128)(2,1)S(1)}, bf16[16,32,128]{2,1,0:T(8,128)(2,1)S(1)}, u32[]{:S(2)}, u32[]{:S(2)}) %collective-permute-start.21) | collective-permute-done | bytes 131104 | tf_op jit(solution)/shard_map/ppermute | solution.py:205
  72.9 0.1 fusion.29
  73.0 0.8 collective-permute-start.22
  73.9 0.1 collective-permute-start.15
  73.9 3.6 %collective-permute-done.22 = bf16[16,32,128]{2,1,0:T(8,128)(2,1)S(1)} collective-permute-done((bf16[16,32,128]{2,1,0:T(8,128)(2,1)S(1)}, bf16[16,32,128]{2,1,0:T(8,128)(2,1)S(1)}, u32[]{:S(2)}, u32[]{:S(2)}) %collective-permute-start.22) | collective-permute-done | bytes 131104 | tf_op jit(solution)/shard_map/ppermute | solution.py:205
  77.6 0.1 fusion.26
  77.7 4.6 %collective-permute-done.15 = bf16[16,32,128]{2,1,0:T(8,128)(2,1)S(1)} collective-permute-done((bf16[16,32,128]{2,1,0:T(8,128)(2,1)S(1)}, bf16[16,32,128]{2,1,0:T(8,128)(2,1)S(1)}, u32[]{:S(2)}, u32[]{:S(2)}) %collective-permute-start.15) | collective-permute-done | bytes 131104 | tf_op jit(solution)/shard_map/ppermute | solution.py:205
  82.3 0.1 fusion.31
  82.4 1.3 %collective-permute-start.16 = (bf16[16,32,128]{2,1,0:T(8,128)(2,1)S(1)}, bf16[16,32,128]{2,1,0:T(8,128)(2,1)S(1)}, u32[]{:S(2)}, u32[]{:S(2)}) collective-permute-start(bf16[16,32,128]{2,1,0:T(8,128)(2,1)S(1)} %fusion.31), channel_id=1, source_target_pairs={{0,2},{1,3},{2,0},{3,1},{4,6},{5,7},{6,4},{7,5},{8,10},{9,11},{10,... | collective-permute-start | bytes 393224 | tf_op jit(solution)/shard_map/ppermute | solution.py:205
  83.6 0.1 add_convert_fusion
  83.8 0.8 collective-permute-start.23
  84.6 2.4 %collective-permute-done.16 = bf16[16,32,128]{2,1,0:T(8,128)(2,1)S(1)} collective-permute-done((bf16[16,32,128]{2,1,0:T(8,128)(2,1)S(1)}, bf16[16,32,128]{2,1,0:T(8,128)(2,1)S(1)}, u32[]{:S(2)}, u32[]{:S(2)}) %collective-permute-start.16) | collective-permute-done | bytes 131104 | tf_op jit(solution)/shard_map/ppermute | solution.py:205
  87.0 0.1 fusion.22
  87.1 0.1 add_convert_fusion.1
  87.2 1.4 %collective-permute-start.17 = (bf16[2,16,32,128]{3,2,1,0:T(8,128)(2,1)S(1)}, bf16[2,16,32,128]{3,2,1,0:T(8,128)(2,1)S(1)}, u32[]{:S(2)}, u32[]{:S(2)}) collective-permute-start(bf16[2,16,32,128]{3,2,1,0:T(8,128)(2,1)S(1)} %get-tuple-element.111), channel_id=1, source_target_pairs={{0,1},{1,0},{2,3},{3,2},{4,5},{5,4},{6,7},{7,6},{8,9},{9,8},{10,11... | collective-permute-start | bytes 786440 | tf_op jit(solution)/shard_map/ppermute | solution.py:205
  88.8 0.7 pad_maximum_fusion.8
  89.4 2.6 %shard_map.111 = (bf16[192,4096]{1,0:T(8,128)(2,1)}, bf16[192,4096]{1,0:T(8,128)(2,1)}) custom-call(s32[1]{0:T(128)} %bitcast.core_ref, bf16[192,4096]{1,0:T(8,128)(2,1)S(1)} %copy-done, bf16[192,4096]{1,0:T(8,128)(2,1)S(1)} %copy-done.1, f32[192,2048]{1,0:T(8,128)S(1)} %get-tuple-element.82.kpart_ref, f32[192,2048]{1,0:T(8,128)S(1)} %get-tuple-element.83.vpart_ref, ...), custom_call_target="tpu_custom_call" | custom-call | flops 201326592 | bytes 6815744 | tf_op jit(solution)/shard_map/pallas_call | solution.py:237
  92.0 2.6 %shard_map.112 = (bf16[192,4096]{1,0:T(8,128)(2,1)}, bf16[192,4096]{1,0:T(8,128)(2,1)}) custom-call(s32[1]{0:T(128)} %bitcast.core_ref, bf16[192,4096]{1,0:T(8,128)(2,1)S(1)} %copy-done, bf16[192,4096]{1,0:T(8,128)(2,1)S(1)} %copy-done.1, f32[192,2048]{1,0:T(8,128)S(1)} %get-tuple-element.78.kpart_ref, ...), custom_call_target="tpu_custom_call", output_to_operand_aliasing={{0}: (7, {}), {1}: (8, {})} | custom-call | flops 201326592 | bytes 6815744 | tf_op jit(solution)/shard_map/pallas_call | solution.py:237
  (49 shorter events, 0.9 us)
Async XLA Ops:
  0.6 3.3 %copy-start = (bf16[192,4096]{1,0:T(8,128)(2,1)S(1)}, bf16[192,4096]{1,0:T(8,128)(2,1)}, u32[]{:S(2)}) copy-start(bf16[192,4096]{1,0:T(8,128)(2,1)} %k_ref.9) | copy-start | bytes 4718596
  0.7 3.3 %copy-start.1 = (bf16[192,4096]{1,0:T(8,128)(2,1)S(1)}, bf16[192,4096]{1,0:T(8,128)(2,1)}, u32[]{:S(2)}) copy-start(bf16[192,4096]{1,0:T(8,128)(2,1)} %v_ref.9) | copy-start | bytes 4718596
  3.8 2.0 %copy-start.5 = (f32[32,8,128]{2,1,0:T(8,128)S(1)}, f32[32,8,128]{2,1,0:T(8,128)}, u32[]{:S(2)}) copy-start(f32[32,8,128]{2,1,0:T(8,128)} %param.9) | copy-start | bytes 393220
  3.8 2.0 %collective-permute-start.6 = (bf16[2,16,32,128]{3,2,1,0:T(8,128)(2,1)S(1)}, bf16[2,16,32,128]{3,2,1,0:T(8,128)(2,1)S(1)}, u32[]{:S(2)}, u32[]{:S(2)}) collective-permute-start(bf16[2,16,32,128]{3,2,1,0:T(8,128)(2,1)S(1)} %get-tuple-element.61), channel_id=1, source_target_pairs={{0,1},{1,0},{2,3},{3,2},{4,5},{5,4},{6,7},{7,6},{8,9},{9,8},{10,11... | collective-permute-start | bytes 786440 | tf_op jit(solution)/shard_map/ppermute | solution.py:205
  5.3 3.0 %collective-permute-start = (bf16[2,16,32,128]{3,2,1,0:T(8,128)(2,1)S(1)}, bf16[2,16,32,128]{3,2,1,0:T(8,128)(2,1)S(1)}, u32[]{:S(2)}, u32[]{:S(2)}) collective-permute-start(bf16[2,16,32,128]{3,2,1,0:T(8,128)(2,1)S(1)} %get-tuple-element.55), channel_id=1, source_target_pairs={{0,1},{1,0},{2,3},{3,2},{4,5},{5,4},{6,7},{7,6},{8,9},{9,8},{10,11... | collective-permute-start | bytes 786440 | tf_op jit(solution)/shard_map/ppermute | solution.py:205
  6.0 5.7 %collective-permute-start.7 = (bf16[16,32,128]{2,1,0:T(8,128)(2,1)S(1)}, bf16[16,32,128]{2,1,0:T(8,128)(2,1)S(1)}, u32[]{:S(2)}, u32[]{:S(2)}) collective-permute-start(bf16[16,32,128]{2,1,0:T(8,128)(2,1)S(1)} %fusion.41), channel_id=1, source_target_pairs={{0,2},{1,3},{2,0},{3,1},{4,6},{5,7},{6,4},{7,5},{8,10},{9,11},{10,... | collective-permute-start | bytes 393224 | tf_op jit(solution)/shard_map/ppermute | solution.py:205
  11.8 4.8 %collective-permute-start.8 = (bf16[16,40,128]{2,1,0:T(8,128)(2,1)S(1)}, bf16[16,40,128]{2,1,0:T(8,128)(2,1)S(1)}, u32[]{:S(2)}, u32[]{:S(2)}) collective-permute-start(bf16[16,40,128]{2,1,0:T(8,128)(2,1)S(1)} %pad_maximum_fusion.5), channel_id=1, source_target_pairs={{0,4},{1,5},{2,6},{3,7},{4,0},{5,1},{6,2},{7,3},{8,12},{9,13},{10,... | collective-permute-start | bytes 491528 | tf_op jit(solution)/shard_map/ppermute | solution.py:205
  13.1 5.4 %collective-permute-start.1 = (bf16[16,32,128]{2,1,0:T(8,128)(2,1)S(1)}, bf16[16,32,128]{2,1,0:T(8,128)(2,1)S(1)}, u32[]{:S(2)}, u32[]{:S(2)}) collective-permute-start(bf16[16,32,128]{2,1,0:T(8,128)(2,1)S(1)} %fusion.40), channel_id=1, source_target_pairs={{0,2},{1,3},{2,0},{3,1},{4,6},{5,7},{6,4},{7,5},{8,10},{9,11},{10,... | collective-permute-start | bytes 393224 | tf_op jit(solution)/shard_map/ppermute | solution.py:205
  16.7 7.0 %collective-permute-start.9 = (bf16[16,32,128]{2,1,0:T(8,128)(2,1)S(1)}, bf16[16,32,128]{2,1,0:T(8,128)(2,1)S(1)}, u32[]{:S(2)}, u32[]{:S(2)}) collective-permute-start(bf16[16,32,128]{2,1,0:T(8,128)(2,1)S(1)} %fusion.17), channel_id=1, source_target_pairs={{0,8},{1,9},{2,10},{3,11},{4,12},{5,13},{6,14},{7,15},{8,0},{9,1},... | collective-permute-start | bytes 393224 | tf_op jit(solution)/shard_map/ppermute | solution.py:205
  18.6 6.6 %collective-permute-start.2 = (bf16[16,40,128]{2,1,0:T(8,128)(2,1)S(1)}, bf16[16,40,128]{2,1,0:T(8,128)(2,1)S(1)}, u32[]{:S(2)}, u32[]{:S(2)}) collective-permute-start(bf16[16,40,128]{2,1,0:T(8,128)(2,1)S(1)} %pad_maximum_fusion.4), channel_id=1, source_target_pairs={{0,4},{1,5},{2,6},{3,7},{4,0},{5,1},{6,2},{7,3},{8,12},{9,13},{10,... | collective-permute-start | bytes 491528 | tf_op jit(solution)/shard_map/ppermute | solution.py:205
  23.8 3.9 %collective-permute-start.10 = (bf16[16,32,128]{2,1,0:T(8,128)(2,1)S(1)}, bf16[16,32,128]{2,1,0:T(8,128)(2,1)S(1)}, u32[]{:S(2)}, u32[]{:S(2)}) collective-permute-start(bf16[16,32,128]{2,1,0:T(8,128)(2,1)S(1)} %fusion.33), channel_id=1, source_target_pairs={{0,2},{1,3},{2,0},{3,1},{4,6},{5,7},{6,4},{7,5},{8,10},{9,11},{10,... | collective-permute-start | bytes 393224 | tf_op jit(solution)/shard_map/ppermute | solution.py:205
  25.3 6.7 %collective-permute-start.3 = (bf16[16,32,128]{2,1,0:T(8,128)(2,1)S(1)}, bf16[16,32,128]{2,1,0:T(8,128)(2,1)S(1)}, u32[]{:S(2)}, u32[]{:S(2)}) collective-permute-start(bf16[16,32,128]{2,1,0:T(8,128)(2,1)S(1)} %fusion.11), channel_id=1, source_target_pairs={{0,8},{1,9},{2,10},{3,11},{4,12},{5,13},{6,14},{7,15},{8,0},{9,1},... | collective-permute-start | bytes 393224 | tf_op jit(solution)/shard_map/ppermute | solution.py:205
  27.8 5.1 %copy-start.2 = (bf16[192,4096]{1,0:T(8,128)(2,1)S(1)}, bf16[192,4096]{1,0:T(8,128)(2,1)}, u32[]{:S(2)}) copy-start(bf16[192,4096]{1,0:T(8,128)(2,1)} %q_ref.15) | copy-start | bytes 4718596
  27.9 8.8 %collective-permute-start.11 = (bf16[2,16,32,128]{3,2,1,0:T(8,128)(2,1)S(1)}, bf16[2,16,32,128]{3,2,1,0:T(8,128)(2,1)S(1)}, u32[]{:S(2)}, u32[]{:S(2)}) collective-permute-start(bf16[2,16,32,128]{3,2,1,0:T(8,128)(2,1)S(1)} %get-tuple-element.115), channel_id=1, source_target_pairs={{0,1},{1,0},{2,3},{3,2},{4,5},{5,4},{6,7},{7,6},{8,9},{9,8},{10,11... | collective-permute-start | bytes 786440 | tf_op jit(solution)/shard_map/ppermute | solution.py:205
  32.1 11.8 %collective-permute-start.4 = (bf16[16,32,128]{2,1,0:T(8,128)(2,1)S(1)}, bf16[16,32,128]{2,1,0:T(8,128)(2,1)S(1)}, u32[]{:S(2)}, u32[]{:S(2)}) collective-permute-start(bf16[16,32,128]{2,1,0:T(8,128)(2,1)S(1)} %fusion.35), channel_id=1, source_target_pairs={{0,2},{1,3},{2,0},{3,1},{4,6},{5,7},{6,4},{7,5},{8,10},{9,11},{10,... | collective-permute-start | bytes 393224 | tf_op jit(solution)/shard_map/ppermute | solution.py:205
  34.8 2.0 %copy-start.3 = (bf16[192,4096]{1,0:T(8,128)(2,1)S(1)}, bf16[192,4096]{1,0:T(8,128)(2,1)}, u32[]{:S(2)}) copy-start(bf16[192,4096]{1,0:T(8,128)(2,1)} %do_ref.3) | copy-start | bytes 4718596
  34.8 2.0 %copy-start.4 = (f32[4096]{0:T(1024)S(1)}, f32[4096]{0:T(1024)}, u32[]{:S(2)}) copy-start(f32[4096]{0:T(1024)} %param.10) | copy-start | bytes 49156
  40.5 4.6 %collective-permute-start.18 = (bf16[2,16,32,128]{3,2,1,0:T(8,128)(2,1)S(1)}, bf16[2,16,32,128]{3,2,1,0:T(8,128)(2,1)S(1)}, u32[]{:S(2)}, u32[]{:S(2)}) collective-permute-start(bf16[2,16,32,128]{3,2,1,0:T(8,128)(2,1)S(1)} %get-tuple-element.85), channel_id=1, source_target_pairs={{0,1},{1,0},{2,3},{3,2},{4,5},{5,4},{6,7},{7,6},{8,9},{9,8},{10,11... | collective-permute-start | bytes 786440 | tf_op jit(solution)/shard_map/ppermute | solution.py:205
  44.2 5.8 %collective-permute-start.5 = (bf16[2,16,32,128]{3,2,1,0:T(8,128)(2,1)S(1)}, bf16[2,16,32,128]{3,2,1,0:T(8,128)(2,1)S(1)}, u32[]{:S(2)}, u32[]{:S(2)}) collective-permute-start(bf16[2,16,32,128]{3,2,1,0:T(8,128)(2,1)S(1)} %get-tuple-element.117), channel_id=1, source_target_pairs={{0,1},{1,0},{2,3},{3,2},{4,5},{5,4},{6,7},{7,6},{8,9},{9,8},{10,11... | collective-permute-start | bytes 786440 | tf_op jit(solution)/shard_map/ppermute | solution.py:205
  45.2 13.2 %collective-permute-start.19 = (bf16[16,32,128]{2,1,0:T(8,128)(2,1)S(1)}, bf16[16,32,128]{2,1,0:T(8,128)(2,1)S(1)}, u32[]{:S(2)}, u32[]{:S(2)}) collective-permute-start(bf16[16,32,128]{2,1,0:T(8,128)(2,1)S(1)} %fusion.43), channel_id=1, source_target_pairs={{0,2},{1,3},{2,0},{3,1},{4,6},{5,7},{6,4},{7,5},{8,10},{9,11},{10,... | collective-permute-start | bytes 393224 | tf_op jit(solution)/shard_map/ppermute | solution.py:205
  53.7 4.9 %collective-permute-start.12 = (bf16[2,16,32,128]{3,2,1,0:T(8,128)(2,1)S(1)}, bf16[2,16,32,128]{3,2,1,0:T(8,128)(2,1)S(1)}, u32[]{:S(2)}, u32[]{:S(2)}) collective-permute-start(bf16[2,16,32,128]{3,2,1,0:T(8,128)(2,1)S(1)} %get-tuple-element.81), channel_id=1, source_target_pairs={{0,1},{1,0},{2,3},{3,2},{4,5},{5,4},{6,7},{7,6},{8,9},{9,8},{10,11... | collective-permute-start | bytes 786440 | tf_op jit(solution)/shard_map/ppermute | solution.py:205
  58.5 5.1 %collective-permute-start.20 = (bf16[16,32,128]{2,1,0:T(8,128)(2,1)S(1)}, bf16[16,32,128]{2,1,0:T(8,128)(2,1)S(1)}, u32[]{:S(2)}, u32[]{:S(2)}) collective-permute-start(bf16[16,32,128]{2,1,0:T(8,128)(2,1)S(1)} %get-tuple-element.93), channel_id=1, source_target_pairs={{0,4},{1,5},{2,6},{3,7},{4,0},{5,1},{6,2},{7,3},{8,12},{9,13},{10,... | collective-permute-start | bytes 393224 | tf_op jit(solution)/shard_map/ppermute | solution.py:205
  58.7 6.2 %collective-permute-start.13 = (bf16[16,32,128]{2,1,0:T(8,128)(2,1)S(1)}, bf16[16,32,128]{2,1,0:T(8,128)(2,1)S(1)}, u32[]{:S(2)}, u32[]{:S(2)}) collective-permute-start(bf16[16,32,128]{2,1,0:T(8,128)(2,1)S(1)} %fusion.42), channel_id=1, source_target_pairs={{0,2},{1,3},{2,0},{3,1},{4,6},{5,7},{6,4},{7,5},{8,10},{9,11},{10,... | collective-permute-start | bytes 393224 | tf_op jit(solution)/shard_map/ppermute | solution.py:205
  63.7 9.2 %collective-permute-start.21 = (bf16[16,32,128]{2,1,0:T(8,128)(2,1)S(1)}, bf16[16,32,128]{2,1,0:T(8,128)(2,1)S(1)}, u32[]{:S(2)}, u32[]{:S(2)}) collective-permute-start(bf16[16,32,128]{2,1,0:T(8,128)(2,1)S(1)} %get-tuple-element.91), channel_id=1, source_target_pairs={{0,8},{1,9},{2,10},{3,11},{4,12},{5,13},{6,14},{7,15},{8,0},{9,1},... | collective-permute-start | bytes 393224 | tf_op jit(solution)/shard_map/ppermute | solution.py:205
  65.0 8.8 %collective-permute-start.14 = (bf16[16,32,128]{2,1,0:T(8,128)(2,1)S(1)}, bf16[16,32,128]{2,1,0:T(8,128)(2,1)S(1)}, u32[]{:S(2)}, u32[]{:S(2)}) collective-permute-start(bf16[16,32,128]{2,1,0:T(8,128)(2,1)S(1)} %get-tuple-element.97), channel_id=1, source_target_pairs={{0,4},{1,5},{2,6},{3,7},{4,0},{5,1},{6,2},{7,3},{8,12},{9,13},{10,... | collective-permute-start | bytes 393224 | tf_op jit(solution)/shard_map/ppermute | solution.py:205
  73.0 4.6 %collective-permute-start.22 = (bf16[16,32,128]{2,1,0:T(8,128)(2,1)S(1)}, bf16[16,32,128]{2,1,0:T(8,128)(2,1)S(1)}, u32[]{:S(2)}, u32[]{:S(2)}) collective-permute-start(bf16[16,32,128]{2,1,0:T(8,128)(2,1)S(1)} %fusion.29), channel_id=1, source_target_pairs={{0,2},{1,3},{2,0},{3,1},{4,6},{5,7},{6,4},{7,5},{8,10},{9,11},{10,... | collective-permute-start | bytes 393224 | tf_op jit(solution)/shard_map/ppermute | solution.py:205
  73.9 8.4 %collective-permute-start.15 = (bf16[16,32,128]{2,1,0:T(8,128)(2,1)S(1)}, bf16[16,32,128]{2,1,0:T(8,128)(2,1)S(1)}, u32[]{:S(2)}, u32[]{:S(2)}) collective-permute-start(bf16[16,32,128]{2,1,0:T(8,128)(2,1)S(1)} %get-tuple-element.95), channel_id=1, source_target_pairs={{0,8},{1,9},{2,10},{3,11},{4,12},{5,13},{6,14},{7,15},{8,0},{9,1},... | collective-permute-start | bytes 393224 | tf_op jit(solution)/shard_map/ppermute | solution.py:205
  82.4 4.6 %collective-permute-start.16 = (bf16[16,32,128]{2,1,0:T(8,128)(2,1)S(1)}, bf16[16,32,128]{2,1,0:T(8,128)(2,1)S(1)}, u32[]{:S(2)}, u32[]{:S(2)}) collective-permute-start(bf16[16,32,128]{2,1,0:T(8,128)(2,1)S(1)} %fusion.31), channel_id=1, source_target_pairs={{0,2},{1,3},{2,0},{3,1},{4,6},{5,7},{6,4},{7,5},{8,10},{9,11},{10,... | collective-permute-start | bytes 393224 | tf_op jit(solution)/shard_map/ppermute | solution.py:205
  83.8 5.6 %collective-permute-start.23 = (bf16[2,16,32,128]{3,2,1,0:T(8,128)(2,1)S(1)}, bf16[2,16,32,128]{3,2,1,0:T(8,128)(2,1)S(1)}, u32[]{:S(2)}, u32[]{:S(2)}) collective-permute-start(bf16[2,16,32,128]{3,2,1,0:T(8,128)(2,1)S(1)} %get-tuple-element.107), channel_id=1, source_target_pairs={{0,1},{1,0},{2,3},{3,2},{4,5},{5,4},{6,7},{7,6},{8,9},{9,8},{10,11... | collective-permute-start | bytes 786440 | tf_op jit(solution)/shard_map/ppermute | solution.py:205
  87.2 4.7 %collective-permute-start.17 = (bf16[2,16,32,128]{3,2,1,0:T(8,128)(2,1)S(1)}, bf16[2,16,32,128]{3,2,1,0:T(8,128)(2,1)S(1)}, u32[]{:S(2)}, u32[]{:S(2)}) collective-permute-start(bf16[2,16,32,128]{3,2,1,0:T(8,128)(2,1)S(1)} %get-tuple-element.111), channel_id=1, source_target_pairs={{0,1},{1,0},{2,3},{3,2},{4,5},{5,4},{6,7},{7,6},{8,9},{9,8},{10,11... | collective-permute-start | bytes 786440 | tf_op jit(solution)/shard_map/ppermute | solution.py:205

commit v3 on v2

--- a/solution.py
+++ b/solution.py
@@ -11,10 +11,10 @@
 
 BF16 = jnp.bfloat16
 F32 = jnp.float32
-CHUNKS = 2
-HEAD_BLOCK = 4
-LOCAL_SPLIT = 2
-VMEM_LIMIT = 6 * 1024 * 1024
+CHUNK_EIGHTHS = (4, 4)
+BLOCKS = {"state": 8, "intra": 16, "mix": 16, "local": 16, "final": 16}
+LOCAL_SPLIT = 1
+VMEM_LIMIT = 20 * 1024 * 1024
 
 
 def causal_mask(count):
@@ -183,8 +183,10 @@
     tokens, width = queries.shape
     heads, owned, dim = carried_state.shape
     slab_rows = dim // 4
-    part = heads // CHUNKS
-    hb = HEAD_BLOCK
+    bounds = [0]
+    for share in CHUNK_EIGHTHS:
+        bounds.append(bounds[-1] + heads * share // sum(CHUNK_EIGHTHS))
+    chunks = range(len(CHUNK_EIGHTHS))
     rank = lax.axis_index("ctx").astype(jnp.int32)
     core_arg = (rank & 1).reshape(1)
     odd_core, odd_pair = (rank & 1) == 1, (rank & 2) == 2
@@ -204,10 +206,12 @@
     def swap(x, bit):
         return lax.ppermute(x, "ctx", [(i, i ^ bit) for i in range(n)])
 
-    def call(body, chunk, ins, outs, flops, with_core=True, keep=(), sub=0, subs=1):
-        count = part // hb // subs
-        first = sub * count
-        off = chunk * (part // hb) + first
+    def call(name, body, chunk, ins, outs, flops, with_core=True, keep=(), sub=0, subs=1):
+        part = bounds[chunk + 1] - bounds[chunk]
+        hb = BLOCKS[name]
+        cuts = [part // hb * i // subs for i in range(subs + 1)]
+        first, count = cuts[sub], cuts[sub + 1] - cuts[sub]
+        off = bounds[chunk] // hb + first
         specs = {
             "flat": pl.BlockSpec((tokens, hb * dim), lambda i, *_: (0, i + off)),
             "row": pl.BlockSpec((1, hb * dim), lambda i, *_: (0, i + off)),
@@ -296,7 +300,6 @@
         return own_half, got_half, total
 
     mac = 2 * tokens * dim
-    chunks = range(CHUNKS)
     states, intras, priors, mixes, locals_ = [], [], [], [], []
     for g in chunks:
         pair = (keys, values)
@@ -304,13 +307,13 @@
             pair = [pltpu.with_memory_space_constraint(x, pltpu.HBM) for x in pair]
         ins = [("flat", x) for x in pair]
         outs = [("half", F32), ("half", BF16)]
-        states.append(call(state_kernel, g, ins, outs, mac * dim))
+        states.append(call("state", state_kernel, g, ins, outs, mac * dim))
     for g in chunks:
         ins = [("flat", queries), ("flat", keys), ("flat", values)]
         outs = [("sq", BF16), ("local", F32)]
-        intras.append(call(intra_kernel, g, ins, outs, 2 * mac * tokens, with_core=False))
-    for g in chunks:
-        carried = carried_state[g * part : (g + 1) * part].astype(BF16)
+        intras.append(call("intra", intra_kernel, g, ins, outs, 2 * mac * tokens, with_core=False))
+    for g in chunks:
+        carried = carried_state[bounds[g] : bounds[g + 1]].astype(BF16)
         priors.append(scan_out(*states[g], carried))
     keep = []
     for g in chunks:
@@ -323,7 +326,7 @@
             ("flat", out_grad),
         ]
         outs = [("flat", BF16), ("local", BF16), ("state", BF16), ("half", F32), ("half", BF16)]
-        mixes.append(call(mix_kernel, g, ins, outs, 2 * mac * dim, keep=keep))
+        mixes.append(call("mix", mix_kernel, g, ins, outs, 2 * mac * dim, keep=keep))
         keep = [(0, mixes[g][0])]
     keep = []
     for g in chunks:
@@ -339,7 +342,7 @@
         flops = 4 * mac * tokens + mac * dim
         for sub in range(LOCAL_SPLIT):
             at = dict(sub=sub, subs=LOCAL_SPLIT)
-            made = call(local_grad_kernel, g, ins, outs, flops, False, keep, **at)
+            made = call("local", local_grad_kernel, g, ins, outs, flops, False, keep, **at)
             keep = list(enumerate(made))
         locals_.append(made)
         keep = [(0, made[0])]
@@ -354,11 +357,12 @@
             ("half", laters[g][0]),
             ("half", laters[g][1]),
         ]
-        made = call(final_kernel, g, ins, [("flat", BF16)] * 2, 2 * mac * dim, keep=keep)
+        made = call("final", final_kernel, g, ins, [("flat", BF16)] * 2, 2 * mac * dim, keep=keep)
         keep = list(enumerate(made))
     zero = jnp.uint32(0)
     owned_rows = [
-        lax.dynamic_slice(later, (zero, owned_at, zero), (part, owned, dim)) for _, _, later in laters
+        lax.dynamic_slice(later, (zero, owned_at, zero), later.shape[:1] + (owned, dim))
+        for _, _, later in laters
     ]
     state_grad = jnp.concatenate(owned_rows, axis=0)
     return mixes[-1][0], locals_[-1][0], made[0], made[1], state_grad
@@ -368,7 +372,7 @@
     heads, owned, dim = carried_state.shape
     power = n >= 4 and (n & (n - 1)) == 0
     fits = power and owned % 8 == 0 and owned == 8 and dim % 128 == 0
-    if fits and heads % (CHUNKS * HEAD_BLOCK) == 0 and queries.shape[0] % 16 == 0:
+    if fits and heads % 8 == 0 and queries.shape[0] % 16 == 0:
         return fused_on_device(n, queries, keys, values, carried_state, gain, out_grad)
     return plain_on_device(queries, keys, values, carried_state, gain, out_grad)
 

time: 94.7 us -> 86.3 us (0.911)
  the two profiles are of different devices: /device:TPU:1 before, /device:TPU:0 now
where the time goes in v3:
time: 86.3 us; the launch traced here: 86.1 us
  waiting for transfers between devices  37.6 us (44%)
  starting transfers between devices  24.3 us (28%)
  Pallas kernels  19.5 us (23%)
  other arithmetic  3.23 us (4%)
  between operations  1.04 us (1%)
    ppermute x24, waiting for transfers between devices, swap(): return lax.ppermute(x, 'ctx', [(i, i ^ bit) for i in range(n)])  37.6 us
    ppermute x24, starting transfers between devices, swap(): return lax.ppermute(x, 'ctx', [(i, i ^ bit) for i in range(n)])  24.3 us
    pallas_call x10, Pallas kernels, call(): pl.pallas_call(body, out_shape=[jax.ShapeDtypeStruct(shapes[kind], t) for...  19.5 us
  transfers between devices with their start and end apart: 24, of which 11 were waited for; matrix products, arithmetic and copies ran while one was open for 4% of the time, Pallas kernels for 18%

profile of v3, /device:TPU:0, one launch (start us, length us, event | category | flops | bytes accessed | tf_op | source)
XLA Modules:
  0.0 86.1 jit_solution(18416229100706066854)
XLA Ops:
  0.7 2.1 %shard_map.104 = (f32[2,16,32,128]{3,2,1,0:T(8,128)S(1)}, bf16[2,16,32,128]{3,2,1,0:T(8,128)(2,1)S(1)}) custom-call(s32[1]{0:T(128)} %bitcast.core_ref, bf16[192,4096]{1,0:T(8,128)(2,1)} %k_ref.7, bf16[192,4096]{1,0:T(8,128)(2,1)} %v_ref.7), custom_call_target="tpu_custom_call" | custom-call | flops 100663296 | bytes 2359296 | tf_op jit(solution)/shard_map/pallas_call | solution.py:241
  2.7 0.6 collective-permute-start.6
  3.3 0.9 %shard_map.102 = (f32[2,16,32,128]{3,2,1,0:T(8,128)S(1)}, bf16[2,16,32,128]{3,2,1,0:T(8,128)(2,1)S(1)}) custom-call(s32[1]{0:T(128)} %bitcast.core_ref, bf16[192,4096]{1,0:T(8,128)(2,1)S(1)} %copy-done, bf16[192,4096]{1,0:T(8,128)(2,1)S(1)} %copy-done.1), custom_call_target="tpu_custom_call" | custom-call | flops 100663296 | bytes 2359296 | tf_op jit(solution)/shard_map/pallas_call | solution.py:241
  4.2 0.3 collective-permute-start
  4.5 0.1 convert_add_fusion.2
  4.6 2.9 %collective-permute-start.7 = (bf16[16,32,128]{2,1,0:T(8,128)(2,1)S(1)}, bf16[16,32,128]{2,1,0:T(8,128)(2,1)S(1)}, u32[]{:S(2)}, u32[]{:S(2)}) collective-permute-start(bf16[16,32,128]{2,1,0:T(8,128)(2,1)S(1)} %fusion.41), channel_id=1, source_target_pairs={{0,2},{1,3},{2,0},{3,1},{4,6},{5,7},{6,4},{7,5},{8,10},{9,11},{10,... | collective-permute-start | bytes 393224 | tf_op jit(solution)/shard_map/ppermute | solution.py:207
  7.5 0.1 convert_add_fusion.3
  7.6 3.8 %collective-permute-done.7 = bf16[16,32,128]{2,1,0:T(8,128)(2,1)S(1)} collective-permute-done((bf16[16,32,128]{2,1,0:T(8,128)(2,1)S(1)}, bf16[16,32,128]{2,1,0:T(8,128)(2,1)S(1)}, u32[]{:S(2)}, u32[]{:S(2)}) %collective-permute-start.7) | collective-permute-done | bytes 131104 | tf_op jit(solution)/shard_map/ppermute | solution.py:207
  11.5 1.9 %collective-permute-start.8 = (bf16[16,40,128]{2,1,0:T(8,128)(2,1)S(1)}, bf16[16,40,128]{2,1,0:T(8,128)(2,1)S(1)}, u32[]{:S(2)}, u32[]{:S(2)}) collective-permute-start(bf16[16,40,128]{2,1,0:T(8,128)(2,1)S(1)} %pad_maximum_fusion.5), channel_id=1, source_target_pairs={{0,4},{1,5},{2,6},{3,7},{4,0},{5,1},{6,2},{7,3},{8,12},{9,13},{10,... | collective-permute-start | bytes 491528 | tf_op jit(solution)/shard_map/ppermute | solution.py:207
  13.3 1.6 %collective-permute-start.1 = (bf16[16,32,128]{2,1,0:T(8,128)(2,1)S(1)}, bf16[16,32,128]{2,1,0:T(8,128)(2,1)S(1)}, u32[]{:S(2)}, u32[]{:S(2)}) collective-permute-start(bf16[16,32,128]{2,1,0:T(8,128)(2,1)S(1)} %fusion.40), channel_id=1, source_target_pairs={{0,2},{1,3},{2,0},{3,1},{4,6},{5,7},{6,4},{7,5},{8,10},{9,11},{10,... | collective-permute-start | bytes 393224 | tf_op jit(solution)/shard_map/ppermute | solution.py:207
  14.9 2.3 %collective-permute-done.8 = bf16[16,40,128]{2,1,0:T(8,128)(2,1)S(1)} collective-permute-done((bf16[16,40,128]{2,1,0:T(8,128)(2,1)S(1)}, bf16[16,40,128]{2,1,0:T(8,128)(2,1)S(1)}, u32[]{:S(2)}, u32[]{:S(2)}) %collective-permute-start.8) | collective-permute-done | bytes 163872 | tf_op jit(solution)/shard_map/ppermute | solution.py:207
  17.3 0.1 fusion.17
  17.4 2.6 %collective-permute-start.9 = (bf16[16,32,128]{2,1,0:T(8,128)(2,1)S(1)}, bf16[16,32,128]{2,1,0:T(8,128)(2,1)S(1)}, u32[]{:S(2)}, u32[]{:S(2)}) collective-permute-start(bf16[16,32,128]{2,1,0:T(8,128)(2,1)S(1)} %fusion.17), channel_id=1, source_target_pairs={{0,8},{1,9},{2,10},{3,11},{4,12},{5,13},{6,14},{7,15},{8,0},{9,1},... | collective-permute-start | bytes 393224 | tf_op jit(solution)/shard_map/ppermute | solution.py:207
  20.1 1.6 %collective-permute-start.2 = (bf16[16,40,128]{2,1,0:T(8,128)(2,1)S(1)}, bf16[16,40,128]{2,1,0:T(8,128)(2,1)S(1)}, u32[]{:S(2)}, u32[]{:S(2)}) collective-permute-start(bf16[16,40,128]{2,1,0:T(8,128)(2,1)S(1)} %pad_maximum_fusion.4), channel_id=1, source_target_pairs={{0,4},{1,5},{2,6},{3,7},{4,0},{5,1},{6,2},{7,3},{8,12},{9,13},{10,... | collective-permute-start | bytes 491528 | tf_op jit(solution)/shard_map/ppermute | solution.py:207
  21.7 3.7 %collective-permute-done.9 = bf16[16,32,128]{2,1,0:T(8,128)(2,1)S(1)} collective-permute-done((bf16[16,32,128]{2,1,0:T(8,128)(2,1)S(1)}, bf16[16,32,128]{2,1,0:T(8,128)(2,1)S(1)}, u32[]{:S(2)}, u32[]{:S(2)}) %collective-permute-start.9) | collective-permute-done | bytes 131104 | tf_op jit(solution)/shard_map/ppermute | solution.py:207
  25.4 0.1 fusion.33
  25.5 1.2 %collective-permute-start.10 = (bf16[16,32,128]{2,1,0:T(8,128)(2,1)S(1)}, bf16[16,32,128]{2,1,0:T(8,128)(2,1)S(1)}, u32[]{:S(2)}, u32[]{:S(2)}) collective-permute-start(bf16[16,32,128]{2,1,0:T(8,128)(2,1)S(1)} %fusion.33), channel_id=1, source_target_pairs={{0,2},{1,3},{2,0},{3,1},{4,6},{5,7},{6,4},{7,5},{8,10},{9,11},{10,... | collective-permute-start | bytes 393224 | tf_op jit(solution)/shard_map/ppermute | solution.py:207
  26.8 0.1 fusion.11
  26.9 1.6 %collective-permute-start.3 = (bf16[16,32,128]{2,1,0:T(8,128)(2,1)S(1)}, bf16[16,32,128]{2,1,0:T(8,128)(2,1)S(1)}, u32[]{:S(2)}, u32[]{:S(2)}) collective-permute-start(bf16[16,32,128]{2,1,0:T(8,128)(2,1)S(1)} %fusion.11), channel_id=1, source_target_pairs={{0,8},{1,9},{2,10},{3,11},{4,12},{5,13},{6,14},{7,15},{8,0},{9,1},... | collective-permute-start | bytes 393224 | tf_op jit(solution)/shard_map/ppermute | solution.py:207
  28.5 2.0 %collective-permute-done.10 = bf16[16,32,128]{2,1,0:T(8,128)(2,1)S(1)} collective-permute-done((bf16[16,32,128]{2,1,0:T(8,128)(2,1)S(1)}, bf16[16,32,128]{2,1,0:T(8,128)(2,1)S(1)}, u32[]{:S(2)}, u32[]{:S(2)}) %collective-permute-start.10) | collective-permute-done | bytes 131104 | tf_op jit(solution)/shard_map/ppermute | solution.py:207
  30.6 0.1 fusion.18
  30.7 0.1 add_convert_fusion.2
  30.8 0.1 collective-permute-start.11
  30.9 3.3 %collective-permute-done.3 = bf16[16,32,128]{2,1,0:T(8,128)(2,1)S(1)} collective-permute-done((bf16[16,32,128]{2,1,0:T(8,128)(2,1)S(1)}, bf16[16,32,128]{2,1,0:T(8,128)(2,1)S(1)}, u32[]{:S(2)}, u32[]{:S(2)}) %collective-permute-start.3) | collective-permute-done | bytes 131104 | tf_op jit(solution)/shard_map/ppermute | solution.py:207
  34.2 0.1 fusion.35
  34.3 1.2 %collective-permute-start.4 = (bf16[16,32,128]{2,1,0:T(8,128)(2,1)S(1)}, bf16[16,32,128]{2,1,0:T(8,128)(2,1)S(1)}, u32[]{:S(2)}, u32[]{:S(2)}) collective-permute-start(bf16[16,32,128]{2,1,0:T(8,128)(2,1)S(1)} %fusion.35), channel_id=1, source_target_pairs={{0,2},{1,3},{2,0},{3,1},{4,6},{5,7},{6,4},{7,5},{8,10},{9,11},{10,... | collective-permute-start | bytes 393224 | tf_op jit(solution)/shard_map/ppermute | solution.py:207
  35.5 1.0 %shard_map.103 = (bf16[16,192,192]{2,1,0:T(8,128)(2,1)S(1)}, f32[192,2048]{1,0:T(8,128)S(1)}) custom-call(bf16[192,4096]{1,0:T(8,128)(2,1)S(1)} %copy-done.2, bf16[192,4096]{1,0:T(8,128)(2,1)S(1)} %copy-done, bf16[192,4096]{1,0:T(8,128)(2,1)S(1)} %copy-done.1), custom_call_target="tpu_custom_call" | custom-call | flops 301989888 | bytes 5111808 | tf_op jit(solution)/shard_map/pallas_call | solution.py:241
  36.6 1.0 %shard_map.101 = (bf16[16,192,192]{2,1,0:T(8,128)(2,1)S(1)}, f32[192,2048]{1,0:T(8,128)S(1)}) custom-call(bf16[192,4096]{1,0:T(8,128)(2,1)S(1)} %copy-done.2, bf16[192,4096]{1,0:T(8,128)(2,1)S(1)} %copy-done, bf16[192,4096]{1,0:T(8,128)(2,1)S(1)} %copy-done.1), custom_call_target="tpu_custom_call" | custom-call | flops 301989888 | bytes 5111808 | tf_op jit(solution)/shard_map/pallas_call | solution.py:241
  37.6 0.3 copy-done.3
  37.9 2.7 %shard_map.105 = (bf16[192,4096]{1,0:T(8,128)(2,1)}, bf16[192,2048]{1,0:T(8,128)(2,1)S(1)}, bf16[16,128,128]{2,1,0:T(8,128)(2,1)S(1)}, f32[2,16,32,128]{3,2,1,0:T(8,128)S(1)}, bf16[2,16,32,128]{3,2,1,0:T(8,128)(2,1)S(1)}) custom-call(s32[1]{0:T(128)} %bitcast.core_ref, bf16[192,4096]{1,0:T(8,128)(2,1)S(1)} %copy-done.2, ...), custom_call_target="tpu_custom_call" | custom-call | flops 201326592 | bytes 6561792 | tf_op jit(solution)/shard_map/pallas_call | solution.py:241
  40.6 0.1 fusion.12
  40.7 0.1 add_convert_fusion.3
  40.9 0.6 collective-permute-start.5
  41.5 0.7 collective-permute-done.18
  42.2 0.1 convert_add_fusion
  42.3 1.0 %collective-permute-start.19 = (bf16[16,32,128]{2,1,0:T(8,128)(2,1)S(1)}, bf16[16,32,128]{2,1,0:T(8,128)(2,1)S(1)}, u32[]{:S(2)}, u32[]{:S(2)}) collective-permute-start(bf16[16,32,128]{2,1,0:T(8,128)(2,1)S(1)} %fusion.43), channel_id=1, source_target_pairs={{0,2},{1,3},{2,0},{3,1},{4,6},{5,7},{6,4},{7,5},{8,10},{9,11},{10,... | collective-permute-start | bytes 393224 | tf_op jit(solution)/shard_map/ppermute | solution.py:207
  43.3 2.9 %shard_map.107 = (bf16[192,4096]{1,0:T(8,128)(2,1)}, f32[192,2048]{1,0:T(8,128)S(1)}, f32[192,2048]{1,0:T(8,128)S(1)}) custom-call(bf16[192,4096]{1,0:T(8,128)(2,1)S(1)} %copy-done.2, bf16[192,4096]{1,0:T(8,128)(2,1)S(1)} %copy-done, bf16[192,4096]{1,0:T(8,128)(2,1)S(1)} %copy-done.1, bf16[192,2048]{1,0:T(8,128)(2,1)S(1)} %get-tuple-element.61.gm_ref, ...), custom_call_target="tpu_custom_call" | custom-call | flops 704643072 | bytes 8781824 | tf_op jit(solution)/shard_map/pallas_call | solution.py:241
  46.1 2.6 %shard_map.106 = (bf16[192,4096]{1,0:T(8,128)(2,1)}, bf16[192,2048]{1,0:T(8,128)(2,1)S(1)}, bf16[16,128,128]{2,1,0:T(8,128)(2,1)S(1)}, f32[2,16,32,128]{3,2,1,0:T(8,128)S(1)}, bf16[2,16,32,128]{3,2,1,0:T(8,128)(2,1)S(1)}) custom-call(s32[1]{0:T(128)} %bitcast.core_ref, bf16[192,4096]{1,0:T(8,128)(2,1)S(1)} %copy-done.2, ...), custom_call_target="tpu_custom_call", output_to_operand_aliasing={{0}: (7, {})} | custom-call | flops 201326592 | bytes 6561792 | tf_op jit(solution)/shard_map/pallas_call | solution.py:241
  48.8 2.9 %shard_map.108 = (bf16[192,4096]{1,0:T(8,128)(2,1)}, f32[192,2048]{1,0:T(8,128)S(1)}, f32[192,2048]{1,0:T(8,128)S(1)}) custom-call(bf16[192,4096]{1,0:T(8,128)(2,1)S(1)} %copy-done.2, bf16[192,4096]{1,0:T(8,128)(2,1)S(1)} %copy-done, bf16[192,4096]{1,0:T(8,128)(2,1)S(1)} %copy-done.1, ...), custom_call_target="tpu_custom_call", output_to_operand_aliasing={{0}: (6, {})} | custom-call | flops 704643072 | bytes 8781824 | tf_op jit(solution)/shard_map/pallas_call | solution.py:241
  51.7 0.1 collective-permute-start.20
  51.8 0.3 convert_add_fusion.1
  52.1 1.2 %collective-permute-start.13 = (bf16[16,32,128]{2,1,0:T(8,128)(2,1)S(1)}, bf16[16,32,128]{2,1,0:T(8,128)(2,1)S(1)}, u32[]{:S(2)}, u32[]{:S(2)}) collective-permute-start(bf16[16,32,128]{2,1,0:T(8,128)(2,1)S(1)} %fusion.42), channel_id=1, source_target_pairs={{0,2},{1,3},{2,0},{3,1},{4,6},{5,7},{6,4},{7,5},{8,10},{9,11},{10,... | collective-permute-start | bytes 393224 | tf_op jit(solution)/shard_map/ppermute | solution.py:207
  53.3 4.4 %collective-permute-done.20 = bf16[16,32,128]{2,1,0:T(8,128)(2,1)S(1)} collective-permute-done((bf16[16,32,128]{2,1,0:T(8,128)(2,1)S(1)}, bf16[16,32,128]{2,1,0:T(8,128)(2,1)S(1)}, u32[]{:S(2)}, u32[]{:S(2)}) %collective-permute-start.20) | collective-permute-done | bytes 131104 | tf_op jit(solution)/shard_map/ppermute | solution.py:207
  57.7 1.4 %collective-permute-start.21 = (bf16[16,32,128]{2,1,0:T(8,128)(2,1)S(1)}, bf16[16,32,128]{2,1,0:T(8,128)(2,1)S(1)}, u32[]{:S(2)}, u32[]{:S(2)}) collective-permute-start(bf16[16,32,128]{2,1,0:T(8,128)(2,1)S(1)} %get-tuple-element.79), channel_id=1, source_target_pairs={{0,8},{1,9},{2,10},{3,11},{4,12},{5,13},{6,14},{7,15},{8,0},{9,1},... | collective-permute-start | bytes 393224 | tf_op jit(solution)/shard_map/ppermute | solution.py:207
  59.1 0.1 fusion.38
  59.2 1.8 %collective-permute-start.14 = (bf16[16,32,128]{2,1,0:T(8,128)(2,1)S(1)}, bf16[16,32,128]{2,1,0:T(8,128)(2,1)S(1)}, u32[]{:S(2)}, u32[]{:S(2)}) collective-permute-start(bf16[16,32,128]{2,1,0:T(8,128)(2,1)S(1)} %get-tuple-element.85), channel_id=1, source_target_pairs={{0,4},{1,5},{2,6},{3,7},{4,0},{5,1},{6,2},{7,3},{8,12},{9,13},{10,... | collective-permute-start | bytes 393224 | tf_op jit(solution)/shard_map/ppermute | solution.py:207
  61.0 5.7 %collective-permute-done.21 = bf16[16,32,128]{2,1,0:T(8,128)(2,1)S(1)} collective-permute-done((bf16[16,32,128]{2,1,0:T(8,128)(2,1)S(1)}, bf16[16,32,128]{2,1,0:T(8,128)(2,1)S(1)}, u32[]{:S(2)}, u32[]{:S(2)}) %collective-permute-start.21) | collective-permute-done | bytes 131104 | tf_op jit(solution)/shard_map/ppermute | solution.py:207
  66.7 0.1 fusion.29
  66.7 1.1 %collective-permute-start.22 = (bf16[16,32,128]{2,1,0:T(8,128)(2,1)S(1)}, bf16[16,32,128]{2,1,0:T(8,128)(2,1)S(1)}, u32[]{:S(2)}, u32[]{:S(2)}) collective-permute-start(bf16[16,32,128]{2,1,0:T(8,128)(2,1)S(1)} %fusion.29), channel_id=1, source_target_pairs={{0,2},{1,3},{2,0},{3,1},{4,6},{5,7},{6,4},{7,5},{8,10},{9,11},{10,... | collective-permute-start | bytes 393224 | tf_op jit(solution)/shard_map/ppermute | solution.py:207
  67.9 0.1 collective-permute-start.15
  68.0 4.2 %collective-permute-done.22 = bf16[16,32,128]{2,1,0:T(8,128)(2,1)S(1)} collective-permute-done((bf16[16,32,128]{2,1,0:T(8,128)(2,1)S(1)}, bf16[16,32,128]{2,1,0:T(8,128)(2,1)S(1)}, u32[]{:S(2)}, u32[]{:S(2)}) %collective-permute-start.22) | collective-permute-done | bytes 131104 | tf_op jit(solution)/shard_map/ppermute | solution.py:207
  72.2 0.1 fusion.26
  72.3 3.8 %collective-permute-done.15 = bf16[16,32,128]{2,1,0:T(8,128)(2,1)S(1)} collective-permute-done((bf16[16,32,128]{2,1,0:T(8,128)(2,1)S(1)}, bf16[16,32,128]{2,1,0:T(8,128)(2,1)S(1)}, u32[]{:S(2)}, u32[]{:S(2)}) %collective-permute-start.15) | collective-permute-done | bytes 131104 | tf_op jit(solution)/shard_map/ppermute | solution.py:207
  76.0 0.1 fusion.31
  76.1 1.6 %collective-permute-start.16 = (bf16[16,32,128]{2,1,0:T(8,128)(2,1)S(1)}, bf16[16,32,128]{2,1,0:T(8,128)(2,1)S(1)}, u32[]{:S(2)}, u32[]{:S(2)}) collective-permute-start(bf16[16,32,128]{2,1,0:T(8,128)(2,1)S(1)} %fusion.31), channel_id=1, source_target_pairs={{0,2},{1,3},{2,0},{3,1},{4,6},{5,7},{6,4},{7,5},{8,10},{9,11},{10,... | collective-permute-start | bytes 393224 | tf_op jit(solution)/shard_map/ppermute | solution.py:207
  77.7 0.1 add_convert_fusion
  77.9 0.1 collective-permute-start.23
  77.9 3.7 %collective-permute-done.16 = bf16[16,32,128]{2,1,0:T(8,128)(2,1)S(1)} collective-permute-done((bf16[16,32,128]{2,1,0:T(8,128)(2,1)S(1)}, bf16[16,32,128]{2,1,0:T(8,128)(2,1)S(1)}, u32[]{:S(2)}, u32[]{:S(2)}) %collective-permute-start.16) | collective-permute-done | bytes 131104 | tf_op jit(solution)/shard_map/ppermute | solution.py:207
  81.6 0.1 fusion.22
  81.7 0.1 add_convert_fusion.1
  81.8 0.1 collective-permute-start.17
  82.0 0.7 pad_maximum_fusion.8
  82.7 1.7 %shard_map.109 = (bf16[192,4096]{1,0:T(8,128)(2,1)}, bf16[192,4096]{1,0:T(8,128)(2,1)}) custom-call(s32[1]{0:T(128)} %bitcast.core_ref, bf16[192,4096]{1,0:T(8,128)(2,1)S(1)} %copy-done, bf16[192,4096]{1,0:T(8,128)(2,1)S(1)} %copy-done.1, f32[192,2048]{1,0:T(8,128)S(1)} %get-tuple-element.70.kpart_ref, f32[192,2048]{1,0:T(8,128)S(1)} %get-tuple-element.71.vpart_ref, ...), custom_call_target="tpu_custom_call" | custom-call | flops 201326592 | bytes 6815744 | tf_op jit(solution)/shard_map/pallas_call | solution.py:241
  84.4 1.7 %shard_map.110 = (bf16[192,4096]{1,0:T(8,128)(2,1)}, bf16[192,4096]{1,0:T(8,128)(2,1)}) custom-call(s32[1]{0:T(128)} %bitcast.core_ref, bf16[192,4096]{1,0:T(8,128)(2,1)S(1)} %copy-done, bf16[192,4096]{1,0:T(8,128)(2,1)S(1)} %copy-done.1, f32[192,2048]{1,0:T(8,128)S(1)} %get-tuple-element.66.kpart_ref, ...), custom_call_target="tpu_custom_call", output_to_operand_aliasing={{0}: (7, {}), {1}: (8, {})} | custom-call | flops 201326592 | bytes 6815744 | tf_op jit(solution)/shard_map/pallas_call | solution.py:241
  (47 shorter events, 0.7 us)
Async XLA Ops:
  0.6 2.7 %copy-start = (bf16[192,4096]{1,0:T(8,128)(2,1)S(1)}, bf16[192,4096]{1,0:T(8,128)(2,1)}, u32[]{:S(2)}) copy-start(bf16[192,4096]{1,0:T(8,128)(2,1)} %k_ref.7) | copy-start | bytes 4718596
  0.7 2.6 %copy-start.1 = (bf16[192,4096]{1,0:T(8,128)(2,1)S(1)}, bf16[192,4096]{1,0:T(8,128)(2,1)}, u32[]{:S(2)}) copy-start(bf16[192,4096]{1,0:T(8,128)(2,1)} %v_ref.7) | copy-start | bytes 4718596
  2.7 1.8 %copy-start.5 = (f32[32,8,128]{2,1,0:T(8,128)S(1)}, f32[32,8,128]{2,1,0:T(8,128)}, u32[]{:S(2)}) copy-start(f32[32,8,128]{2,1,0:T(8,128)} %param.9) | copy-start | bytes 393220
  2.7 1.8 %collective-permute-start.6 = (bf16[2,16,32,128]{3,2,1,0:T(8,128)(2,1)S(1)}, bf16[2,16,32,128]{3,2,1,0:T(8,128)(2,1)S(1)}, u32[]{:S(2)}, u32[]{:S(2)}) collective-permute-start(bf16[2,16,32,128]{3,2,1,0:T(8,128)(2,1)S(1)} %get-tuple-element.55), channel_id=1, source_target_pairs={{0,1},{1,0},{2,3},{3,2},{4,5},{5,4},{6,7},{7,6},{8,9},{9,8},{10,11... | collective-permute-start | bytes 786440 | tf_op jit(solution)/shard_map/ppermute | solution.py:207
  4.2 3.3 %collective-permute-start = (bf16[2,16,32,128]{3,2,1,0:T(8,128)(2,1)S(1)}, bf16[2,16,32,128]{3,2,1,0:T(8,128)(2,1)S(1)}, u32[]{:S(2)}, u32[]{:S(2)}) collective-permute-start(bf16[2,16,32,128]{3,2,1,0:T(8,128)(2,1)S(1)} %get-tuple-element.49), channel_id=1, source_target_pairs={{0,1},{1,0},{2,3},{3,2},{4,5},{5,4},{6,7},{7,6},{8,9},{9,8},{10,11... | collective-permute-start | bytes 786440 | tf_op jit(solution)/shard_map/ppermute | solution.py:207
  4.6 6.7 %collective-permute-start.7 = (bf16[16,32,128]{2,1,0:T(8,128)(2,1)S(1)}, bf16[16,32,128]{2,1,0:T(8,128)(2,1)S(1)}, u32[]{:S(2)}, u32[]{:S(2)}) collective-permute-start(bf16[16,32,128]{2,1,0:T(8,128)(2,1)S(1)} %fusion.41), channel_id=1, source_target_pairs={{0,2},{1,3},{2,0},{3,1},{4,6},{5,7},{6,4},{7,5},{8,10},{9,11},{10,... | collective-permute-start | bytes 393224 | tf_op jit(solution)/shard_map/ppermute | solution.py:207
  11.5 5.8 %collective-permute-start.8 = (bf16[16,40,128]{2,1,0:T(8,128)(2,1)S(1)}, bf16[16,40,128]{2,1,0:T(8,128)(2,1)S(1)}, u32[]{:S(2)}, u32[]{:S(2)}) collective-permute-start(bf16[16,40,128]{2,1,0:T(8,128)(2,1)S(1)} %pad_maximum_fusion.5), channel_id=1, source_target_pairs={{0,4},{1,5},{2,6},{3,7},{4,0},{5,1},{6,2},{7,3},{8,12},{9,13},{10,... | collective-permute-start | bytes 491528 | tf_op jit(solution)/shard_map/ppermute | solution.py:207
  13.3 6.6 %collective-permute-start.1 = (bf16[16,32,128]{2,1,0:T(8,128)(2,1)S(1)}, bf16[16,32,128]{2,1,0:T(8,128)(2,1)S(1)}, u32[]{:S(2)}, u32[]{:S(2)}) collective-permute-start(bf16[16,32,128]{2,1,0:T(8,128)(2,1)S(1)} %fusion.40), channel_id=1, source_target_pairs={{0,2},{1,3},{2,0},{3,1},{4,6},{5,7},{6,4},{7,5},{8,10},{9,11},{10,... | collective-permute-start | bytes 393224 | tf_op jit(solution)/shard_map/ppermute | solution.py:207
  17.4 8.1 %collective-permute-start.9 = (bf16[16,32,128]{2,1,0:T(8,128)(2,1)S(1)}, bf16[16,32,128]{2,1,0:T(8,128)(2,1)S(1)}, u32[]{:S(2)}, u32[]{:S(2)}) collective-permute-start(bf16[16,32,128]{2,1,0:T(8,128)(2,1)S(1)} %fusion.17), channel_id=1, source_target_pairs={{0,8},{1,9},{2,10},{3,11},{4,12},{5,13},{6,14},{7,15},{8,0},{9,1},... | collective-permute-start | bytes 393224 | tf_op jit(solution)/shard_map/ppermute | solution.py:207
  20.1 6.7 %collective-permute-start.2 = (bf16[16,40,128]{2,1,0:T(8,128)(2,1)S(1)}, bf16[16,40,128]{2,1,0:T(8,128)(2,1)S(1)}, u32[]{:S(2)}, u32[]{:S(2)}) collective-permute-start(bf16[16,40,128]{2,1,0:T(8,128)(2,1)S(1)} %pad_maximum_fusion.4), channel_id=1, source_target_pairs={{0,4},{1,5},{2,6},{3,7},{4,0},{5,1},{6,2},{7,3},{8,12},{9,13},{10,... | collective-permute-start | bytes 491528 | tf_op jit(solution)/shard_map/ppermute | solution.py:207
  25.5 5.0 %collective-permute-start.10 = (bf16[16,32,128]{2,1,0:T(8,128)(2,1)S(1)}, bf16[16,32,128]{2,1,0:T(8,128)(2,1)S(1)}, u32[]{:S(2)}, u32[]{:S(2)}) collective-permute-start(bf16[16,32,128]{2,1,0:T(8,128)(2,1)S(1)} %fusion.33), channel_id=1, source_target_pairs={{0,2},{1,3},{2,0},{3,1},{4,6},{5,7},{6,4},{7,5},{8,10},{9,11},{10,... | collective-permute-start | bytes 393224 | tf_op jit(solution)/shard_map/ppermute | solution.py:207
  26.9 7.3 %collective-permute-start.3 = (bf16[16,32,128]{2,1,0:T(8,128)(2,1)S(1)}, bf16[16,32,128]{2,1,0:T(8,128)(2,1)S(1)}, u32[]{:S(2)}, u32[]{:S(2)}) collective-permute-start(bf16[16,32,128]{2,1,0:T(8,128)(2,1)S(1)} %fusion.11), channel_id=1, source_target_pairs={{0,8},{1,9},{2,10},{3,11},{4,12},{5,13},{6,14},{7,15},{8,0},{9,1},... | collective-permute-start | bytes 393224 | tf_op jit(solution)/shard_map/ppermute | solution.py:207
  30.7 4.8 %copy-start.2 = (bf16[192,4096]{1,0:T(8,128)(2,1)S(1)}, bf16[192,4096]{1,0:T(8,128)(2,1)}, u32[]{:S(2)}) copy-start(bf16[192,4096]{1,0:T(8,128)(2,1)} %q_ref.11) | copy-start | bytes 4718596
  30.8 6.8 %collective-permute-start.11 = (bf16[2,16,32,128]{3,2,1,0:T(8,128)(2,1)S(1)}, bf16[2,16,32,128]{3,2,1,0:T(8,128)(2,1)S(1)}, u32[]{:S(2)}, u32[]{:S(2)}) collective-permute-start(bf16[2,16,32,128]{3,2,1,0:T(8,128)(2,1)S(1)} %get-tuple-element.103), channel_id=1, source_target_pairs={{0,1},{1,0},{2,3},{3,2},{4,5},{5,4},{6,7},{7,6},{8,9},{9,8},{10,11... | collective-permute-start | bytes 786440 | tf_op jit(solution)/shard_map/ppermute | solution.py:207
  34.3 6.3 %collective-permute-start.4 = (bf16[16,32,128]{2,1,0:T(8,128)(2,1)S(1)}, bf16[16,32,128]{2,1,0:T(8,128)(2,1)S(1)}, u32[]{:S(2)}, u32[]{:S(2)}) collective-permute-start(bf16[16,32,128]{2,1,0:T(8,128)(2,1)S(1)} %fusion.35), channel_id=1, source_target_pairs={{0,2},{1,3},{2,0},{3,1},{4,6},{5,7},{6,4},{7,5},{8,10},{9,11},{10,... | collective-permute-start | bytes 393224 | tf_op jit(solution)/shard_map/ppermute | solution.py:207
  36.5 1.4 %copy-start.3 = (bf16[192,4096]{1,0:T(8,128)(2,1)S(1)}, bf16[192,4096]{1,0:T(8,128)(2,1)}, u32[]{:S(2)}) copy-start(bf16[192,4096]{1,0:T(8,128)(2,1)} %do_ref.3) | copy-start | bytes 4718596
  36.5 1.4 %copy-start.4 = (f32[4096]{0:T(1024)S(1)}, f32[4096]{0:T(1024)}, u32[]{:S(2)}) copy-start(f32[4096]{0:T(1024)} %param.10) | copy-start | bytes 49156
  40.6 1.5 %collective-permute-start.18 = (bf16[2,16,32,128]{3,2,1,0:T(8,128)(2,1)S(1)}, bf16[2,16,32,128]{3,2,1,0:T(8,128)(2,1)S(1)}, u32[]{:S(2)}, u32[]{:S(2)}) collective-permute-start(bf16[2,16,32,128]{3,2,1,0:T(8,128)(2,1)S(1)} %get-tuple-element.73), channel_id=1, source_target_pairs={{0,1},{1,0},{2,3},{3,2},{4,5},{5,4},{6,7},{7,6},{8,9},{9,8},{10,11... | collective-permute-start | bytes 786440 | tf_op jit(solution)/shard_map/ppermute | solution.py:207
  40.9 5.3 %collective-permute-start.5 = (bf16[2,16,32,128]{3,2,1,0:T(8,128)(2,1)S(1)}, bf16[2,16,32,128]{3,2,1,0:T(8,128)(2,1)S(1)}, u32[]{:S(2)}, u32[]{:S(2)}) collective-permute-start(bf16[2,16,32,128]{3,2,1,0:T(8,128)(2,1)S(1)} %get-tuple-element.105), channel_id=1, source_target_pairs={{0,1},{1,0},{2,3},{3,2},{4,5},{5,4},{6,7},{7,6},{8,9},{9,8},{10,11... | collective-permute-start | bytes 786440 | tf_op jit(solution)/shard_map/ppermute | solution.py:207
  42.3 9.4 %collective-permute-start.19 = (bf16[16,32,128]{2,1,0:T(8,128)(2,1)S(1)}, bf16[16,32,128]{2,1,0:T(8,128)(2,1)S(1)}, u32[]{:S(2)}, u32[]{:S(2)}) collective-permute-start(bf16[16,32,128]{2,1,0:T(8,128)(2,1)S(1)} %fusion.43), channel_id=1, source_target_pairs={{0,2},{1,3},{2,0},{3,1},{4,6},{5,7},{6,4},{7,5},{8,10},{9,11},{10,... | collective-permute-start | bytes 393224 | tf_op jit(solution)/shard_map/ppermute | solution.py:207
  48.8 3.0 %collective-permute-start.12 = (bf16[2,16,32,128]{3,2,1,0:T(8,128)(2,1)S(1)}, bf16[2,16,32,128]{3,2,1,0:T(8,128)(2,1)S(1)}, u32[]{:S(2)}, u32[]{:S(2)}) collective-permute-start(bf16[2,16,32,128]{3,2,1,0:T(8,128)(2,1)S(1)} %get-tuple-element.69), channel_id=1, source_target_pairs={{0,1},{1,0},{2,3},{3,2},{4,5},{5,4},{6,7},{7,6},{8,9},{9,8},{10,11... | collective-permute-start | bytes 786440 | tf_op jit(solution)/shard_map/ppermute | solution.py:207
  51.7 6.0 %collective-permute-start.20 = (bf16[16,32,128]{2,1,0:T(8,128)(2,1)S(1)}, bf16[16,32,128]{2,1,0:T(8,128)(2,1)S(1)}, u32[]{:S(2)}, u32[]{:S(2)}) collective-permute-start(bf16[16,32,128]{2,1,0:T(8,128)(2,1)S(1)} %get-tuple-element.81), channel_id=1, source_target_pairs={{0,4},{1,5},{2,6},{3,7},{4,0},{5,1},{6,2},{7,3},{8,12},{9,13},{10,... | collective-permute-start | bytes 393224 | tf_op jit(solution)/shard_map/ppermute | solution.py:207
  52.1 7.0 %collective-permute-start.13 = (bf16[16,32,128]{2,1,0:T(8,128)(2,1)S(1)}, bf16[16,32,128]{2,1,0:T(8,128)(2,1)S(1)}, u32[]{:S(2)}, u32[]{:S(2)}) collective-permute-start(bf16[16,32,128]{2,1,0:T(8,128)(2,1)S(1)} %fusion.42), channel_id=1, source_target_pairs={{0,2},{1,3},{2,0},{3,1},{4,6},{5,7},{6,4},{7,5},{8,10},{9,11},{10,... | collective-permute-start | bytes 393224 | tf_op jit(solution)/shard_map/ppermute | solution.py:207
  57.7 8.9 %collective-permute-start.21 = (bf16[16,32,128]{2,1,0:T(8,128)(2,1)S(1)}, bf16[16,32,128]{2,1,0:T(8,128)(2,1)S(1)}, u32[]{:S(2)}, u32[]{:S(2)}) collective-permute-start(bf16[16,32,128]{2,1,0:T(8,128)(2,1)S(1)} %get-tuple-element.79), channel_id=1, source_target_pairs={{0,8},{1,9},{2,10},{3,11},{4,12},{5,13},{6,14},{7,15},{8,0},{9,1},... | collective-permute-start | bytes 393224 | tf_op jit(solution)/shard_map/ppermute | solution.py:207
  59.2 8.7 %collective-permute-start.14 = (bf16[16,32,128]{2,1,0:T(8,128)(2,1)S(1)}, bf16[16,32,128]{2,1,0:T(8,128)(2,1)S(1)}, u32[]{:S(2)}, u32[]{:S(2)}) collective-permute-start(bf16[16,32,128]{2,1,0:T(8,128)(2,1)S(1)} %get-tuple-element.85), channel_id=1, source_target_pairs={{0,4},{1,5},{2,6},{3,7},{4,0},{5,1},{6,2},{7,3},{8,12},{9,13},{10,... | collective-permute-start | bytes 393224 | tf_op jit(solution)/shard_map/ppermute | solution.py:207
  66.7 5.4 %collective-permute-start.22 = (bf16[16,32,128]{2,1,0:T(8,128)(2,1)S(1)}, bf16[16,32,128]{2,1,0:T(8,128)(2,1)S(1)}, u32[]{:S(2)}, u32[]{:S(2)}) collective-permute-start(bf16[16,32,128]{2,1,0:T(8,128)(2,1)S(1)} %fusion.29), channel_id=1, source_target_pairs={{0,2},{1,3},{2,0},{3,1},{4,6},{5,7},{6,4},{7,5},{8,10},{9,11},{10,... | collective-permute-start | bytes 393224 | tf_op jit(solution)/shard_map/ppermute | solution.py:207
  67.9 8.1 %collective-permute-start.15 = (bf16[16,32,128]{2,1,0:T(8,128)(2,1)S(1)}, bf16[16,32,128]{2,1,0:T(8,128)(2,1)S(1)}, u32[]{:S(2)}, u32[]{:S(2)}) collective-permute-start(bf16[16,32,128]{2,1,0:T(8,128)(2,1)S(1)} %get-tuple-element.83), channel_id=1, source_target_pairs={{0,8},{1,9},{2,10},{3,11},{4,12},{5,13},{6,14},{7,15},{8,0},{9,1},... | collective-permute-start | bytes 393224 | tf_op jit(solution)/shard_map/ppermute | solution.py:207
  76.1 5.5 %collective-permute-start.16 = (bf16[16,32,128]{2,1,0:T(8,128)(2,1)S(1)}, bf16[16,32,128]{2,1,0:T(8,128)(2,1)S(1)}, u32[]{:S(2)}, u32[]{:S(2)}) collective-permute-start(bf16[16,32,128]{2,1,0:T(8,128)(2,1)S(1)} %fusion.31), channel_id=1, source_target_pairs={{0,2},{1,3},{2,0},{3,1},{4,6},{5,7},{6,4},{7,5},{8,10},{9,11},{10,... | collective-permute-start | bytes 393224 | tf_op jit(solution)/shard_map/ppermute | solution.py:207
  77.9 4.8 %collective-permute-start.23 = (bf16[2,16,32,128]{3,2,1,0:T(8,128)(2,1)S(1)}, bf16[2,16,32,128]{3,2,1,0:T(8,128)(2,1)S(1)}, u32[]{:S(2)}, u32[]{:S(2)}) collective-permute-start(bf16[2,16,32,128]{3,2,1,0:T(8,128)(2,1)S(1)} %get-tuple-element.95), channel_id=1, source_target_pairs={{0,1},{1,0},{2,3},{3,2},{4,5},{5,4},{6,7},{7,6},{8,9},{9,8},{10,11... | collective-permute-start | bytes 786440 | tf_op jit(solution)/shard_map/ppermute | solution.py:207
  81.8 2.6 %collective-permute-start.17 = (bf16[2,16,32,128]{3,2,1,0:T(8,128)(2,1)S(1)}, bf16[2,16,32,128]{3,2,1,0:T(8,128)(2,1)S(1)}, u32[]{:S(2)}, u32[]{:S(2)}) collective-permute-start(bf16[2,16,32,128]{3,2,1,0:T(8,128)(2,1)S(1)} %get-tuple-element.99), channel_id=1, source_target_pairs={{0,1},{1,0},{2,3},{3,2},{4,5},{5,4},{6,7},{7,6},{8,9},{9,8},{10,11... | collective-permute-start | bytes 786440 | tf_op jit(solution)/shard_map/ppermute | solution.py:207

commit v4 on v3

--- a/solution.py
+++ b/solution.py
@@ -12,8 +12,8 @@
 BF16 = jnp.bfloat16
 F32 = jnp.float32
 CHUNK_EIGHTHS = (4, 4)
-BLOCKS = {"state": 8, "intra": 16, "mix": 16, "local": 16, "final": 16}
-LOCAL_SPLIT = 1
+BLOCKS = {"state": 8, "intra": 16, "mix": 16, "local": 8, "final": 16}
+LOCAL_SPLIT = 2
 VMEM_LIMIT = 20 * 1024 * 1024
 
 
@@ -137,12 +137,13 @@
     crosses = [dot(q_ref[:, at], prior_ref[h], NN) for h, at in enumerate(ats)]
     for at, cross in zip(ats, crosses):
         mixed = intra_ref[:, at] + cross
-        gain = gain_ref[:, at]
-        inv = lax.rsqrt(jnp.mean(mixed * mixed, axis=1, keepdims=True) + 1e-06)
-        att_ref[:, at] = (gain * mixed * inv).astype(BF16)
-        scaled = gain * do_ref[:, at].astype(F32)
-        along = jnp.mean(scaled * mixed, axis=1, keepdims=True)
-        gm_ref[:, at] = (inv * scaled - mixed * (inv * inv * inv * along)).astype(BF16)
+        gain = gain_ref[:, at] * math.sqrt(dim)
+        r = lax.rsqrt(jnp.sum(mixed * mixed, axis=1, keepdims=True) + dim * 1e-06)
+        gained = gain * mixed
+        att_ref[:, at] = (gained * r).astype(BF16)
+        do = do_ref[:, at].astype(F32)
+        along = jnp.sum(gained * do, axis=1, keepdims=True)
+        gm_ref[:, at] = (r * (gain * do - mixed * (r * r * along))).astype(BF16)
     grads = [dot(q_ref[:, at], gm_ref[:, at], TN) for at in ats]
     for h, grad in enumerate(grads):
         put_halves(core, grad, h, mine_ref, theirs_ref)
@@ -372,7 +373,8 @@
     heads, owned, dim = carried_state.shape
     power = n >= 4 and (n & (n - 1)) == 0
     fits = power and owned % 8 == 0 and owned == 8 and dim % 128 == 0
-    if fits and heads % 8 == 0 and queries.shape[0] % 16 == 0:
+    even = heads % (len(CHUNK_EIGHTHS) * max(BLOCKS.values())) == 0
+    if fits and even and queries.shape[0] % 16 == 0:
         return fused_on_device(n, queries, keys, values, carried_state, gain, out_grad)
     return plain_on_device(queries, keys, values, carried_state, gain, out_grad)
 

time: 86.3 us -> 86.7 us (level)
    pallas_call x10 -> x12, Pallas kernels: 19.5 us -> 19.7 us  [call(): pl.pallas_call(body, out_shape=[jax.ShapeDtypeStruct(shapes[kind], t) for...]
where the time goes in v4:
time: 86.7 us; the launch traced here: 86.5 us
  waiting for transfers between devices  37.8 us (44%)
  starting transfers between devices  24.4 us (28%)
  Pallas kernels  19.7 us (23%)
  other arithmetic  3.27 us (4%)
  between operations  1.03 us (1%)
    ppermute x24, waiting for transfers between devices, swap(): return lax.ppermute(x, 'ctx', [(i, i ^ bit) for i in range(n)])  37.8 us
    ppermute x24, starting transfers between devices, swap(): return lax.ppermute(x, 'ctx', [(i, i ^ bit) for i in range(n)])  24.4 us
    pallas_call x12, Pallas kernels, call(): pl.pallas_call(body, out_shape=[jax.ShapeDtypeStruct(shapes[kind], t) for...  19.7 us
  transfers between devices with their start and end apart: 24, of which 11 were waited for; matrix products, arithmetic and copies ran while one was open for 4% of the time, Pallas kernels for 18%

profile of v4, /device:TPU:0, one launch (start us, length us, event | category | flops | bytes accessed | tf_op | source)
XLA Modules:
  0.0 86.5 jit_solution(12476091372139964477)
XLA Ops:
  0.7 2.1 %shard_map.104 = (f32[2,16,32,128]{3,2,1,0:T(8,128)S(1)}, bf16[2,16,32,128]{3,2,1,0:T(8,128)(2,1)S(1)}) custom-call(s32[1]{0:T(128)} %bitcast.core_ref, bf16[192,4096]{1,0:T(8,128)(2,1)} %k_ref.9, bf16[192,4096]{1,0:T(8,128)(2,1)} %v_ref.9), custom_call_target="tpu_custom_call" | custom-call | flops 100663296 | bytes 2359296 | tf_op jit(solution)/shard_map/pallas_call | solution.py:242
  2.7 0.6 collective-permute-start.6
  3.3 0.9 %shard_map.102 = (f32[2,16,32,128]{3,2,1,0:T(8,128)S(1)}, bf16[2,16,32,128]{3,2,1,0:T(8,128)(2,1)S(1)}) custom-call(s32[1]{0:T(128)} %bitcast.core_ref, bf16[192,4096]{1,0:T(8,128)(2,1)S(1)} %copy-done, bf16[192,4096]{1,0:T(8,128)(2,1)S(1)} %copy-done.1), custom_call_target="tpu_custom_call" | custom-call | flops 100663296 | bytes 2359296 | tf_op jit(solution)/shard_map/pallas_call | solution.py:242
  4.2 0.3 collective-permute-start
  4.6 2.9 %collective-permute-start.7 = (bf16[16,32,128]{2,1,0:T(8,128)(2,1)S(1)}, bf16[16,32,128]{2,1,0:T(8,128)(2,1)S(1)}, u32[]{:S(2)}, u32[]{:S(2)}) collective-permute-start(bf16[16,32,128]{2,1,0:T(8,128)(2,1)S(1)} %fusion.41), channel_id=1, source_target_pairs={{0,2},{1,3},{2,0},{3,1},{4,6},{5,7},{6,4},{7,5},{8,10},{9,11},{10,... | collective-permute-start | bytes 393224 | tf_op jit(solution)/shard_map/ppermute | solution.py:208
  7.5 0.1 convert_add_fusion.3
  7.6 3.8 %collective-permute-done.7 = bf16[16,32,128]{2,1,0:T(8,128)(2,1)S(1)} collective-permute-done((bf16[16,32,128]{2,1,0:T(8,128)(2,1)S(1)}, bf16[16,32,128]{2,1,0:T(8,128)(2,1)S(1)}, u32[]{:S(2)}, u32[]{:S(2)}) %collective-permute-start.7) | collective-permute-done | bytes 131104 | tf_op jit(solution)/shard_map/ppermute | solution.py:208
  11.5 1.9 %collective-permute-start.8 = (bf16[16,40,128]{2,1,0:T(8,128)(2,1)S(1)}, bf16[16,40,128]{2,1,0:T(8,128)(2,1)S(1)}, u32[]{:S(2)}, u32[]{:S(2)}) collective-permute-start(bf16[16,40,128]{2,1,0:T(8,128)(2,1)S(1)} %pad_maximum_fusion.5), channel_id=1, source_target_pairs={{0,4},{1,5},{2,6},{3,7},{4,0},{5,1},{6,2},{7,3},{8,12},{9,13},{10,... | collective-permute-start | bytes 491528 | tf_op jit(solution)/shard_map/ppermute | solution.py:208
  13.3 1.6 %collective-permute-start.1 = (bf16[16,32,128]{2,1,0:T(8,128)(2,1)S(1)}, bf16[16,32,128]{2,1,0:T(8,128)(2,1)S(1)}, u32[]{:S(2)}, u32[]{:S(2)}) collective-permute-start(bf16[16,32,128]{2,1,0:T(8,128)(2,1)S(1)} %fusion.40), channel_id=1, source_target_pairs={{0,2},{1,3},{2,0},{3,1},{4,6},{5,7},{6,4},{7,5},{8,10},{9,11},{10,... | collective-permute-start | bytes 393224 | tf_op jit(solution)/shard_map/ppermute | solution.py:208
  14.9 2.3 %collective-permute-done.8 = bf16[16,40,128]{2,1,0:T(8,128)(2,1)S(1)} collective-permute-done((bf16[16,40,128]{2,1,0:T(8,128)(2,1)S(1)}, bf16[16,40,128]{2,1,0:T(8,128)(2,1)S(1)}, u32[]{:S(2)}, u32[]{:S(2)}) %collective-permute-start.8) | collective-permute-done | bytes 163872 | tf_op jit(solution)/shard_map/ppermute | solution.py:208
  17.3 0.1 fusion.17
  17.4 2.6 %collective-permute-start.9 = (bf16[16,32,128]{2,1,0:T(8,128)(2,1)S(1)}, bf16[16,32,128]{2,1,0:T(8,128)(2,1)S(1)}, u32[]{:S(2)}, u32[]{:S(2)}) collective-permute-start(bf16[16,32,128]{2,1,0:T(8,128)(2,1)S(1)} %fusion.17), channel_id=1, source_target_pairs={{0,8},{1,9},{2,10},{3,11},{4,12},{5,13},{6,14},{7,15},{8,0},{9,1},... | collective-permute-start | bytes 393224 | tf_op jit(solution)/shard_map/ppermute | solution.py:208
  20.1 1.6 %collective-permute-start.2 = (bf16[16,40,128]{2,1,0:T(8,128)(2,1)S(1)}, bf16[16,40,128]{2,1,0:T(8,128)(2,1)S(1)}, u32[]{:S(2)}, u32[]{:S(2)}) collective-permute-start(bf16[16,40,128]{2,1,0:T(8,128)(2,1)S(1)} %pad_maximum_fusion.4), channel_id=1, source_target_pairs={{0,4},{1,5},{2,6},{3,7},{4,0},{5,1},{6,2},{7,3},{8,12},{9,13},{10,... | collective-permute-start | bytes 491528 | tf_op jit(solution)/shard_map/ppermute | solution.py:208
  21.7 3.7 %collective-permute-done.9 = bf16[16,32,128]{2,1,0:T(8,128)(2,1)S(1)} collective-permute-done((bf16[16,32,128]{2,1,0:T(8,128)(2,1)S(1)}, bf16[16,32,128]{2,1,0:T(8,128)(2,1)S(1)}, u32[]{:S(2)}, u32[]{:S(2)}) %collective-permute-start.9) | collective-permute-done | bytes 131104 | tf_op jit(solution)/shard_map/ppermute | solution.py:208
  25.4 0.1 fusion.33
  25.5 1.2 %collective-permute-start.10 = (bf16[16,32,128]{2,1,0:T(8,128)(2,1)S(1)}, bf16[16,32,128]{2,1,0:T(8,128)(2,1)S(1)}, u32[]{:S(2)}, u32[]{:S(2)}) collective-permute-start(bf16[16,32,128]{2,1,0:T(8,128)(2,1)S(1)} %fusion.33), channel_id=1, source_target_pairs={{0,2},{1,3},{2,0},{3,1},{4,6},{5,7},{6,4},{7,5},{8,10},{9,11},{10,... | collective-permute-start | bytes 393224 | tf_op jit(solution)/shard_map/ppermute | solution.py:208
  26.8 0.1 fusion.11
  26.9 1.6 %collective-permute-start.3 = (bf16[16,32,128]{2,1,0:T(8,128)(2,1)S(1)}, bf16[16,32,128]{2,1,0:T(8,128)(2,1)S(1)}, u32[]{:S(2)}, u32[]{:S(2)}) collective-permute-start(bf16[16,32,128]{2,1,0:T(8,128)(2,1)S(1)} %fusion.11), channel_id=1, source_target_pairs={{0,8},{1,9},{2,10},{3,11},{4,12},{5,13},{6,14},{7,15},{8,0},{9,1},... | collective-permute-start | bytes 393224 | tf_op jit(solution)/shard_map/ppermute | solution.py:208
  28.5 2.0 %collective-permute-done.10 = bf16[16,32,128]{2,1,0:T(8,128)(2,1)S(1)} collective-permute-done((bf16[16,32,128]{2,1,0:T(8,128)(2,1)S(1)}, bf16[16,32,128]{2,1,0:T(8,128)(2,1)S(1)}, u32[]{:S(2)}, u32[]{:S(2)}) %collective-permute-start.10) | collective-permute-done | bytes 131104 | tf_op jit(solution)/shard_map/ppermute | solution.py:208
  30.6 0.1 fusion.18
  30.7 0.1 add_convert_fusion.2
  30.8 0.1 collective-permute-start.11
  30.9 3.3 %collective-permute-done.3 = bf16[16,32,128]{2,1,0:T(8,128)(2,1)S(1)} collective-permute-done((bf16[16,32,128]{2,1,0:T(8,128)(2,1)S(1)}, bf16[16,32,128]{2,1,0:T(8,128)(2,1)S(1)}, u32[]{:S(2)}, u32[]{:S(2)}) %collective-permute-start.3) | collective-permute-done | bytes 131104 | tf_op jit(solution)/shard_map/ppermute | solution.py:208
  34.2 0.1 fusion.35
  34.3 1.2 %collective-permute-start.4 = (bf16[16,32,128]{2,1,0:T(8,128)(2,1)S(1)}, bf16[16,32,128]{2,1,0:T(8,128)(2,1)S(1)}, u32[]{:S(2)}, u32[]{:S(2)}) collective-permute-start(bf16[16,32,128]{2,1,0:T(8,128)(2,1)S(1)} %fusion.35), channel_id=1, source_target_pairs={{0,2},{1,3},{2,0},{3,1},{4,6},{5,7},{6,4},{7,5},{8,10},{9,11},{10,... | collective-permute-start | bytes 393224 | tf_op jit(solution)/shard_map/ppermute | solution.py:208
  35.5 1.0 %shard_map.103 = (bf16[16,192,192]{2,1,0:T(8,128)(2,1)S(1)}, f32[192,2048]{1,0:T(8,128)S(1)}) custom-call(bf16[192,4096]{1,0:T(8,128)(2,1)S(1)} %copy-done.2, bf16[192,4096]{1,0:T(8,128)(2,1)S(1)} %copy-done, bf16[192,4096]{1,0:T(8,128)(2,1)S(1)} %copy-done.1), custom_call_target="tpu_custom_call" | custom-call | flops 301989888 | bytes 5111808 | tf_op jit(solution)/shard_map/pallas_call | solution.py:242
  36.6 1.0 %shard_map.101 = (bf16[16,192,192]{2,1,0:T(8,128)(2,1)S(1)}, f32[192,2048]{1,0:T(8,128)S(1)}) custom-call(bf16[192,4096]{1,0:T(8,128)(2,1)S(1)} %copy-done.2, bf16[192,4096]{1,0:T(8,128)(2,1)S(1)} %copy-done, bf16[192,4096]{1,0:T(8,128)(2,1)S(1)} %copy-done.1), custom_call_target="tpu_custom_call" | custom-call | flops 301989888 | bytes 5111808 | tf_op jit(solution)/shard_map/pallas_call | solution.py:242
  37.6 0.3 copy-done.3
  38.0 2.6 %shard_map.105 = (bf16[192,4096]{1,0:T(8,128)(2,1)}, bf16[192,2048]{1,0:T(8,128)(2,1)S(1)}, bf16[16,128,128]{2,1,0:T(8,128)(2,1)S(1)}, f32[2,16,32,128]{3,2,1,0:T(8,128)S(1)}, bf16[2,16,32,128]{3,2,1,0:T(8,128)(2,1)S(1)}) custom-call(s32[1]{0:T(128)} %bitcast.core_ref, bf16[192,4096]{1,0:T(8,128)(2,1)S(1)} %copy-done.2, ...), custom_call_target="tpu_custom_call" | custom-call | flops 201326592 | bytes 6561792 | tf_op jit(solution)/shard_map/pallas_call | solution.py:242
  40.6 0.1 fusion.12
  40.7 0.1 add_convert_fusion.3
  40.8 0.6 collective-permute-start.5
  41.4 0.7 collective-permute-done.18
  42.1 0.1 convert_add_fusion
  42.2 1.0 %collective-permute-start.19 = (bf16[16,32,128]{2,1,0:T(8,128)(2,1)S(1)}, bf16[16,32,128]{2,1,0:T(8,128)(2,1)S(1)}, u32[]{:S(2)}, u32[]{:S(2)}) collective-permute-start(bf16[16,32,128]{2,1,0:T(8,128)(2,1)S(1)} %fusion.43), channel_id=1, source_target_pairs={{0,2},{1,3},{2,0},{3,1},{4,6},{5,7},{6,4},{7,5},{8,10},{9,11},{10,... | collective-permute-start | bytes 393224 | tf_op jit(solution)/shard_map/ppermute | solution.py:208
  43.2 1.5 %shard_map.107 = (bf16[192,4096]{1,0:T(8,128)(2,1)}, f32[192,2048]{1,0:T(8,128)S(1)}, f32[192,2048]{1,0:T(8,128)S(1)}) custom-call(bf16[192,4096]{1,0:T(8,128)(2,1)S(1)} %copy-done.2, bf16[192,4096]{1,0:T(8,128)(2,1)S(1)} %copy-done, bf16[192,4096]{1,0:T(8,128)(2,1)S(1)} %copy-done.1, bf16[192,2048]{1,0:T(8,128)(2,1)S(1)} %get-tuple-element.67.gm_ref, ...), custom_call_target="tpu_custom_call" | custom-call | flops 352321536 | bytes 4390912 | tf_op jit(solution)/shard_map/pallas_call | solution.py:242
  44.7 1.5 %shard_map.108 = (bf16[192,4096]{1,0:T(8,128)(2,1)}, f32[192,2048]{1,0:T(8,128)S(1)}, f32[192,2048]{1,0:T(8,128)S(1)}) custom-call(bf16[192,4096]{1,0:T(8,128)(2,1)S(1)} %copy-done.2, bf16[192,4096]{1,0:T(8,128)(2,1)S(1)} %copy-done, bf16[192,4096]{1,0:T(8,128)(2,1)S(1)} %copy-done.1, ...), custom_call_target="tpu_custom_call", output_to_operand_aliasing={{0}: (6, {}), {1}: (7, {}), {2}: (8, {})} | custom-call | flops 352321536 | bytes 4390912 | tf_op jit(solution)/shard_map/pallas_call | solution.py:242
  46.2 2.6 %shard_map.106 = (bf16[192,4096]{1,0:T(8,128)(2,1)}, bf16[192,2048]{1,0:T(8,128)(2,1)S(1)}, bf16[16,128,128]{2,1,0:T(8,128)(2,1)S(1)}, f32[2,16,32,128]{3,2,1,0:T(8,128)S(1)}, bf16[2,16,32,128]{3,2,1,0:T(8,128)(2,1)S(1)}) custom-call(s32[1]{0:T(128)} %bitcast.core_ref, bf16[192,4096]{1,0:T(8,128)(2,1)S(1)} %copy-done.2, ...), custom_call_target="tpu_custom_call", output_to_operand_aliasing={{0}: (7, {})} | custom-call | flops 201326592 | bytes 6561792 | tf_op jit(solution)/shard_map/pallas_call | solution.py:242
  48.8 1.5 %shard_map.109 = (bf16[192,4096]{1,0:T(8,128)(2,1)}, f32[192,2048]{1,0:T(8,128)S(1)}, f32[192,2048]{1,0:T(8,128)S(1)}) custom-call(bf16[192,4096]{1,0:T(8,128)(2,1)S(1)} %copy-done.2, bf16[192,4096]{1,0:T(8,128)(2,1)S(1)} %copy-done, bf16[192,4096]{1,0:T(8,128)(2,1)S(1)} %copy-done.1, ...), custom_call_target="tpu_custom_call", output_to_operand_aliasing={{0}: (6, {})} | custom-call | flops 352321536 | bytes 4390912 | tf_op jit(solution)/shard_map/pallas_call | solution.py:242
  50.3 1.5 %shard_map.110 = (bf16[192,4096]{1,0:T(8,128)(2,1)}, f32[192,2048]{1,0:T(8,128)S(1)}, f32[192,2048]{1,0:T(8,128)S(1)}) custom-call(bf16[192,4096]{1,0:T(8,128)(2,1)S(1)} %copy-done.2, bf16[192,4096]{1,0:T(8,128)(2,1)S(1)} %copy-done, bf16[192,4096]{1,0:T(8,128)(2,1)S(1)} %copy-done.1, ...), custom_call_target="tpu_custom_call", output_to_operand_aliasing={{0}: (6, {}), {1}: (7, {}), {2}: (8, {})} | custom-call | flops 352321536 | bytes 4390912 | tf_op jit(solution)/shard_map/pallas_call | solution.py:242
  51.9 0.2 fusion.39
  52.1 0.1 collective-permute-start.20
  52.2 0.1 convert_add_fusion.1
  52.3 1.2 %collective-permute-start.13 = (bf16[16,32,128]{2,1,0:T(8,128)(2,1)S(1)}, bf16[16,32,128]{2,1,0:T(8,128)(2,1)S(1)}, u32[]{:S(2)}, u32[]{:S(2)}) collective-permute-start(bf16[16,32,128]{2,1,0:T(8,128)(2,1)S(1)} %fusion.42), channel_id=1, source_target_pairs={{0,2},{1,3},{2,0},{3,1},{4,6},{5,7},{6,4},{7,5},{8,10},{9,11},{10,... | collective-permute-start | bytes 393224 | tf_op jit(solution)/shard_map/ppermute | solution.py:208
  53.5 4.6 %collective-permute-done.20 = bf16[16,32,128]{2,1,0:T(8,128)(2,1)S(1)} collective-permute-done((bf16[16,32,128]{2,1,0:T(8,128)(2,1)S(1)}, bf16[16,32,128]{2,1,0:T(8,128)(2,1)S(1)}, u32[]{:S(2)}, u32[]{:S(2)}) %collective-permute-start.20) | collective-permute-done | bytes 131104 | tf_op jit(solution)/shard_map/ppermute | solution.py:208
  58.1 1.4 %collective-permute-start.21 = (bf16[16,32,128]{2,1,0:T(8,128)(2,1)S(1)}, bf16[16,32,128]{2,1,0:T(8,128)(2,1)S(1)}, u32[]{:S(2)}, u32[]{:S(2)}) collective-permute-start(bf16[16,32,128]{2,1,0:T(8,128)(2,1)S(1)} %get-tuple-element.91), channel_id=1, source_target_pairs={{0,8},{1,9},{2,10},{3,11},{4,12},{5,13},{6,14},{7,15},{8,0},{9,1},... | collective-permute-start | bytes 393224 | tf_op jit(solution)/shard_map/ppermute | solution.py:208
  59.6 1.8 %collective-permute-start.14 = (bf16[16,32,128]{2,1,0:T(8,128)(2,1)S(1)}, bf16[16,32,128]{2,1,0:T(8,128)(2,1)S(1)}, u32[]{:S(2)}, u32[]{:S(2)}) collective-permute-start(bf16[16,32,128]{2,1,0:T(8,128)(2,1)S(1)} %get-tuple-element.97), channel_id=1, source_target_pairs={{0,4},{1,5},{2,6},{3,7},{4,0},{5,1},{6,2},{7,3},{8,12},{9,13},{10,... | collective-permute-start | bytes 393224 | tf_op jit(solution)/shard_map/ppermute | solution.py:208
  61.4 5.7 %collective-permute-done.21 = bf16[16,32,128]{2,1,0:T(8,128)(2,1)S(1)} collective-permute-done((bf16[16,32,128]{2,1,0:T(8,128)(2,1)S(1)}, bf16[16,32,128]{2,1,0:T(8,128)(2,1)S(1)}, u32[]{:S(2)}, u32[]{:S(2)}) %collective-permute-start.21) | collective-permute-done | bytes 131104 | tf_op jit(solution)/shard_map/ppermute | solution.py:208
  67.1 0.1 fusion.29
  67.2 1.1 %collective-permute-start.22 = (bf16[16,32,128]{2,1,0:T(8,128)(2,1)S(1)}, bf16[16,32,128]{2,1,0:T(8,128)(2,1)S(1)}, u32[]{:S(2)}, u32[]{:S(2)}) collective-permute-start(bf16[16,32,128]{2,1,0:T(8,128)(2,1)S(1)} %fusion.29), channel_id=1, source_target_pairs={{0,2},{1,3},{2,0},{3,1},{4,6},{5,7},{6,4},{7,5},{8,10},{9,11},{10,... | collective-permute-start | bytes 393224 | tf_op jit(solution)/shard_map/ppermute | solution.py:208
  68.3 0.1 collective-permute-start.15
  68.4 4.2 %collective-permute-done.22 = bf16[16,32,128]{2,1,0:T(8,128)(2,1)S(1)} collective-permute-done((bf16[16,32,128]{2,1,0:T(8,128)(2,1)S(1)}, bf16[16,32,128]{2,1,0:T(8,128)(2,1)S(1)}, u32[]{:S(2)}, u32[]{:S(2)}) %collective-permute-start.22) | collective-permute-done | bytes 131104 | tf_op jit(solution)/shard_map/ppermute | solution.py:208
  72.6 0.1 fusion.26
  72.7 3.8 %collective-permute-done.15 = bf16[16,32,128]{2,1,0:T(8,128)(2,1)S(1)} collective-permute-done((bf16[16,32,128]{2,1,0:T(8,128)(2,1)S(1)}, bf16[16,32,128]{2,1,0:T(8,128)(2,1)S(1)}, u32[]{:S(2)}, u32[]{:S(2)}) %collective-permute-start.15) | collective-permute-done | bytes 131104 | tf_op jit(solution)/shard_map/ppermute | solution.py:208
  76.4 0.1 fusion.31
  76.5 1.6 %collective-permute-start.16 = (bf16[16,32,128]{2,1,0:T(8,128)(2,1)S(1)}, bf16[16,32,128]{2,1,0:T(8,128)(2,1)S(1)}, u32[]{:S(2)}, u32[]{:S(2)}) collective-permute-start(bf16[16,32,128]{2,1,0:T(8,128)(2,1)S(1)} %fusion.31), channel_id=1, source_target_pairs={{0,2},{1,3},{2,0},{3,1},{4,6},{5,7},{6,4},{7,5},{8,10},{9,11},{10,... | collective-permute-start | bytes 393224 | tf_op jit(solution)/shard_map/ppermute | solution.py:208
  78.1 0.1 add_convert_fusion
  78.3 3.7 %collective-permute-done.16 = bf16[16,32,128]{2,1,0:T(8,128)(2,1)S(1)} collective-permute-done((bf16[16,32,128]{2,1,0:T(8,128)(2,1)S(1)}, bf16[16,32,128]{2,1,0:T(8,128)(2,1)S(1)}, u32[]{:S(2)}, u32[]{:S(2)}) %collective-permute-start.16) | collective-permute-done | bytes 131104 | tf_op jit(solution)/shard_map/ppermute | solution.py:208
  82.0 0.1 fusion.22
  82.1 0.2 add_convert_fusion.1
  82.3 0.1 collective-permute-start.17
  82.4 0.7 pad_maximum_fusion.8
  83.1 1.7 %shard_map.111 = (bf16[192,4096]{1,0:T(8,128)(2,1)}, bf16[192,4096]{1,0:T(8,128)(2,1)}) custom-call(s32[1]{0:T(128)} %bitcast.core_ref, bf16[192,4096]{1,0:T(8,128)(2,1)S(1)} %copy-done, bf16[192,4096]{1,0:T(8,128)(2,1)S(1)} %copy-done.1, f32[192,2048]{1,0:T(8,128)S(1)} %get-tuple-element.82.kpart_ref, f32[192,2048]{1,0:T(8,128)S(1)} %get-tuple-element.83.vpart_ref, ...), custom_call_target="tpu_custom_call" | custom-call | flops 201326592 | bytes 6815744 | tf_op jit(solution)/shard_map/pallas_call | solution.py:242
  84.8 1.7 %shard_map.112 = (bf16[192,4096]{1,0:T(8,128)(2,1)}, bf16[192,4096]{1,0:T(8,128)(2,1)}) custom-call(s32[1]{0:T(128)} %bitcast.core_ref, bf16[192,4096]{1,0:T(8,128)(2,1)S(1)} %copy-done, bf16[192,4096]{1,0:T(8,128)(2,1)S(1)} %copy-done.1, f32[192,2048]{1,0:T(8,128)S(1)} %get-tuple-element.78.kpart_ref, ...), custom_call_target="tpu_custom_call", output_to_operand_aliasing={{0}: (7, {}), {1}: (8, {})} | custom-call | flops 201326592 | bytes 6815744 | tf_op jit(solution)/shard_map/pallas_call | solution.py:242
  (49 shorter events, 0.8 us)
Async XLA Ops:
  0.6 2.7 %copy-start = (bf16[192,4096]{1,0:T(8,128)(2,1)S(1)}, bf16[192,4096]{1,0:T(8,128)(2,1)}, u32[]{:S(2)}) copy-start(bf16[192,4096]{1,0:T(8,128)(2,1)} %k_ref.9) | copy-start | bytes 4718596
  0.7 2.6 %copy-start.1 = (bf16[192,4096]{1,0:T(8,128)(2,1)S(1)}, bf16[192,4096]{1,0:T(8,128)(2,1)}, u32[]{:S(2)}) copy-start(bf16[192,4096]{1,0:T(8,128)(2,1)} %v_ref.9) | copy-start | bytes 4718596
  2.7 1.8 %copy-start.5 = (f32[32,8,128]{2,1,0:T(8,128)S(1)}, f32[32,8,128]{2,1,0:T(8,128)}, u32[]{:S(2)}) copy-start(f32[32,8,128]{2,1,0:T(8,128)} %param.9) | copy-start | bytes 393220
  2.7 1.8 %collective-permute-start.6 = (bf16[2,16,32,128]{3,2,1,0:T(8,128)(2,1)S(1)}, bf16[2,16,32,128]{3,2,1,0:T(8,128)(2,1)S(1)}, u32[]{:S(2)}, u32[]{:S(2)}) collective-permute-start(bf16[2,16,32,128]{3,2,1,0:T(8,128)(2,1)S(1)} %get-tuple-element.61), channel_id=1, source_target_pairs={{0,1},{1,0},{2,3},{3,2},{4,5},{5,4},{6,7},{7,6},{8,9},{9,8},{10,11... | collective-permute-start | bytes 786440 | tf_op jit(solution)/shard_map/ppermute | solution.py:208
  4.2 3.3 %collective-permute-start = (bf16[2,16,32,128]{3,2,1,0:T(8,128)(2,1)S(1)}, bf16[2,16,32,128]{3,2,1,0:T(8,128)(2,1)S(1)}, u32[]{:S(2)}, u32[]{:S(2)}) collective-permute-start(bf16[2,16,32,128]{3,2,1,0:T(8,128)(2,1)S(1)} %get-tuple-element.55), channel_id=1, source_target_pairs={{0,1},{1,0},{2,3},{3,2},{4,5},{5,4},{6,7},{7,6},{8,9},{9,8},{10,11... | collective-permute-start | bytes 786440 | tf_op jit(solution)/shard_map/ppermute | solution.py:208
  4.6 6.7 %collective-permute-start.7 = (bf16[16,32,128]{2,1,0:T(8,128)(2,1)S(1)}, bf16[16,32,128]{2,1,0:T(8,128)(2,1)S(1)}, u32[]{:S(2)}, u32[]{:S(2)}) collective-permute-start(bf16[16,32,128]{2,1,0:T(8,128)(2,1)S(1)} %fusion.41), channel_id=1, source_target_pairs={{0,2},{1,3},{2,0},{3,1},{4,6},{5,7},{6,4},{7,5},{8,10},{9,11},{10,... | collective-permute-start | bytes 393224 | tf_op jit(solution)/shard_map/ppermute | solution.py:208
  11.5 5.8 %collective-permute-start.8 = (bf16[16,40,128]{2,1,0:T(8,128)(2,1)S(1)}, bf16[16,40,128]{2,1,0:T(8,128)(2,1)S(1)}, u32[]{:S(2)}, u32[]{:S(2)}) collective-permute-start(bf16[16,40,128]{2,1,0:T(8,128)(2,1)S(1)} %pad_maximum_fusion.5), channel_id=1, source_target_pairs={{0,4},{1,5},{2,6},{3,7},{4,0},{5,1},{6,2},{7,3},{8,12},{9,13},{10,... | collective-permute-start | bytes 491528 | tf_op jit(solution)/shard_map/ppermute | solution.py:208
  13.3 6.6 %collective-permute-start.1 = (bf16[16,32,128]{2,1,0:T(8,128)(2,1)S(1)}, bf16[16,32,128]{2,1,0:T(8,128)(2,1)S(1)}, u32[]{:S(2)}, u32[]{:S(2)}) collective-permute-start(bf16[16,32,128]{2,1,0:T(8,128)(2,1)S(1)} %fusion.40), channel_id=1, source_target_pairs={{0,2},{1,3},{2,0},{3,1},{4,6},{5,7},{6,4},{7,5},{8,10},{9,11},{10,... | collective-permute-start | bytes 393224 | tf_op jit(solution)/shard_map/ppermute | solution.py:208
  17.4 8.1 %collective-permute-start.9 = (bf16[16,32,128]{2,1,0:T(8,128)(2,1)S(1)}, bf16[16,32,128]{2,1,0:T(8,128)(2,1)S(1)}, u32[]{:S(2)}, u32[]{:S(2)}) collective-permute-start(bf16[16,32,128]{2,1,0:T(8,128)(2,1)S(1)} %fusion.17), channel_id=1, source_target_pairs={{0,8},{1,9},{2,10},{3,11},{4,12},{5,13},{6,14},{7,15},{8,0},{9,1},... | collective-permute-start | bytes 393224 | tf_op jit(solution)/shard_map/ppermute | solution.py:208
  20.1 6.7 %collective-permute-start.2 = (bf16[16,40,128]{2,1,0:T(8,128)(2,1)S(1)}, bf16[16,40,128]{2,1,0:T(8,128)(2,1)S(1)}, u32[]{:S(2)}, u32[]{:S(2)}) collective-permute-start(bf16[16,40,128]{2,1,0:T(8,128)(2,1)S(1)} %pad_maximum_fusion.4), channel_id=1, source_target_pairs={{0,4},{1,5},{2,6},{3,7},{4,0},{5,1},{6,2},{7,3},{8,12},{9,13},{10,... | collective-permute-start | bytes 491528 | tf_op jit(solution)/shard_map/ppermute | solution.py:208
  25.5 5.0 %collective-permute-start.10 = (bf16[16,32,128]{2,1,0:T(8,128)(2,1)S(1)}, bf16[16,32,128]{2,1,0:T(8,128)(2,1)S(1)}, u32[]{:S(2)}, u32[]{:S(2)}) collective-permute-start(bf16[16,32,128]{2,1,0:T(8,128)(2,1)S(1)} %fusion.33), channel_id=1, source_target_pairs={{0,2},{1,3},{2,0},{3,1},{4,6},{5,7},{6,4},{7,5},{8,10},{9,11},{10,... | collective-permute-start | bytes 393224 | tf_op jit(solution)/shard_map/ppermute | solution.py:208
  26.9 7.3 %collective-permute-start.3 = (bf16[16,32,128]{2,1,0:T(8,128)(2,1)S(1)}, bf16[16,32,128]{2,1,0:T(8,128)(2,1)S(1)}, u32[]{:S(2)}, u32[]{:S(2)}) collective-permute-start(bf16[16,32,128]{2,1,0:T(8,128)(2,1)S(1)} %fusion.11), channel_id=1, source_target_pairs={{0,8},{1,9},{2,10},{3,11},{4,12},{5,13},{6,14},{7,15},{8,0},{9,1},... | collective-permute-start | bytes 393224 | tf_op jit(solution)/shard_map/ppermute | solution.py:208
  30.7 4.9 %copy-start.2 = (bf16[192,4096]{1,0:T(8,128)(2,1)S(1)}, bf16[192,4096]{1,0:T(8,128)(2,1)}, u32[]{:S(2)}) copy-start(bf16[192,4096]{1,0:T(8,128)(2,1)} %q_ref.15) | copy-start | bytes 4718596
  30.8 6.8 %collective-permute-start.11 = (bf16[2,16,32,128]{3,2,1,0:T(8,128)(2,1)S(1)}, bf16[2,16,32,128]{3,2,1,0:T(8,128)(2,1)S(1)}, u32[]{:S(2)}, u32[]{:S(2)}) collective-permute-start(bf16[2,16,32,128]{3,2,1,0:T(8,128)(2,1)S(1)} %get-tuple-element.115), channel_id=1, source_target_pairs={{0,1},{1,0},{2,3},{3,2},{4,5},{5,4},{6,7},{7,6},{8,9},{9,8},{10,11... | collective-permute-start | bytes 786440 | tf_op jit(solution)/shard_map/ppermute | solution.py:208
  34.3 6.2 %collective-permute-start.4 = (bf16[16,32,128]{2,1,0:T(8,128)(2,1)S(1)}, bf16[16,32,128]{2,1,0:T(8,128)(2,1)S(1)}, u32[]{:S(2)}, u32[]{:S(2)}) collective-permute-start(bf16[16,32,128]{2,1,0:T(8,128)(2,1)S(1)} %fusion.35), channel_id=1, source_target_pairs={{0,2},{1,3},{2,0},{3,1},{4,6},{5,7},{6,4},{7,5},{8,10},{9,11},{10,... | collective-permute-start | bytes 393224 | tf_op jit(solution)/shard_map/ppermute | solution.py:208
  36.6 1.4 %copy-start.3 = (bf16[192,4096]{1,0:T(8,128)(2,1)S(1)}, bf16[192,4096]{1,0:T(8,128)(2,1)}, u32[]{:S(2)}) copy-start(bf16[192,4096]{1,0:T(8,128)(2,1)} %do_ref.3) | copy-start | bytes 4718596
  36.6 1.4 %copy-start.4 = (f32[4096]{0:T(1024)S(1)}, f32[4096]{0:T(1024)}, u32[]{:S(2)}) copy-start(f32[4096]{0:T(1024)} %param.10) | copy-start | bytes 49156
  40.6 1.5 %collective-permute-start.18 = (bf16[2,16,32,128]{3,2,1,0:T(8,128)(2,1)S(1)}, bf16[2,16,32,128]{3,2,1,0:T(8,128)(2,1)S(1)}, u32[]{:S(2)}, u32[]{:S(2)}) collective-permute-start(bf16[2,16,32,128]{3,2,1,0:T(8,128)(2,1)S(1)} %get-tuple-element.85), channel_id=1, source_target_pairs={{0,1},{1,0},{2,3},{3,2},{4,5},{5,4},{6,7},{7,6},{8,9},{9,8},{10,11... | collective-permute-start | bytes 786440 | tf_op jit(solution)/shard_map/ppermute | solution.py:208
  40.8 5.4 %collective-permute-start.5 = (bf16[2,16,32,128]{3,2,1,0:T(8,128)(2,1)S(1)}, bf16[2,16,32,128]{3,2,1,0:T(8,128)(2,1)S(1)}, u32[]{:S(2)}, u32[]{:S(2)}) collective-permute-start(bf16[2,16,32,128]{3,2,1,0:T(8,128)(2,1)S(1)} %get-tuple-element.117), channel_id=1, source_target_pairs={{0,1},{1,0},{2,3},{3,2},{4,5},{5,4},{6,7},{7,6},{8,9},{9,8},{10,11... | collective-permute-start | bytes 786440 | tf_op jit(solution)/shard_map/ppermute | solution.py:208
  42.2 9.7 %collective-permute-start.19 = (bf16[16,32,128]{2,1,0:T(8,128)(2,1)S(1)}, bf16[16,32,128]{2,1,0:T(8,128)(2,1)S(1)}, u32[]{:S(2)}, u32[]{:S(2)}) collective-permute-start(bf16[16,32,128]{2,1,0:T(8,128)(2,1)S(1)} %fusion.43), channel_id=1, source_target_pairs={{0,2},{1,3},{2,0},{3,1},{4,6},{5,7},{6,4},{7,5},{8,10},{9,11},{10,... | collective-permute-start | bytes 393224 | tf_op jit(solution)/shard_map/ppermute | solution.py:208
  48.8 3.4 %collective-permute-start.12 = (bf16[2,16,32,128]{3,2,1,0:T(8,128)(2,1)S(1)}, bf16[2,16,32,128]{3,2,1,0:T(8,128)(2,1)S(1)}, u32[]{:S(2)}, u32[]{:S(2)}) collective-permute-start(bf16[2,16,32,128]{3,2,1,0:T(8,128)(2,1)S(1)} %get-tuple-element.81), channel_id=1, source_target_pairs={{0,1},{1,0},{2,3},{3,2},{4,5},{5,4},{6,7},{7,6},{8,9},{9,8},{10,11... | collective-permute-start | bytes 786440 | tf_op jit(solution)/shard_map/ppermute | solution.py:208
  52.1 6.0 %collective-permute-start.20 = (bf16[16,32,128]{2,1,0:T(8,128)(2,1)S(1)}, bf16[16,32,128]{2,1,0:T(8,128)(2,1)S(1)}, u32[]{:S(2)}, u32[]{:S(2)}) collective-permute-start(bf16[16,32,128]{2,1,0:T(8,128)(2,1)S(1)} %get-tuple-element.93), channel_id=1, source_target_pairs={{0,4},{1,5},{2,6},{3,7},{4,0},{5,1},{6,2},{7,3},{8,12},{9,13},{10,... | collective-permute-start | bytes 393224 | tf_op jit(solution)/shard_map/ppermute | solution.py:208
  52.3 7.2 %collective-permute-start.13 = (bf16[16,32,128]{2,1,0:T(8,128)(2,1)S(1)}, bf16[16,32,128]{2,1,0:T(8,128)(2,1)S(1)}, u32[]{:S(2)}, u32[]{:S(2)}) collective-permute-start(bf16[16,32,128]{2,1,0:T(8,128)(2,1)S(1)} %fusion.42), channel_id=1, source_target_pairs={{0,2},{1,3},{2,0},{3,1},{4,6},{5,7},{6,4},{7,5},{8,10},{9,11},{10,... | collective-permute-start | bytes 393224 | tf_op jit(solution)/shard_map/ppermute | solution.py:208
  58.1 8.9 %collective-permute-start.21 = (bf16[16,32,128]{2,1,0:T(8,128)(2,1)S(1)}, bf16[16,32,128]{2,1,0:T(8,128)(2,1)S(1)}, u32[]{:S(2)}, u32[]{:S(2)}) collective-permute-start(bf16[16,32,128]{2,1,0:T(8,128)(2,1)S(1)} %get-tuple-element.91), channel_id=1, source_target_pairs={{0,8},{1,9},{2,10},{3,11},{4,12},{5,13},{6,14},{7,15},{8,0},{9,1},... | collective-permute-start | bytes 393224 | tf_op jit(solution)/shard_map/ppermute | solution.py:208
  59.6 8.7 %collective-permute-start.14 = (bf16[16,32,128]{2,1,0:T(8,128)(2,1)S(1)}, bf16[16,32,128]{2,1,0:T(8,128)(2,1)S(1)}, u32[]{:S(2)}, u32[]{:S(2)}) collective-permute-start(bf16[16,32,128]{2,1,0:T(8,128)(2,1)S(1)} %get-tuple-element.97), channel_id=1, source_target_pairs={{0,4},{1,5},{2,6},{3,7},{4,0},{5,1},{6,2},{7,3},{8,12},{9,13},{10,... | collective-permute-start | bytes 393224 | tf_op jit(solution)/shard_map/ppermute | solution.py:208
  67.2 5.4 %collective-permute-start.22 = (bf16[16,32,128]{2,1,0:T(8,128)(2,1)S(1)}, bf16[16,32,128]{2,1,0:T(8,128)(2,1)S(1)}, u32[]{:S(2)}, u32[]{:S(2)}) collective-permute-start(bf16[16,32,128]{2,1,0:T(8,128)(2,1)S(1)} %fusion.29), channel_id=1, source_target_pairs={{0,2},{1,3},{2,0},{3,1},{4,6},{5,7},{6,4},{7,5},{8,10},{9,11},{10,... | collective-permute-start | bytes 393224 | tf_op jit(solution)/shard_map/ppermute | solution.py:208
  68.3 8.1 %collective-permute-start.15 = (bf16[16,32,128]{2,1,0:T(8,128)(2,1)S(1)}, bf16[16,32,128]{2,1,0:T(8,128)(2,1)S(1)}, u32[]{:S(2)}, u32[]{:S(2)}) collective-permute-start(bf16[16,32,128]{2,1,0:T(8,128)(2,1)S(1)} %get-tuple-element.95), channel_id=1, source_target_pairs={{0,8},{1,9},{2,10},{3,11},{4,12},{5,13},{6,14},{7,15},{8,0},{9,1},... | collective-permute-start | bytes 393224 | tf_op jit(solution)/shard_map/ppermute | solution.py:208
  76.5 5.5 %collective-permute-start.16 = (bf16[16,32,128]{2,1,0:T(8,128)(2,1)S(1)}, bf16[16,32,128]{2,1,0:T(8,128)(2,1)S(1)}, u32[]{:S(2)}, u32[]{:S(2)}) collective-permute-start(bf16[16,32,128]{2,1,0:T(8,128)(2,1)S(1)} %fusion.31), channel_id=1, source_target_pairs={{0,2},{1,3},{2,0},{3,1},{4,6},{5,7},{6,4},{7,5},{8,10},{9,11},{10,... | collective-permute-start | bytes 393224 | tf_op jit(solution)/shard_map/ppermute | solution.py:208
  78.3 4.8 %collective-permute-start.23 = (bf16[2,16,32,128]{3,2,1,0:T(8,128)(2,1)S(1)}, bf16[2,16,32,128]{3,2,1,0:T(8,128)(2,1)S(1)}, u32[]{:S(2)}, u32[]{:S(2)}) collective-permute-start(bf16[2,16,32,128]{3,2,1,0:T(8,128)(2,1)S(1)} %get-tuple-element.107), channel_id=1, source_target_pairs={{0,1},{1,0},{2,3},{3,2},{4,5},{5,4},{6,7},{7,6},{8,9},{9,8},{10,11... | collective-permute-start | bytes 786440 | tf_op jit(solution)/shard_map/ppermute | solution.py:208
  82.3 2.6 %collective-permute-start.17 = (bf16[2,16,32,128]{3,2,1,0:T(8,128)(2,1)S(1)}, bf16[2,16,32,128]{3,2,1,0:T(8,128)(2,1)S(1)}, u32[]{:S(2)}, u32[]{:S(2)}) collective-permute-start(bf16[2,16,32,128]{3,2,1,0:T(8,128)(2,1)S(1)} %get-tuple-element.111), channel_id=1, source_target_pairs={{0,1},{1,0},{2,3},{3,2},{4,5},{5,4},{6,7},{7,6},{8,9},{9,8},{10,11... | collective-permute-start | bytes 786440 | tf_op jit(solution)/shard_map/ppermute | solution.py:208
